TPU v7x, 768 devices: a whole 4x8x12 slice. The times are simulated.
768 devices in a mesh: px: 48 (over z, y_hi), py: 4 (over x), dz: 4 (over y_lo, core).
Axes of the slice: x: 4, y: 8 (y_hi: 4, y_lo: 2; y = y_hi * 2 + y_lo), z: 12, core: 2. Of those that a mesh axis runs over, the one named last changes fastest.
Arguments:
- near_state: float32 [3, 384, 192, 1024], P(None, 'px', 'dz', 'py'), may hold values from -1 to 1, as said below
- column_owner: int32 [48, 16, 512, 1], P('px', ('py', 'dz')), may hold values from 0 to 15; in each aligned block of 512 rows (0 to 511, 512 to 1023, ..., all dimensions but the last counted through in order) at most 128 rows name the same one
- landing: int32 [48, 16, 512], P('px', ('py', 'dz')), may hold values from 0 to 16383
- far_depth: float32 [3072, 4096], P('px', ('py', 'dz')), may hold values from 3 to 6
- far_flows: float32 [2, 3072, 4096], P(None, 'px', ('py', 'dz')), may hold values from -3 to 3
- wet_mask: int32 [3072, 4096], P('px', ('py', 'dz')), may hold values 0 or 1
Outputs:
- near_fraction: float32 [384, 192, 1024], P('px', 'dz', 'py')
- far_new: float32 [3, 3072, 4096], P(None, 'px', ('py', 'dz'))
Inputs may be any that keep to these rules, and one draw needn't show every extreme that they name: `near_state`: the volume fraction (first field) lies in 0 to 1; the velocities lie in -1 to 1. `column_owner`: in each near tile no owner receives more than 128 columns; some owner receives exactly 128.
All inputs are finite; a program needn't handle non-finite values. No bound on the sum of `wet_mask` on one device may be relied on, other than what follows from the above.
Results may differ from a plain program's by a relative error of at most 0.00002.
Values sent between devices are 32-bit elements; how exact they have to be, the bound alone decides.
No kernel may reach another device: no remote copies, remote signals or barrier semaphores. Data moves between devices by JAX's collectives and lax.ppermute only.
A program may use at most 32 MiB of HBM per device.

v0:
```python
import jax
import jax.numpy as jnp
from jax import lax
from jax.sharding import PartitionSpec as P

CAP = 128


advect_coef = 0.25
diffuse_coef = 0.1
slope_coef = 0.5
flux_coef = 0.1
gravity = 1.0
column_height = 4.0


def padded_2(cells, sides, width):
    for axis, dim in sides:
        count = lax.axis_size(axis)
        ends = count - 1
        head = lax.slice_in_dim(cells, 0, width, axis=dim)
        tail = lax.slice_in_dim(cells, cells.shape[dim] - width, cells.shape[dim], axis=dim)
        cells = jnp.concatenate(
            [
                lax.ppermute(tail, axis, [(i, (i + 1) % count) for i in range(ends)]),
                cells,
                lax.ppermute(head, axis, [((i + 1) % count, i) for i in range(ends)]),
            ],
            axis=dim,
        )
    return cells


def near_update(center, xplus, xminus, yplus, yminus, zplus, zminus):
    velx = center[1]
    vely = center[2]
    lap = xplus + xminus + yplus + yminus + zplus + zminus - 6.0 * center
    moved = (
        center
        - advect_coef * (velx * (xplus - xminus) + vely * (yplus - yminus))
        + diffuse_coef * lap
    )
    new_frac = moved[0]
    new_velx = moved[1] - slope_coef * (xplus[0] - xminus[0])
    new_vely = moved[2] - slope_coef * (yplus[0] - yminus[0])
    return (new_frac, new_velx, new_vely)


def fluxes(state, divisor):
    depth = state[0]
    flow_x = state[1]
    flow_y = state[2]
    cross = flow_x * flow_y / divisor
    press = 0.5 * gravity * depth * depth
    xflux = jnp.stack([flow_x, flow_x * flow_x / divisor + press, cross])
    yflux = jnp.stack([flow_y, cross, flow_y * flow_y / divisor + press])
    return (xflux, yflux)


def local(near_state, column_owner, landing, far_depth, far_flows, wet_mask):
    padded = padded_2(near_state, (("px", 1), ("py", 3), ("dz", 2)), 1)
    center = padded[:, 1:-1, 1:-1, 1:-1]
    new_frac, new_velx, new_vely = near_update(
        center,
        padded[:, 2:, 1:-1, 1:-1],
        padded[:, :-2, 1:-1, 1:-1],
        padded[:, 1:-1, 1:-1, 2:],
        padded[:, 1:-1, 1:-1, :-2],
        padded[:, 1:-1, 2:, 1:-1],
        padded[:, 1:-1, :-2, 1:-1],
    )
    inv_depth = column_height / (near_state.shape[2] * lax.axis_size("dz"))
    partial_sums = jnp.stack(
        [
            jnp.sum(new_frac, axis=1),
            jnp.sum(new_frac * new_velx, axis=1),
            jnp.sum(new_frac * new_vely, axis=1),
        ]
    )
    columns = lax.psum_scatter(partial_sums, "dz", scatter_dimension=2, tiled=True) * inv_depth
    count_cols = columns.shape[1] * columns.shape[2]
    columns = columns.reshape(3, count_cols)
    owners = lax.axis_size("py") * lax.axis_size("dz")
    capacity = CAP
    dest = column_owner[0, 0, :, 0]
    land = landing[0, 0, :]
    onehot = (dest[:, None] == jnp.arange(owners, dtype=jnp.int32)[None, :]).astype(jnp.int32)
    rank = jnp.sum(jnp.cumsum(onehot, axis=0) * onehot, axis=1) - 1
    slot = dest * capacity + rank
    packed = jnp.concatenate([columns, land.astype(jnp.float32)[None, :]], axis=0)
    blank = jnp.concatenate(
        [
            jnp.zeros((3, owners * capacity), jnp.float32),
            jnp.full((1, owners * capacity), -1.0, jnp.float32),
        ],
        axis=0,
    )
    buffer = blank.at[:, slot].set(packed)
    arrived = lax.all_to_all(
        buffer.reshape(4, owners, capacity), ("py", "dz"), split_axis=1, concat_axis=1, tiled=True
    )
    arrived = arrived.reshape(4, owners * capacity)
    far_x = far_depth.shape[0]
    far_y = far_depth.shape[1]
    valid = arrived[3] >= 0.0
    target = jnp.where(valid, arrived[3], 0.0).astype(jnp.int32)
    values = jnp.where(valid[None, :], arrived[0:3], 0.0)
    source = (
        jnp.zeros((3, far_x * far_y), jnp.float32)
        .at[:, target]
        .add(values)
        .reshape(3, far_x, far_y)
    )
    wet = wet_mask.astype(jnp.float32)
    state = jnp.stack([far_depth, far_flows[0], far_flows[1]]) + source
    state = jnp.stack([state[0], state[1] * wet, state[2] * wet])
    xflux, yflux = fluxes(state, state[0])
    stacked = jnp.concatenate([state, xflux, yflux], axis=0)
    padded_far = padded_2(stacked, (("px", 1), (("py", "dz"), 2)), 1)
    state_pad = padded_far[0:3]
    xpad = padded_far[3:6]
    ypad = padded_far[6:9]
    avg = 0.25 * (
        state_pad[:, 2:, 1:-1]
        + state_pad[:, :-2, 1:-1]
        + state_pad[:, 1:-1, 2:]
        + state_pad[:, 1:-1, :-2]
    )
    far_new = (
        avg
        - flux_coef * (xpad[:, 2:, 1:-1] - xpad[:, :-2, 1:-1])
        - flux_coef * (ypad[:, 1:-1, 2:] - ypad[:, 1:-1, :-2])
    )
    return (new_frac, far_new)


def solution(mesh):
    return jax.shard_map(
        local,
        mesh=mesh,
        in_specs=(
            P(None, "px", "dz", "py"),
            P("px", ("py", "dz"), None, None),
            P("px", ("py", "dz"), None),
            P("px", ("py", "dz")),
            P(None, "px", ("py", "dz")),
            P("px", ("py", "dz")),
        ),
        out_specs=(P("px", "dz", "py"), P(None, "px", ("py", "dz"))),
        check_vma=False,
    )
```

profile of v0, /device:TPU:18, one launch (start us, length us, event | category | flops | bytes accessed | tf_op | source)
XLA Modules:
  0.0 151.2 jit_solution(6820347197349529834)
XLA Ops:
  7.2 1.7 %fusion.40 = (f32[3,1,48,256]{3,2,1,0:T(8,128)}, f32[3,1,48,256]{3,2,1,0:T(8,128)S(1)}) fusion(f32[3,8,48,256]{3,2,1,0:T(8,128)} %param.6), kind=kLoop, calls=%fused_computation.111 | loop fusion | bytes 589824 | tf_op jit(solution)/shard_map/slice | solution.py:21
  8.9 2.4 %collective-permute-start = (f32[3,1,48,256]{3,2,1,0:T(8,128)}, f32[3,1,48,256]{3,2,1,0:T(8,128)S(1)}, u32[]{:S(2)}, u32[]{:S(2)}) collective-permute-start(f32[3,1,48,256]{3,2,1,0:T(8,128)} %get-tuple-element.22), channel_id=1, source_target_pairs={{16,0},{32,16},{48,32},{64,48},{80,64},{96,80},{112,96},{128,112},... | collective-permute-start | bytes 442376 | tf_op jit(solution)/shard_map/ppermute | solution.py:27
  11.3 5.7 %collective-permute-start.1 = (f32[3,1,48,256]{3,2,1,0:T(8,128)S(1)}, f32[3,1,48,256]{3,2,1,0:T(8,128)S(1)}, u32[]{:S(2)}, u32[]{:S(2)}) collective-permute-start(f32[3,1,48,256]{3,2,1,0:T(8,128)S(1)} %get-tuple-element.23), channel_id=1, source_target_pairs={{0,16},{16,32},{32,48},{48,64},{64,80},{80,96},{96,112},{112,128},... | collective-permute-start | bytes 442376 | tf_op jit(solution)/shard_map/ppermute | solution.py:25
  17.0 1.9 %slice_bitcast_fusion.1 = (f32[8,48,256]{2,1,0:T(8,128)S(1)}, f32[8,48,256]{2,1,0:T(8,128)}) fusion(f32[3,8,48,256]{3,2,1,0:T(8,128)} %param.6), kind=kLoop, calls=%fused_computation.37 | loop fusion | bytes 1572864 | tf_op jit(solution)/shard_map/mul | solution.py:40
  20.4 2.5 %collective-permute-done.1 = f32[3,1,48,256]{3,2,1,0:T(8,128)S(1)} collective-permute-done((f32[3,1,48,256]{3,2,1,0:T(8,128)S(1)}, f32[3,1,48,256]{3,2,1,0:T(8,128)S(1)}, u32[]{:S(2)}, u32[]{:S(2)}) %collective-permute-start.1) | collective-permute-done | bytes 147488 | tf_op jit(solution)/shard_map/ppermute | solution.py:25
  25.4 7.7 %collective-permute-start.2 = (f32[3,10,48,1]{2,3,1,0:T(1,128)S(1)}, f32[3,10,48,1]{2,3,1,0:T(1,128)S(1)}, u32[]{:S(2)}, u32[]{:S(2)}) collective-permute-start(f32[3,10,48,1]{2,3,1,0:T(1,128)S(1)} %copy.60), channel_id=1, source_target_pairs={{4,0},{8,4},{12,8},{5,1},{9,5},{13,9},{6,2},{10,6},{14,10},{7,3},{... | collective-permute-start | bytes 17288 | tf_op jit(solution)/shard_map/ppermute | solution.py:27
  33.1 1.9 %collective-permute-start.3 = (f32[3,10,48,1]{2,3,1,0:T(1,128)S(1)}, f32[3,10,48,1]{2,3,1,0:T(1,128)S(1)}, u32[]{:S(2)}, u32[]{:S(2)}) collective-permute-start(f32[3,10,48,1]{2,3,1,0:T(1,128)S(1)} %copy.61), channel_id=1, source_target_pairs={{0,4},{4,8},{8,12},{1,5},{5,9},{9,13},{2,6},{6,10},{10,14},{3,7},{... | collective-permute-start | bytes 17288 | tf_op jit(solution)/shard_map/ppermute | solution.py:25
  35.1 3.7 %collective-permute-done.3 = f32[3,10,48,1]{2,3,1,0:T(1,128)S(1)} collective-permute-done((f32[3,10,48,1]{2,3,1,0:T(1,128)S(1)}, f32[3,10,48,1]{2,3,1,0:T(1,128)S(1)}, u32[]{:S(2)}, u32[]{:S(2)}) %collective-permute-start.3) | collective-permute-done | bytes 5792 | tf_op jit(solution)/shard_map/ppermute | solution.py:25
  39.8 1.4 collective-permute-start.4
  41.2 3.0 %collective-permute-start.5 = (f32[3,10,1,258]{3,2,1,0:T(1,128)S(1)}, f32[3,10,1,258]{3,2,1,0:T(1,128)S(1)}, u32[]{:S(2)}, u32[]{:S(2)}) collective-permute-start(f32[3,10,1,258]{3,2,1,0:T(1,128)S(1)} %get-tuple-element.14), channel_id=1, source_target_pairs={{0,1},{1,2},{2,3},{4,5},{5,6},{6,7},{8,9},{9,10},{10,11},{12,13},{... | collective-permute-start | bytes 92888 | tf_op jit(solution)/shard_map/ppermute | solution.py:25
  45.1 3.5 %fusion.7 = f32[3,8,48,256]{3,2,1,0:T(8,128)S(1)} fusion(f32[3,10,1,258]{3,2,1,0:T(1,128)S(1)} %collective-permute-done.5, f32[3,10,48,1]{3,2,1,0:T(8,128)S(1)} %copy.47, f32[3,10,48,256]{3,2,1,0:T(8,128)S(1)} %get-tuple-element.28, f32[3,10,48,1]{3,2,1,0:T(8,128)S(1)} %copy.49, f32[3,10,1,258]{3,2,1,0:T(1,128)S(1)} %collective-permute-done.4, ...), kind=kLoop, calls=%fused_computation.14 | loop fusion | flops 7077888 | bytes 7053024 | tf_op jit(solution)/shard_map/add | solution.py:39
  48.6 2.1 %fusion.19 = (f32[8,256]{1,0:T(8,128)S(1)}, f32[8,256]{1,0:T(8,128)S(1)}, f32[8,48,256]{2,1,0:T(8,128)}) fusion(f32[3,9,48,256]{3,2,1,0:T(8,128)} %copy-done.5, f32[3,9,48,256]{3,2,1,0:T(8,128)S(1)} %copy-done.3, f32[3,8,48,256]{3,2,1,0:T(8,128)S(1)} %fusion.7, f32[3,10,48,256]{3,2,1,0:T(8,128)S(1)} %get-tuple-element.28, f32[3,10,48,1]{3,2,1,0:T(8,128)S(1)} %copy.49, ...), kind=kLoop, calls=%fused_computation.35 | loop fusion | flops 1175552 | bytes 3861760 | tf_op jit(solution)/shard_map/reduce_sum | solution.py:76
  51.9 29.4 %reduce-scatter.4.cloned.1.call-done = f32[64,24]{1,0:T(8,128)} async-done(((f32[256,24]{1,0:T(8,128)}), f32[64,24]{1,0:T(8,128)}) %reduce-scatter.4.cloned.1.call-update) | async-done | bytes 6160
  82.6 2.1 %scatter_fusion = f32[4,2048]{0,1:T(8,128)S(1)} fusion(f32[4,2048]{0,1:T(8,128)S(1)} %copy-done.4, s32[512]{0:T(512)S(1)} %bitcast.125, f32[512,4]{1,0:T(8,128)S(1)} %copy.53), kind=kCustom, calls=%fused_computation | custom fusion | bytes 26624 | tf_op jit(solution)/shard_map/scatter | solution.py:98
  85.0 9.4 %all_to_all.5 = f32[4,16,128]{2,0,1:T(4,128)S(1)} all-to-all(f32[4,16,128]{2,0,1:T(4,128)S(1)} %copy.54), channel_id=1, replica_groups=mesh['px'=48,'py'=4,'dz'=4] {'py','dz'}, dimensions={1} | all-to-all | bytes 65536 | tf_op jit(solution)/shard_map/all_to_all | solution.py:99
  94.9 17.5 %scatter_custom_fusion.1 = f32[3,16384]{0,1:T(8,128)} fusion(s32[2048]{0:T(1024)S(1)} %bitcast.127, f32[2048,3]{1,0:T(8,128)S(1)} %copy.56, f32[]{:T(128)} %constant.15.clone.1), kind=kCustom, calls=%fused_computation.2 | custom fusion | flops 6144 | bytes 196612 | tf_op jit(solution)/shard_map/scatter-add | solution.py:111
  112.4 5.3 %copy.57 = f32[3,64,256]{2,1,0:T(8,128)S(1)} copy(f32[3,64,256]{0,2,1:T(8,128)} %bitcast.114) | data formatting | bytes 393216 | tf_op jit(solution)/shard_map/reshape | solution.py:112
  117.9 5.5 %collective-permute-start.7 = (f32[9,1,256]{2,1,0:T(1,128)S(1)}, f32[9,1,256]{2,1,0:T(1,128)S(1)}, u32[]{:S(2)}, u32[]{:S(2)}) collective-permute-start(f32[9,1,256]{2,1,0:T(1,128)S(1)} %get-tuple-element.26), channel_id=1, source_target_pairs={{0,16},{16,32},{32,48},{48,64},{64,80},{80,96},{96,112},{112,128},... | collective-permute-start | bytes 27656 | tf_op jit(solution)/shard_map/ppermute | solution.py:25
  123.5 1.9 %collective-permute-start.6 = (f32[9,1,256]{2,1,0:T(1,128)S(1)}, f32[9,1,256]{2,1,0:T(1,128)S(1)}, u32[]{:S(2)}, u32[]{:S(2)}) collective-permute-start(f32[9,1,256]{2,1,0:T(1,128)S(1)} %get-tuple-element.27), channel_id=1, source_target_pairs={{16,0},{32,16},{48,32},{64,48},{80,64},{96,80},{112,96},{128,112},... | collective-permute-start | bytes 27656 | tf_op jit(solution)/shard_map/ppermute | solution.py:27
  125.4 5.7 %collective-permute-done.6 = f32[9,1,256]{2,1,0:T(1,128)S(1)} collective-permute-done((f32[9,1,256]{2,1,0:T(1,128)S(1)}, f32[9,1,256]{2,1,0:T(1,128)S(1)}, u32[]{:S(2)}, u32[]{:S(2)}) %collective-permute-start.6) | collective-permute-done | bytes 9248 | tf_op jit(solution)/shard_map/ppermute | solution.py:27
  131.4 2.0 %collective-permute-start.8 = (f32[9,66,1]{2,1,0:T(8,128)S(1)}, f32[9,66,1]{2,1,0:T(8,128)S(1)}, u32[]{:S(2)}, u32[]{:S(2)}) collective-permute-start(f32[9,66,1]{2,1,0:T(8,128)S(1)} %get-tuple-element.24), channel_id=1, source_target_pairs={{1,0},{2,1},{3,2},{4,3},{5,4},{6,5},{7,6},{8,7},{9,8},{10,9},{11,1... | collective-permute-start | bytes 7136 | tf_op jit(solution)/shard_map/ppermute | solution.py:27
  133.3 2.4 %collective-permute-start.9 = (f32[9,66,1]{2,1,0:T(8,128)S(1)}, f32[9,66,1]{2,1,0:T(8,128)S(1)}, u32[]{:S(2)}, u32[]{:S(2)}) collective-permute-start(f32[9,66,1]{2,1,0:T(8,128)S(1)} %get-tuple-element.25), channel_id=1, source_target_pairs={{0,1},{1,2},{2,3},{3,4},{4,5},{5,6},{6,7},{7,8},{8,9},{9,10},{10,1... | collective-permute-start | bytes 7136 | tf_op jit(solution)/shard_map/ppermute | solution.py:25
  135.7 4.1 %collective-permute-done.8 = f32[9,66,1]{2,1,0:T(8,128)S(1)} collective-permute-done((f32[9,66,1]{2,1,0:T(8,128)S(1)}, f32[9,66,1]{2,1,0:T(8,128)S(1)}, u32[]{:S(2)}, u32[]{:S(2)}) %collective-permute-start.8) | collective-permute-done | bytes 2408 | tf_op jit(solution)/shard_map/ppermute | solution.py:27
  139.8 3.5 %collective-permute-done.9 = f32[9,66,1]{2,1,0:T(8,128)S(1)} collective-permute-done((f32[9,66,1]{2,1,0:T(8,128)S(1)}, f32[9,66,1]{2,1,0:T(8,128)S(1)}, u32[]{:S(2)}, u32[]{:S(2)}) %collective-permute-start.9) | collective-permute-done | bytes 2408 | tf_op jit(solution)/shard_map/ppermute | solution.py:25
  (79 shorter events, 10.4 us)
Async XLA Ops:
  7.2 11.7 %copy-start.10 = (s32[1,1,512,1]{2,3,1,0:T(1,128)S(1)}, s32[1,1,512,1]{2,3,1,0:T(1,128)}, u32[]{:S(2)}) copy-start(s32[1,1,512,1]{2,3,1,0:T(1,128)} %param.7) | copy-start | bytes 6148
  7.2 74.2 %reduce-scatter.4.cloned.1.call-start = ((), (), s32[]{:S(2)}) async-start(), calls=%async_computation.2 | async-start | bytes 163840
  8.9 14.0 %copy-start = (f32[3,8,48,256]{3,2,1,0:T(8,128)S(1)}, f32[3,8,48,256]{3,2,1,0:T(8,128)}, u32[]{:S(2)}) copy-start(f32[3,8,48,256]{3,2,1,0:T(8,128)} %param.6) | copy-start | bytes 3538948
  8.9 14.4 %collective-permute-start = (f32[3,1,48,256]{3,2,1,0:T(8,128)}, f32[3,1,48,256]{3,2,1,0:T(8,128)S(1)}, u32[]{:S(2)}, u32[]{:S(2)}) collective-permute-start(f32[3,1,48,256]{3,2,1,0:T(8,128)} %get-tuple-element.22), channel_id=1, source_target_pairs={{16,0},{32,16},{48,32},{64,48},{80,64},{96,80},{112,96},{128,112},... | collective-permute-start | bytes 442376 | tf_op jit(solution)/shard_map/ppermute | solution.py:27
  11.3 11.6 %collective-permute-start.1 = (f32[3,1,48,256]{3,2,1,0:T(8,128)S(1)}, f32[3,1,48,256]{3,2,1,0:T(8,128)S(1)}, u32[]{:S(2)}, u32[]{:S(2)}) collective-permute-start(f32[3,1,48,256]{3,2,1,0:T(8,128)S(1)} %get-tuple-element.23), channel_id=1, source_target_pairs={{0,16},{16,32},{32,48},{48,64},{64,80},{80,96},{96,112},{112,128},... | collective-permute-start | bytes 442376 | tf_op jit(solution)/shard_map/ppermute | solution.py:25
  23.3 1.1 copy-start.5
  23.3 1.5 copy-start.2
  25.4 13.7 %collective-permute-start.2 = (f32[3,10,48,1]{2,3,1,0:T(1,128)S(1)}, f32[3,10,48,1]{2,3,1,0:T(1,128)S(1)}, u32[]{:S(2)}, u32[]{:S(2)}) collective-permute-start(f32[3,10,48,1]{2,3,1,0:T(1,128)S(1)} %copy.60), channel_id=1, source_target_pairs={{4,0},{8,4},{12,8},{5,1},{9,5},{13,9},{6,2},{10,6},{14,10},{7,3},{... | collective-permute-start | bytes 17288 | tf_op jit(solution)/shard_map/ppermute | solution.py:27
  33.1 5.6 %collective-permute-start.3 = (f32[3,10,48,1]{2,3,1,0:T(1,128)S(1)}, f32[3,10,48,1]{2,3,1,0:T(1,128)S(1)}, u32[]{:S(2)}, u32[]{:S(2)}) collective-permute-start(f32[3,10,48,1]{2,3,1,0:T(1,128)S(1)} %copy.61), channel_id=1, source_target_pairs={{0,4},{4,8},{8,12},{1,5},{5,9},{9,13},{2,6},{6,10},{10,14},{3,7},{... | collective-permute-start | bytes 17288 | tf_op jit(solution)/shard_map/ppermute | solution.py:25
  39.4 5.7 %copy-start.1 = (f32[3,8,48,256]{3,2,1,0:T(8,128)S(1)}, f32[3,8,48,256]{3,2,1,0:T(8,128)}, u32[]{:S(2)}) copy-start(f32[3,8,48,256]{3,2,1,0:T(8,128)} %param.6) | copy-start | bytes 3538948
  39.4 5.7 %copy-start.3 = (f32[3,9,48,256]{3,2,1,0:T(8,128)S(1)}, f32[3,9,48,256]{3,2,1,0:T(8,128)}, u32[]{:S(2)}) copy-start(f32[3,9,48,256]{3,2,1,0:T(8,128)} %copy-done.2) | copy-start | bytes 3981316
  39.4 5.7 %copy-start.6 = (f32[8,48,256]{2,1,0:T(8,128)S(1)}, f32[8,48,256]{2,1,0:T(8,128)}, u32[]{:S(2)}) copy-start(f32[8,48,256]{2,1,0:T(8,128)} %get-tuple-element.18) | copy-start | bytes 1179652
  39.8 4.5 %collective-permute-start.4 = (f32[3,10,1,258]{3,2,1,0:T(1,128)S(1)}, f32[3,10,1,258]{3,2,1,0:T(1,128)S(1)}, u32[]{:S(2)}, u32[]{:S(2)}) collective-permute-start(f32[3,10,1,258]{3,2,1,0:T(1,128)S(1)} %get-tuple-element.13), channel_id=1, source_target_pairs={{1,0},{2,1},{3,2},{5,4},{6,5},{7,6},{9,8},{10,9},{11,10},{13,12},{... | collective-permute-start | bytes 92888 | tf_op jit(solution)/shard_map/ppermute | solution.py:27
  41.2 3.9 %collective-permute-start.5 = (f32[3,10,1,258]{3,2,1,0:T(1,128)S(1)}, f32[3,10,1,258]{3,2,1,0:T(1,128)S(1)}, u32[]{:S(2)}, u32[]{:S(2)}) collective-permute-start(f32[3,10,1,258]{3,2,1,0:T(1,128)S(1)} %get-tuple-element.14), channel_id=1, source_target_pairs={{0,1},{1,2},{2,3},{4,5},{5,6},{6,7},{8,9},{9,10},{10,11},{12,13},{... | collective-permute-start | bytes 92888 | tf_op jit(solution)/shard_map/ppermute | solution.py:25
  50.7 1.2 copy-start.11
  51.9 30.7 %copy-start.4 = (f32[4,2048]{0,1:T(8,128)S(1)}, f32[4,2048]{0,1:T(8,128)}, u32[]{:S(2)}) copy-start(f32[4,2048]{0,1:T(8,128)} %constant.16.clone.1) | copy-start | bytes 98308
  112.4 5.3 %copy-start.8 = (f32[2,64,256]{2,1,0:T(8,128)S(1)}, f32[2,64,256]{2,1,0:T(8,128)}, u32[]{:S(2)}) copy-start(f32[2,64,256]{2,1,0:T(8,128)} %param.10) | copy-start | bytes 393220
  112.4 5.3 %copy-start.9 = (f32[64,256]{1,0:T(8,128)S(1)}, f32[64,256]{1,0:T(8,128)}, u32[]{:S(2)}) copy-start(f32[64,256]{1,0:T(8,128)} %param.9) | copy-start | bytes 196612
  112.4 5.3 %copy-start.7 = (s32[64,256]{1,0:T(8,128)S(1)}, s32[64,256]{1,0:T(8,128)}, u32[]{:S(2)}) copy-start(s32[64,256]{1,0:T(8,128)} %param.11) | copy-start | bytes 196612
  117.9 7.5 %collective-permute-start.7 = (f32[9,1,256]{2,1,0:T(1,128)S(1)}, f32[9,1,256]{2,1,0:T(1,128)S(1)}, u32[]{:S(2)}, u32[]{:S(2)}) collective-permute-start(f32[9,1,256]{2,1,0:T(1,128)S(1)} %get-tuple-element.26), channel_id=1, source_target_pairs={{0,16},{16,32},{32,48},{48,64},{64,80},{80,96},{96,112},{112,128},... | collective-permute-start | bytes 27656 | tf_op jit(solution)/shard_map/ppermute | solution.py:25
  123.5 7.7 %collective-permute-start.6 = (f32[9,1,256]{2,1,0:T(1,128)S(1)}, f32[9,1,256]{2,1,0:T(1,128)S(1)}, u32[]{:S(2)}, u32[]{:S(2)}) collective-permute-start(f32[9,1,256]{2,1,0:T(1,128)S(1)} %get-tuple-element.27), channel_id=1, source_target_pairs={{16,0},{32,16},{48,32},{64,48},{80,64},{96,80},{112,96},{128,112},... | collective-permute-start | bytes 27656 | tf_op jit(solution)/shard_map/ppermute | solution.py:27
  131.4 8.4 %collective-permute-start.8 = (f32[9,66,1]{2,1,0:T(8,128)S(1)}, f32[9,66,1]{2,1,0:T(8,128)S(1)}, u32[]{:S(2)}, u32[]{:S(2)}) collective-permute-start(f32[9,66,1]{2,1,0:T(8,128)S(1)} %get-tuple-element.24), channel_id=1, source_target_pairs={{1,0},{2,1},{3,2},{4,3},{5,4},{6,5},{7,6},{8,7},{9,8},{10,9},{11,1... | collective-permute-start | bytes 7136 | tf_op jit(solution)/shard_map/ppermute | solution.py:27
  133.3 10.0 %collective-permute-start.9 = (f32[9,66,1]{2,1,0:T(8,128)S(1)}, f32[9,66,1]{2,1,0:T(8,128)S(1)}, u32[]{:S(2)}, u32[]{:S(2)}) collective-permute-start(f32[9,66,1]{2,1,0:T(8,128)S(1)} %get-tuple-element.25), channel_id=1, source_target_pairs={{0,1},{1,2},{2,3},{3,4},{4,5},{5,6},{6,7},{7,8},{8,9},{9,10},{10,1... | collective-permute-start | bytes 7136 | tf_op jit(solution)/shard_map/ppermute | solution.py:25
Sparse Core Ops, SparseCore 0:
  52.0 29.2 reduce-scatter.3
where the time goes:
time: 152 us; the launch traced here: 151 us
  waiting for transfers between devices  49.8 us (33%)
  starting transfers between devices  34 us (22%)
  other arithmetic  26.1 us (17%)
  local copies, waits for them, and re-layouts  17.5 us (12%)
  between operations  14.5 us (10%)
  blocking collectives  9.38 us (6%)
    unnamed x2, waiting for transfers between devices  29.4 us
    ppermute x5, starting transfers between devices, padded_2(): lax.ppermute(tail, axis, [(i, (i + 1) % count) for i in range(ends)])  18.6 us
    scatter-add x1, other arithmetic, local(): source = jnp.zeros((3, far_x * far_y), jnp.float32).at[:, target].add(val...  17.5 us
    ppermute x5, starting transfers between devices, padded_2(): lax.ppermute(head, axis, [((i + 1) % count, i) for i in range(ends)])  15.4 us
    ppermute x5, waiting for transfers between devices, padded_2(): lax.ppermute(tail, axis, [(i, (i + 1) % count) for i in range(ends)])  10.5 us
    ppermute x5, waiting for transfers between devices, padded_2(): lax.ppermute(head, axis, [((i + 1) % count, i) for i in range(ends)])  9.84 us
    all_to_all x1, blocking collectives, local(): lax.all_to_all(buffer.reshape(4, owners, capacity), ('py', 'dz'), split_a...  9.38 us
    reshape x1, local copies, waits for them, and re-layouts, local(): source = jnp.zeros((3, far_x * far_y), jnp.float32).at[:, target].add(val...  5.26 us
  transfers between devices with their start and end apart: 11, of which 7 were waited for; matrix products, arithmetic and copies ran while one was open for 3% of the time, Pallas kernels for 0%

commit v1 on v0

v1 whole, which is shorter than its diff:
```python
import functools

import jax
import jax.numpy as jnp
from jax import lax
from jax.experimental import pallas as pl
from jax.experimental.pallas import tpu as pltpu
from jax.sharding import PartitionSpec as P

advect_coef = 0.25
diffuse_coef = 0.1
slope_coef = 0.5
flux_coef = 0.1
gravity = 1.0
column_height = 4.0

NPY = 4
NDZ = 4
GRP = NPY * NDZ
CX = 8
CZ = 48
CY = 256
FX = 64
FY = 256
ROWS = CX * 3 * 2
BLK = ROWS + 8
NROW = FY + 16

f32 = jnp.float32
GROUP = ("py", "dz")
VM = pl.BlockSpec(memory_space=pltpu.VMEM)
PARAMS = pltpu.CompilerParams(vmem_limit_bytes=24 << 20)


def lane_iota(shape):
    return lax.broadcasted_iota(jnp.int32, shape, len(shape) - 1)


def x_order(row):
    return 2 * row if row < 4 else 2 * (row - 4) + 1


def pack_kernel(near, owner, land, depth, flows, mask, out, xlo, xhi):
    py = lax.axis_index("py")
    dz = lax.axis_index("dz")
    me = py * NDZ + dz
    xlo[...] = near[:, 0]
    xhi[...] = near[:, CX - 1]
    code = (owner[...] * (FX * FY) + land[...]).astype(f32)
    swap = pltpu.roll(code, 64, 1)
    odd = (me % 2) == 1
    codes = jnp.concatenate([jnp.where(odd, swap, code), jnp.where(odd, code, swap)], axis=0)
    lanes = lane_iota((8, 128))
    mine = jnp.where(odd, lanes, 127 - lanes) >= 64
    codes = jnp.where(mine, codes, 0.0)
    zero = jnp.zeros((ROWS, 128), f32)
    for b in range(GRP):
        out[b, 0:ROWS] = zero
        out[b, ROWS:BLK] = codes

    def edge(col):
        k = lane_iota((FX, 128))
        m = jnp.zeros((FX, 128), f32)
        for n, part in enumerate((depth[...], flows[0], flows[1], mask[...].astype(f32))):
            m = jnp.where(k == n, part[:, col : col + 1], m)
        turned = jnp.concatenate([m, m], axis=0).T
        return jnp.where(mine, codes, turned[0:8])

    @pl.when(me > 0)
    def _():
        out[me - 1, ROWS:BLK] = edge(0)

    @pl.when(me < GRP - 1)
    def _():
        out[me + 1, ROWS:BLK] = edge(FY - 1)

    def zface(dst, z):
        for f in range(3):
            face = near[f, :, z, :]
            for h in range(2):
                r = (f * 2 + h) * 8
                out[dst, r : r + 8] = face[:, h * 128 : (h + 1) * 128]

    def yface(dst, y):
        k = lane_iota((CZ, 128))
        m = jnp.zeros((CZ, 128), f32)
        for f in range(3):
            for x in range(CX):
                m = jnp.where(k == f * CX + x, near[f, x, :, y : y + 1], m)
        out[dst, 0:ROWS] = m

    @pl.when(dz > 0)
    def _():
        zface(me - 1, 0)

    @pl.when(dz < NDZ - 1)
    def _():
        zface(me + 1, CZ - 1)

    @pl.when(py > 0)
    def _():
        yface(me - NDZ, 0)

    @pl.when(py < NPY - 1)
    def _():
        yface(me + NDZ, CY - 1)


def near_kernel(near, got, xlow, xhigh, frac, sums):
    py = lax.axis_index("py")
    dz = lax.axis_index("dz")
    me = py * NDZ + dz
    at_l = jnp.maximum(me - NDZ, 0)
    at_r = jnp.minimum(me + NDZ, GRP - 1)
    at_d = jnp.maximum(me - 1, 0)
    at_u = jnp.minimum(me + 1, GRP - 1)
    left = jnp.where(py > 0, got[at_l, 0:ROWS], 0.0)
    right = jnp.where(py < NPY - 1, got[at_r, 0:ROWS], 0.0)
    down = jnp.where(dz > 0, got[at_d, 0:ROWS], 0.0)
    up = jnp.where(dz < NDZ - 1, got[at_u, 0:ROWS], 0.0)
    lane = lane_iota((CZ, CY))
    row = lax.broadcasted_iota(jnp.int32, (CZ, CY), 0)

    def face_row(face, f, x):
        return jnp.concatenate(
            [face[(f * 2 + h) * 8 + x : (f * 2 + h) * 8 + x + 1] for h in range(2)], axis=1
        )

    for p in range(CX):
        x = x_order(p)
        velx = near[1, x]
        vely = near[2, x]
        new = []
        for f in range(3):
            q = near[f, x]
            k = f * CX + x
            xp = near[f, x + 1] if x < CX - 1 else xhigh[f]
            xm = near[f, x - 1] if x > 0 else xlow[f]
            yp = jnp.where(lane == CY - 1, right[:, k : k + 1], pltpu.roll(q, CY - 1, 1))
            ym = jnp.where(lane == 0, left[:, k : k + 1], pltpu.roll(q, 1, 1))
            zp = jnp.where(row == CZ - 1, face_row(up, f, x), pltpu.roll(q, CZ - 1, 0))
            zm = jnp.where(row == 0, face_row(down, f, x), pltpu.roll(q, 1, 0))
            dx = xp - xm
            dy = yp - ym
            lap = xp + xm + yp + ym + zp + zm - 6.0 * q
            moved = q - advect_coef * (velx * dx + vely * dy) + diffuse_coef * lap
            if f == 0:
                fdx, fdy = dx, dy
            new.append(moved)
        frac[x] = new[0]
        parts = (
            new[0],
            new[0] * (new[1] - slope_coef * fdx),
            new[0] * (new[2] - slope_coef * fdy),
        )
        for f in range(3):
            total = jnp.sum(parts[f], axis=0, keepdims=True)
            for h in range(2):
                r = (f * 2 + h) * 8 + p
                sums[0, r : r + 1] = total[:, h * 128 : (h + 1) * 128]
    whole = sums[0]
    for b in range(1, GRP):
        sums[b] = whole


def scatter_kernel(scale, got, sums, depth, flows, mask, state, edges, top, bottom, bt, ah, al):
    me = lax.axis_index("py") * NDZ + lax.axis_index("dz")
    lanes = lane_iota((8, 128))
    ycell = lax.broadcasted_iota(jnp.int32, (NROW, 128), 0)
    xcell = lax.broadcasted_iota(jnp.int32, (FX, 128), 0)
    acc = jnp.zeros((NROW, 3 * FX), f32)
    for a in range(NPY):
        total = sums[a * NDZ]
        for b in range(1, NDZ):
            total = total + sums[a * NDZ + b]
        total = total * scale
        for h in range(2):
            d = a * NDZ + 2 * h
            code = jnp.where(lanes < 64, got[d, ROWS:BLK], got[d + 1, ROWS:BLK]).astype(jnp.int32)
            y = (code >> 14) * FY + (code & (FY - 1)) - me * FY
            y = jnp.where(y == -1, FY + 1, jnp.where(y > FY, -1, y))
            x = (code >> 8) & (FX - 1)
            for p in range(8):
                at = slice(p * 128, (p + 1) * 128)
                bt[:, at] = jnp.where(ycell == y[p : p + 1], 1.0, 0.0).astype(jnp.bfloat16)
                here = xcell == x[p : p + 1]
                for f in range(3):
                    r = (f * 2 + h) * 8 + p
                    value = total[r : r + 1]
                    high = value.astype(jnp.bfloat16).astype(f32)
                    cells = slice(f * FX, (f + 1) * FX)
                    ah[cells, at] = jnp.where(here, high, 0.0).astype(jnp.bfloat16)
                    al[cells, at] = jnp.where(here, value - high, 0.0).astype(jnp.bfloat16)
            over = (((1,), (1,)), ((), ()))
            acc = acc + lax.dot_general(bt[...], ah[...], over, preferred_element_type=f32)
            acc = acc + lax.dot_general(bt[...], al[...], over, preferred_element_type=f32)
    source = acc.T
    wet = mask[...].astype(f32)
    raw = (depth[...], flows[0], flows[1])
    cells = []
    for f in range(3):
        s = raw[f] + source[f * FX : (f + 1) * FX, 0:FY]
        cells.append(s if f == 0 else s * wet)
        state[f] = cells[f]
    blank = jnp.zeros((5, FY), f32)
    top[...] = jnp.concatenate([c[0:1] for c in cells] + [blank], axis=0)
    bottom[...] = jnp.concatenate([c[FX - 1 : FX] for c in cells] + [blank], axis=0)
    k = lane_iota((FX, 128))
    m = jnp.zeros((FX, 128), f32)
    for side in range(2):
        other = jnp.maximum(me - 1, 0) if side == 0 else jnp.minimum(me + 1, GRP - 1)
        block = got[other, ROWS:BLK]
        block = jnp.where((other % 2) == 1, block, pltpu.roll(block, 64, 1))
        e = jnp.concatenate([block] * 16, axis=0).T[0:FX]
        inside = (me > 0) if side == 0 else (me < GRP - 1)
        wet_e = e[:, 3:4]
        col = FY + 1 if side == 0 else FY
        for f in range(3):
            s = e[:, f : f + 1] + source[f * FX : (f + 1) * FX, col : col + 1]
            s = s if f == 0 else s * wet_e
            m = jnp.where((k == side * 3 + f) & inside, s, m)
    edges[...] = m


def terms(h, hu, hv, ok):
    inv = 1.0 / jnp.where(ok, h, 1.0)
    cross = hu * hv * inv
    press = 0.5 * gravity * h * h
    xf = (hu, hu * hu * inv + press, cross)
    yf = (hv, cross, hv * hv * inv + press)
    s = (h, hu, hv)
    return [
        (
            0.25 * s[f] - flux_coef * xf[f],
            0.25 * s[f] + flux_coef * xf[f],
            0.25 * s[f] - flux_coef * yf[f],
            0.25 * s[f] + flux_coef * yf[f],
        )
        for f in range(3)
    ]


def far_kernel(state, edges, above, below, out):
    px = lax.axis_index("px")
    n_px = lax.axis_size("px")
    me = lax.axis_index("py") * NDZ + lax.axis_index("dz")
    body = terms(state[0], state[1], state[2], True)
    e = edges[...]
    lo = terms(e[:, 0:1], e[:, 1:2], e[:, 2:3], me > 0)
    hi = terms(e[:, 3:4], e[:, 4:5], e[:, 5:6], me < GRP - 1)
    up = terms(above[0:1], above[1:2], above[2:3], px > 0)
    dn = terms(below[0:1], below[1:2], below[2:3], px < n_px - 1)
    lane = lane_iota((FX, FY))
    row = lax.broadcasted_iota(jnp.int32, (FX, FY), 0)
    for f in range(3):
        xp = jnp.where(row == FX - 1, dn[f][0], pltpu.roll(body[f][0], FX - 1, 0))
        xm = jnp.where(row == 0, up[f][1], pltpu.roll(body[f][1], 1, 0))
        yp = jnp.where(lane == FY - 1, hi[f][2], pltpu.roll(body[f][2], FY - 1, 1))
        ym = jnp.where(lane == 0, lo[f][3], pltpu.roll(body[f][3], 1, 1))
        out[f] = (xp + xm) + (yp + ym)


def shape(*dims):
    return jax.ShapeDtypeStruct(dims, f32)


def local(near_state, column_owner, landing, far_depth, far_flows, wet_mask):
    n_px = lax.axis_size("px")
    forth = [(i, i + 1) for i in range(n_px - 1)]
    back = [(i + 1, i) for i in range(n_px - 1)]
    owner = column_owner.reshape(4, 128)
    land = landing.reshape(4, 128)
    send, xlo, xhi = pl.pallas_call(
        pack_kernel,
        out_shape=(shape(GRP, BLK, 128), shape(3, CZ, CY), shape(3, CZ, CY)),
        in_specs=[VM] * 6,
        out_specs=(VM,) * 3,
        compiler_params=PARAMS,
        name="pack",
    )(near_state, owner, land, far_depth, far_flows, wet_mask)
    xlow = lax.ppermute(xhi, "px", forth)
    xhigh = lax.ppermute(xlo, "px", back)
    got = lax.all_to_all(send, GROUP, split_axis=0, concat_axis=0, tiled=True)
    new_frac, sums = pl.pallas_call(
        near_kernel,
        out_shape=(shape(CX, CZ, CY), shape(GRP, ROWS, 128)),
        in_specs=[VM] * 4,
        out_specs=(VM,) * 2,
        compiler_params=PARAMS,
        name="near",
    )(near_state, got, xlow, xhigh)
    sums = lax.all_to_all(sums, GROUP, split_axis=0, concat_axis=0, tiled=True)
    scale = column_height / (CZ * NDZ)
    state, edges, top, bottom = pl.pallas_call(
        functools.partial(scatter_kernel, scale),
        out_shape=(shape(3, FX, FY), shape(FX, 128), shape(8, FY), shape(8, FY)),
        in_specs=[VM] * 5,
        out_specs=(VM,) * 4,
        scratch_shapes=[
            pltpu.VMEM((NROW, 1024), jnp.bfloat16),
            pltpu.VMEM((3 * FX, 1024), jnp.bfloat16),
            pltpu.VMEM((3 * FX, 1024), jnp.bfloat16),
        ],
        compiler_params=PARAMS,
        name="scatter",
    )(got, sums, far_depth, far_flows, wet_mask)
    above = lax.ppermute(bottom, "px", forth)
    below = lax.ppermute(top, "px", back)
    far_new = pl.pallas_call(
        far_kernel,
        out_shape=shape(3, FX, FY),
        in_specs=[VM] * 4,
        out_specs=VM,
        compiler_params=PARAMS,
        name="far",
    )(state, edges, above, below)
    return (new_frac, far_new)


def solution(mesh):
    return jax.shard_map(
        local,
        mesh=mesh,
        in_specs=(
            P(None, "px", "dz", "py"),
            P("px", ("py", "dz"), None, None),
            P("px", ("py", "dz"), None),
            P("px", ("py", "dz")),
            P(None, "px", ("py", "dz")),
            P("px", ("py", "dz")),
        ),
        out_specs=(P("px", "dz", "py"), P(None, "px", ("py", "dz"))),
        check_vma=False,
    )
```

time: 152 us -> 68.2 us (0.45)
  the two profiles are of different devices: /device:TPU:18 before, /device:TPU:248 now
where the time goes in v1:
time: 68.2 us; the launch traced here: 67.7 us
  starting transfers between devices  20.5 us (30%)
  waiting for transfers between devices  17.8 us (26%)
  blocking collectives  14 us (21%)
  Pallas kernels  9.44 us (14%)
  local copies, waits for them, and re-layouts  5.23 us (8%)
  between operations  0.72 us (1%)
    all_to_all x1, blocking collectives, local(): sums = lax.all_to_all(sums, GROUP, split_axis=0, concat_axis=0, tiled=True)  14 us
    ppermute x1, waiting for transfers between devices, local(): xhigh = lax.ppermute(xlo, 'px', back)  8.6 us
    all_to_all x1, starting transfers between devices, local(): got = lax.all_to_all(send, GROUP, split_axis=0, concat_axis=0, tiled=True)  5.99 us
    ppermute x1, waiting for transfers between devices, local(): below = lax.ppermute(top, 'px', back)  5.95 us
    ppermute x1, starting transfers between devices, local(): xlow = lax.ppermute(xhi, 'px', forth)  5.7 us
    unnamed x20, local copies, waits for them, and re-layouts  5.23 us
    pallas_call x1, Pallas kernels, local(): pl.pallas_call(functools.partial(scatter_kernel, scale), out_shape=(shape...  5.1 us
    ppermute x1, starting transfers between devices, local(): below = lax.ppermute(top, 'px', back)  3.8 us
  transfers between devices with their start and end apart: 5, of which 3 were waited for; matrix products, arithmetic and copies ran while one was open for 0% of the time, Pallas kernels for 0%

profile of v1, /device:TPU:248, one launch (start us, length us, event | category | flops | bytes accessed | tf_op | source)
XLA Modules:
  0.0 67.7 jit_solution(16858658268013225665)
XLA Ops:
  0.6 1.3 %copy-done = f32[3,8,48,256]{3,2,1,0:T(8,128)S(1)} copy-done((f32[3,8,48,256]{3,2,1,0:T(8,128)S(1)}, f32[3,8,48,256]{3,2,1,0:T(8,128)}, u32[]{:S(2)}) %copy-start) | copy-done | bytes 1179672
  1.9 0.9 %copy-done.2 = f32[2,64,256]{2,1,0:T(8,128)S(1)} copy-done((f32[2,64,256]{2,1,0:T(8,128)S(1)}, f32[2,64,256]{2,1,0:T(8,128)}, u32[]{:S(2)}) %copy-start.2) | copy-done | bytes 131096
  2.8 0.8 %copy-done.4 = f32[64,256]{1,0:T(8,128)S(1)} copy-done((f32[64,256]{1,0:T(8,128)S(1)}, f32[64,256]{1,0:T(8,128)}, u32[]{:S(2)}) %copy-start.4) | copy-done | bytes 65560
  3.6 0.8 %copy-done.6 = s32[64,256]{1,0:T(8,128)S(1)} copy-done((s32[64,256]{1,0:T(8,128)S(1)}, s32[64,256]{1,0:T(8,128)}, u32[]{:S(2)}) %copy-start.6) | copy-done | bytes 65560
  4.5 0.7 %copy-done.8 = s32[1,1,512,1]{2,3,1,0:T(1,128)S(1)} copy-done((s32[1,1,512,1]{2,3,1,0:T(1,128)S(1)}, s32[1,1,512,1]{2,3,1,0:T(1,128)}, u32[]{:S(2)}) %copy-start.8) | copy-done | bytes 2072
  5.2 0.7 %copy-done.9 = s32[1,1,512]{2,1,0:T(1,128)S(1)} copy-done((s32[1,1,512]{2,1,0:T(1,128)S(1)}, s32[1,1,512]{2,1,0:T(1,128)}, u32[]{:S(2)}) %copy-start.9) | copy-done | bytes 2072
  5.9 1.4 %pack.1 = (f32[16,56,128]{2,1,0:T(8,128)}, f32[3,48,256]{2,1,0:T(8,128)S(1)}, f32[3,48,256]{2,1,0:T(8,128)S(1)}) custom-call(f32[3,8,48,256]{3,2,1,0:T(8,128)S(1)} %copy-done, s32[4,128]{1,0:T(4,128)S(1)} %bitcast.2, s32[4,128]{1,0:T(4,128)S(1)} %bitcast.3, f32[64,256]{1,0:T(8,128)S(1)} %copy-done.4, f32[2,64,256]{2,1,0:T(8,128)S(1)} %copy-done.2, ...), custom_call_target="tpu_custom_call" | custom-call | tf_op jit(solution)/shard_map/pack/pallas_call | solution.py:273
  7.2 6.0 %all-to-all-start = ((f32[16,56,128]{2,1,0:T(8,128)}), f32[16,56,128]{2,1,0:T(8,128)S(1)}, u32[]{:S(2)}, u32[]{:S(2)}) async-start(f32[16,56,128]{2,1,0:T(8,128)} %get-tuple-element.11), calls=%async_computation | async-start | bytes 917504 | tf_op jit(solution)/shard_map/all_to_all | solution.py:283
  13.2 5.7 %collective-permute-start = (f32[3,48,256]{2,1,0:T(8,128)S(1)}, f32[3,48,256]{2,1,0:T(8,128)S(1)}, u32[]{:S(2)}, u32[]{:S(2)}) collective-permute-start(f32[3,48,256]{2,1,0:T(8,128)S(1)} %get-tuple-element.12), channel_id=1, source_target_pairs={{0,16},{16,32},{32,48},{48,64},{64,80},{80,96},{96,112},{112,128},... | collective-permute-start | bytes 442376 | tf_op jit(solution)/shard_map/ppermute | solution.py:281
  18.9 0.0 copy-start.3
  18.9 0.0 copy-start.5
  18.9 0.0 copy-start.7
  19.0 2.1 %collective-permute-start.1 = (f32[3,48,256]{2,1,0:T(8,128)S(1)}, f32[3,48,256]{2,1,0:T(8,128)S(1)}, u32[]{:S(2)}, u32[]{:S(2)}) collective-permute-start(f32[3,48,256]{2,1,0:T(8,128)S(1)} %get-tuple-element.13), channel_id=1, source_target_pairs={{16,0},{32,16},{48,32},{64,48},{80,64},{96,80},{112,96},{128,112},... | collective-permute-start | bytes 442376 | tf_op jit(solution)/shard_map/ppermute | solution.py:282
  21.0 3.3 %collective-permute-done.xlow = f32[3,48,256]{2,1,0:T(8,128)S(1)} collective-permute-done((f32[3,48,256]{2,1,0:T(8,128)S(1)}, f32[3,48,256]{2,1,0:T(8,128)S(1)}, u32[]{:S(2)}, u32[]{:S(2)}) %collective-permute-start) | collective-permute-done | bytes 147488 | tf_op jit(solution)/shard_map/ppermute | solution.py:281
  24.3 8.6 %collective-permute-done.1.xhigh = f32[3,48,256]{2,1,0:T(8,128)S(1)} collective-permute-done((f32[3,48,256]{2,1,0:T(8,128)S(1)}, f32[3,48,256]{2,1,0:T(8,128)S(1)}, u32[]{:S(2)}, u32[]{:S(2)}) %collective-permute-start.1) | collective-permute-done | bytes 147488 | tf_op jit(solution)/shard_map/ppermute | solution.py:282
  32.9 0.0 all-to-all-done.got
  32.9 1.9 %near.4 = (f32[8,48,256]{2,1,0:T(8,128)}, f32[16,48,128]{2,1,0:T(8,128)S(1)}) custom-call(f32[3,8,48,256]{3,2,1,0:T(8,128)S(1)} %copy-done.1, f32[16,56,128]{2,1,0:T(8,128)S(1)} %all-to-all-done.got, f32[3,48,256]{2,1,0:T(8,128)S(1)} %collective-permute-done.xlow, f32[3,48,256]{2,1,0:T(8,128)S(1)} %collective-permute-done.1.xhigh), custom_call_target="tpu_custom_call" | custom-call | tf_op jit(solution)/shard_map/near/pallas_call | solution.py:284
  34.8 14.0 %all_to_all.10.sums = f32[16,48,128]{2,1,0:T(8,128)S(1)} all-to-all(f32[16,48,128]{2,1,0:T(8,128)S(1)} %get-tuple-element.15), channel_id=1, replica_groups=mesh['px'=48,'py'=4,'dz'=4] {'py','dz'}, dimensions={0} | all-to-all | bytes 786432 | tf_op jit(solution)/shard_map/all_to_all | solution.py:292
  48.8 5.1 %scatter.1 = (f32[3,64,256]{2,1,0:T(8,128)S(1)}, f32[64,128]{1,0:T(8,128)S(1)}, f32[8,256]{1,0:T(8,128)S(1)}, f32[8,256]{1,0:T(8,128)S(1)}) custom-call(f32[16,56,128]{2,1,0:T(8,128)S(1)} %all-to-all-done.got, f32[16,48,128]{2,1,0:T(8,128)S(1)} %all_to_all.10.sums, f32[64,256]{1,0:T(8,128)S(1)} %copy-done.5, f32[2,64,256]{2,1,0:T(8,128)S(1)} %copy-done.3, ...), custom_call_target="tpu_custom_call" | custom-call | tf_op jit(solution)/shard_map/scatter/pallas_call | solution.py:294
  53.9 2.9 %collective-permute-start.2 = (f32[8,256]{1,0:T(8,128)S(1)}, f32[8,256]{1,0:T(8,128)S(1)}, u32[]{:S(2)}, u32[]{:S(2)}) collective-permute-start(f32[8,256]{1,0:T(8,128)S(1)} %get-tuple-element.18), channel_id=1, source_target_pairs={{0,16},{16,32},{32,48},{48,64},{64,80},{80,96},{96,112},{112,128},... | collective-permute-start | bytes 24584 | tf_op jit(solution)/shard_map/ppermute | solution.py:307
  56.9 3.8 %collective-permute-start.3 = (f32[8,256]{1,0:T(8,128)S(1)}, f32[8,256]{1,0:T(8,128)S(1)}, u32[]{:S(2)}, u32[]{:S(2)}) collective-permute-start(f32[8,256]{1,0:T(8,128)S(1)} %get-tuple-element.19), channel_id=1, source_target_pairs={{16,0},{32,16},{48,32},{64,48},{80,64},{96,80},{112,96},{128,112},... | collective-permute-start | bytes 24584 | tf_op jit(solution)/shard_map/ppermute | solution.py:308
  60.7 0.0 collective-permute-done.2.above
  60.7 5.9 %collective-permute-done.3.below = f32[8,256]{1,0:T(8,128)S(1)} collective-permute-done((f32[8,256]{1,0:T(8,128)S(1)}, f32[8,256]{1,0:T(8,128)S(1)}, u32[]{:S(2)}, u32[]{:S(2)}) %collective-permute-start.3) | collective-permute-done | bytes 8224 | tf_op jit(solution)/shard_map/ppermute | solution.py:308
  66.6 1.0 %far.1 = f32[3,64,256]{2,1,0:T(8,128)} custom-call(f32[3,64,256]{2,1,0:T(8,128)S(1)} %get-tuple-element.16.state, f32[64,128]{1,0:T(8,128)S(1)} %get-tuple-element.17.edges, f32[8,256]{1,0:T(8,128)S(1)} %collective-permute-done.2.above, f32[8,256]{1,0:T(8,128)S(1)} %collective-permute-done.3.below), custom_call_target="tpu_custom_call" | custom-call | tf_op jit(solution)/shard_map/far/pallas_call | solution.py:309
  (11 shorter events, 0.0 us)
Async XLA Ops:
  0.6 1.3 %copy-start = (f32[3,8,48,256]{3,2,1,0:T(8,128)S(1)}, f32[3,8,48,256]{3,2,1,0:T(8,128)}, u32[]{:S(2)}) copy-start(f32[3,8,48,256]{3,2,1,0:T(8,128)} %near.5) | copy-start | bytes 3538948
  1.9 0.9 %copy-start.2 = (f32[2,64,256]{2,1,0:T(8,128)S(1)}, f32[2,64,256]{2,1,0:T(8,128)}, u32[]{:S(2)}) copy-start(f32[2,64,256]{2,1,0:T(8,128)} %flows.3) | copy-start | bytes 393220
  2.8 0.8 %copy-start.4 = (f32[64,256]{1,0:T(8,128)S(1)}, f32[64,256]{1,0:T(8,128)}, u32[]{:S(2)}) copy-start(f32[64,256]{1,0:T(8,128)} %depth.3) | copy-start | bytes 196612
  3.6 0.8 %copy-start.6 = (s32[64,256]{1,0:T(8,128)S(1)}, s32[64,256]{1,0:T(8,128)}, u32[]{:S(2)}) copy-start(s32[64,256]{1,0:T(8,128)} %mask.3) | copy-start | bytes 196612
  4.5 0.7 %copy-start.8 = (s32[1,1,512,1]{2,3,1,0:T(1,128)S(1)}, s32[1,1,512,1]{2,3,1,0:T(1,128)}, u32[]{:S(2)}) copy-start(s32[1,1,512,1]{2,3,1,0:T(1,128)} %param.7) | copy-start | bytes 6148
  5.2 0.7 %copy-start.9 = (s32[1,1,512]{2,1,0:T(1,128)S(1)}, s32[1,1,512]{2,1,0:T(1,128)}, u32[]{:S(2)}) copy-start(s32[1,1,512]{2,1,0:T(1,128)} %param.8) | copy-start | bytes 6148
  5.9 27.0 %copy-start.1 = (f32[3,8,48,256]{3,2,1,0:T(8,128)S(1)}, f32[3,8,48,256]{3,2,1,0:T(8,128)}, u32[]{:S(2)}) copy-start(f32[3,8,48,256]{3,2,1,0:T(8,128)} %near.5) | copy-start | bytes 3538948
  7.2 25.7 %all-to-all-start = ((f32[16,56,128]{2,1,0:T(8,128)}), f32[16,56,128]{2,1,0:T(8,128)S(1)}, u32[]{:S(2)}, u32[]{:S(2)}) async-start(f32[16,56,128]{2,1,0:T(8,128)} %get-tuple-element.11), calls=%async_computation | async-start | bytes 917504 | tf_op jit(solution)/shard_map/all_to_all | solution.py:283
  13.2 11.1 %collective-permute-start = (f32[3,48,256]{2,1,0:T(8,128)S(1)}, f32[3,48,256]{2,1,0:T(8,128)S(1)}, u32[]{:S(2)}, u32[]{:S(2)}) collective-permute-start(f32[3,48,256]{2,1,0:T(8,128)S(1)} %get-tuple-element.12), channel_id=1, source_target_pairs={{0,16},{16,32},{32,48},{48,64},{64,80},{80,96},{96,112},{112,128},... | collective-permute-start | bytes 442376 | tf_op jit(solution)/shard_map/ppermute | solution.py:281
  18.9 29.9 %copy-start.3 = (f32[2,64,256]{2,1,0:T(8,128)S(1)}, f32[2,64,256]{2,1,0:T(8,128)}, u32[]{:S(2)}) copy-start(f32[2,64,256]{2,1,0:T(8,128)} %flows.3) | copy-start | bytes 393220
  18.9 29.9 %copy-start.5 = (f32[64,256]{1,0:T(8,128)S(1)}, f32[64,256]{1,0:T(8,128)}, u32[]{:S(2)}) copy-start(f32[64,256]{1,0:T(8,128)} %depth.3) | copy-start | bytes 196612
  18.9 29.9 %copy-start.7 = (s32[64,256]{1,0:T(8,128)S(1)}, s32[64,256]{1,0:T(8,128)}, u32[]{:S(2)}) copy-start(s32[64,256]{1,0:T(8,128)} %mask.3) | copy-start | bytes 196612
  19.0 13.9 %collective-permute-start.1 = (f32[3,48,256]{2,1,0:T(8,128)S(1)}, f32[3,48,256]{2,1,0:T(8,128)S(1)}, u32[]{:S(2)}, u32[]{:S(2)}) collective-permute-start(f32[3,48,256]{2,1,0:T(8,128)S(1)} %get-tuple-element.13), channel_id=1, source_target_pairs={{16,0},{32,16},{48,32},{64,48},{80,64},{96,80},{112,96},{128,112},... | collective-permute-start | bytes 442376 | tf_op jit(solution)/shard_map/ppermute | solution.py:282
  53.9 6.8 %collective-permute-start.2 = (f32[8,256]{1,0:T(8,128)S(1)}, f32[8,256]{1,0:T(8,128)S(1)}, u32[]{:S(2)}, u32[]{:S(2)}) collective-permute-start(f32[8,256]{1,0:T(8,128)S(1)} %get-tuple-element.18), channel_id=1, source_target_pairs={{0,16},{16,32},{32,48},{48,64},{64,80},{80,96},{96,112},{112,128},... | collective-permute-start | bytes 24584 | tf_op jit(solution)/shard_map/ppermute | solution.py:307
  56.9 9.8 %collective-permute-start.3 = (f32[8,256]{1,0:T(8,128)S(1)}, f32[8,256]{1,0:T(8,128)S(1)}, u32[]{:S(2)}, u32[]{:S(2)}) collective-permute-start(f32[8,256]{1,0:T(8,128)S(1)} %get-tuple-element.19), channel_id=1, source_target_pairs={{16,0},{32,16},{48,32},{64,48},{80,64},{96,80},{112,96},{128,112},... | collective-permute-start | bytes 24584 | tf_op jit(solution)/shard_map/ppermute | solution.py:308

commit v2 on v1

--- a/solution.py
+++ b/solution.py
@@ -6,6 +6,7 @@
 from jax.experimental import pallas as pl
 from jax.experimental.pallas import tpu as pltpu
 from jax.sharding import PartitionSpec as P
+
 
 advect_coef = 0.25
 diffuse_coef = 0.1
@@ -29,7 +30,9 @@
 f32 = jnp.float32
 GROUP = ("py", "dz")
 VM = pl.BlockSpec(memory_space=pltpu.VMEM)
-PARAMS = pltpu.CompilerParams(vmem_limit_bytes=24 << 20)
+ANY = pl.BlockSpec(memory_space=pl.ANY)
+PARAMS = pltpu.CompilerParams(vmem_limit_bytes=8 << 20)
+HBM = pl.BlockSpec(memory_space=pltpu.HBM)
 
 
 def lane_iota(shape):
@@ -40,12 +43,20 @@
     return 2 * row if row < 4 else 2 * (row - 4) + 1
 
 
-def pack_kernel(near, owner, land, depth, flows, mask, out, xlo, xhi):
+def load_kernel(*refs):
+    sources, copies, (xlo, xhi), sem = refs[:6], refs[6:12], refs[12:14], refs[14]
+    moves = [(sources[0].at[:, 0], xlo), (sources[0].at[:, CX - 1], xhi), *zip(sources, copies)]
+    moves = [pltpu.make_async_copy(a, b, sem.at[n]) for n, (a, b) in enumerate(moves)]
+    for move in moves:
+        move.start()
+    for move in moves:
+        move.wait()
+
+
+def pack_kernel(near, owner, land, depth, flows, mask, out):
     py = lax.axis_index("py")
     dz = lax.axis_index("dz")
     me = py * NDZ + dz
-    xlo[...] = near[:, 0]
-    xhi[...] = near[:, CX - 1]
     code = (owner[...] * (FX * FY) + land[...]).astype(f32)
     swap = pltpu.roll(code, 64, 1)
     odd = (me % 2) == 1
@@ -163,63 +174,78 @@
         sums[b] = whole
 
 
-def scatter_kernel(scale, got, sums, depth, flows, mask, state, edges, top, bottom, bt, ah, al):
+def decode(got, me, a, h):
+    d = a * NDZ + 2 * h
+    lanes = lane_iota((8, 128))
+    code = jnp.where(lanes < 64, got[d, ROWS:BLK], got[d + 1, ROWS:BLK]).astype(jnp.int32)
+    y = (code >> 14) * FY + (code & (FY - 1)) - me * FY
+    y = jnp.where((y < -1) | (y > FY), -128, y)
+    return y.astype(f32), ((code >> 8) & (FX - 1)).astype(f32)
+
+
+def tall(row, rows):
+    tile = jnp.broadcast_to(row, (16, 128)).astype(jnp.bfloat16)
+    return jnp.concatenate([tile] * (rows // 16), axis=0)
+
+
+def cell_rows(rows):
+    r = lax.broadcasted_iota(jnp.int32, (rows, 128), 0)
+    r = jnp.where(r > FY, FY - r, r)
+    return r.astype(f32).astype(jnp.bfloat16)
+
+
+OVER = (((1,), (1,)), ((), ()))
+
+
+def split(row, rows):
+    tile = jnp.broadcast_to(row, (16, 128))
+    high = tile.astype(jnp.bfloat16)
+    low = (tile - high.astype(f32)).astype(jnp.bfloat16)
+    return [jnp.concatenate([t] * (rows // 16), axis=0) for t in (high, low)]
+
+
+def edge_kernel(scale, got, sums, depth, flows, mask, total, top, bottom, bits, lhs):
     me = lax.axis_index("py") * NDZ + lax.axis_index("dz")
-    lanes = lane_iota((8, 128))
-    ycell = lax.broadcasted_iota(jnp.int32, (NROW, 128), 0)
-    xcell = lax.broadcasted_iota(jnp.int32, (FX, 128), 0)
-    acc = jnp.zeros((NROW, 3 * FX), f32)
+    row = lax.broadcasted_iota(jnp.int32, (16, 128), 0)
+    part = row & 7
+    field = jnp.where(part >= 3, part - 3, part)
+    edge = jnp.where(part >= 3, FX - 1, 0)
+    edge = jnp.where(part >= 6, -1, edge)
+    edge = edge.astype(f32)
+    low = row >= 8
+    ycell = cell_rows(FY)
+    one = jnp.ones((FY, 128), jnp.bfloat16)
+    acc = jnp.zeros((16, FY), f32)
     for a in range(NPY):
-        total = sums[a * NDZ]
+        t = sums[a * NDZ]
         for b in range(1, NDZ):
-            total = total + sums[a * NDZ + b]
-        total = total * scale
+            t = t + sums[a * NDZ + b]
+        t = t * scale
+        total[a] = t
         for h in range(2):
-            d = a * NDZ + 2 * h
-            code = jnp.where(lanes < 64, got[d, ROWS:BLK], got[d + 1, ROWS:BLK]).astype(jnp.int32)
-            y = (code >> 14) * FY + (code & (FY - 1)) - me * FY
-            y = jnp.where(y == -1, FY + 1, jnp.where(y > FY, -1, y))
-            x = (code >> 8) & (FX - 1)
+            y, x = decode(got, me, a, h)
             for p in range(8):
                 at = slice(p * 128, (p + 1) * 128)
-                bt[:, at] = jnp.where(ycell == y[p : p + 1], 1.0, 0.0).astype(jnp.bfloat16)
-                here = xcell == x[p : p + 1]
+                bits[:, at] = jnp.where(ycell == tall(y[p : p + 1], FY), one, one * 0)
+                value = None
                 for f in range(3):
                     r = (f * 2 + h) * 8 + p
-                    value = total[r : r + 1]
-                    high = value.astype(jnp.bfloat16).astype(f32)
-                    cells = slice(f * FX, (f + 1) * FX)
-                    ah[cells, at] = jnp.where(here, high, 0.0).astype(jnp.bfloat16)
-                    al[cells, at] = jnp.where(here, value - high, 0.0).astype(jnp.bfloat16)
-            over = (((1,), (1,)), ((), ()))
-            acc = acc + lax.dot_general(bt[...], ah[...], over, preferred_element_type=f32)
-            acc = acc + lax.dot_general(bt[...], al[...], over, preferred_element_type=f32)
-    source = acc.T
-    wet = mask[...].astype(f32)
-    raw = (depth[...], flows[0], flows[1])
-    cells = []
-    for f in range(3):
-        s = raw[f] + source[f * FX : (f + 1) * FX, 0:FY]
-        cells.append(s if f == 0 else s * wet)
-        state[f] = cells[f]
+                    whole = jnp.broadcast_to(t[r : r + 1], (16, 128))
+                    high = whole.astype(jnp.bfloat16).astype(f32)
+                    both = jnp.where(low, whole - high, high)
+                    value = both if f == 0 else jnp.where(field == f, both, value)
+                value = jnp.where(edge == x[p : p + 1], value, 0.0)
+                lhs[:, at] = value.astype(jnp.bfloat16)
+            acc = acc + lax.dot_general(lhs[...], bits[...], OVER, preferred_element_type=f32)
+    acc = acc[0:8] + acc[8:16]
     blank = jnp.zeros((5, FY), f32)
-    top[...] = jnp.concatenate([c[0:1] for c in cells] + [blank], axis=0)
-    bottom[...] = jnp.concatenate([c[FX - 1 : FX] for c in cells] + [blank], axis=0)
-    k = lane_iota((FX, 128))
-    m = jnp.zeros((FX, 128), f32)
-    for side in range(2):
-        other = jnp.maximum(me - 1, 0) if side == 0 else jnp.minimum(me + 1, GRP - 1)
-        block = got[other, ROWS:BLK]
-        block = jnp.where((other % 2) == 1, block, pltpu.roll(block, 64, 1))
-        e = jnp.concatenate([block] * 16, axis=0).T[0:FX]
-        inside = (me > 0) if side == 0 else (me < GRP - 1)
-        wet_e = e[:, 3:4]
-        col = FY + 1 if side == 0 else FY
-        for f in range(3):
-            s = e[:, f : f + 1] + source[f * FX : (f + 1) * FX, col : col + 1]
-            s = s if f == 0 else s * wet_e
-            m = jnp.where((k == side * 3 + f) & inside, s, m)
-    edges[...] = m
+    for e, out in ((0, top), (1, bottom)):
+        at = 0 if e == 0 else FX - 1
+        wet = mask[at : at + 1].astype(f32)
+        h = depth[at : at + 1] + acc[e * 3 : e * 3 + 1]
+        hu = (flows[0, at : at + 1] + acc[e * 3 + 1 : e * 3 + 2]) * wet
+        hv = (flows[1, at : at + 1] + acc[e * 3 + 2 : e * 3 + 3]) * wet
+        out[...] = jnp.concatenate([h, hu, hv, blank], axis=0)
 
 
 def terms(h, hu, hv, ok):
@@ -240,28 +266,89 @@
     ]
 
 
-def far_kernel(state, edges, above, below, out):
-    px = lax.axis_index("px")
-    n_px = lax.axis_size("px")
+def far_kernel(got, total, depth, flows, mask, out, head, tail, bits, ah, al):
     me = lax.axis_index("py") * NDZ + lax.axis_index("dz")
-    body = terms(state[0], state[1], state[2], True)
-    e = edges[...]
-    lo = terms(e[:, 0:1], e[:, 1:2], e[:, 2:3], me > 0)
-    hi = terms(e[:, 3:4], e[:, 4:5], e[:, 5:6], me < GRP - 1)
-    up = terms(above[0:1], above[1:2], above[2:3], px > 0)
-    dn = terms(below[0:1], below[1:2], below[2:3], px < n_px - 1)
+    xcell = lax.broadcasted_iota(jnp.int32, (FX, 128), 0).astype(f32).astype(jnp.bfloat16)
+    ycell = cell_rows(NROW)
+    one = jnp.ones((NROW, 128), jnp.bfloat16)
+    zero = jnp.zeros((FX, 128), jnp.bfloat16)
+    acc = jnp.zeros((NROW, 3 * FX), f32)
+    for a in range(NPY):
+        for h in range(2):
+            y, x = decode(got, me, a, h)
+            for p in range(8):
+                at = slice(p * 128, (p + 1) * 128)
+                bits[:, at] = jnp.where(ycell == tall(y[p : p + 1], NROW), one, one * 0)
+                here = xcell == tall(x[p : p + 1], FX)
+                for f in range(3):
+                    r = (f * 2 + h) * 8 + p
+                    high, low = split(total[a, r : r + 1], FX)
+                    cells = slice(f * FX, (f + 1) * FX)
+                    ah[cells, at] = jnp.where(here, high, zero)
+                    al[cells, at] = jnp.where(here, low, zero)
+            for part in (ah, al):
+                acc = acc + lax.dot_general(bits[...], part[...], OVER, preferred_element_type=f32)
+    source = acc.T
+    wet = mask[...].astype(f32)
+    raw = (depth[...], flows[0], flows[1])
+    cells = []
+    for f in range(3):
+        s = raw[f] + source[f * FX : (f + 1) * FX, 0:FY]
+        cells.append(s if f == 0 else s * wet)
+    body = terms(*cells, True)
+    sides = []
+    for side in range(2):
+        other = jnp.maximum(me - 1, 0) if side == 0 else jnp.minimum(me + 1, GRP - 1)
+        block = got[other, ROWS:BLK]
+        block = jnp.where((other % 2) == 1, block, pltpu.roll(block, 64, 1))
+        e = jnp.concatenate([block] * 16, axis=0).T[0:FX]
+        inside = (me > 0) if side == 0 else (me < GRP - 1)
+        col = FY + 1 if side == 0 else FY
+        s = []
+        for f in range(3):
+            v = e[:, f : f + 1] + source[f * FX : (f + 1) * FX, col : col + 1]
+            v = v if f == 0 else v * e[:, 3:4]
+            s.append(jnp.where(inside, v, 0.0))
+        sides.append(terms(*s, inside))
     lane = lane_iota((FX, FY))
     row = lax.broadcasted_iota(jnp.int32, (FX, FY), 0)
     for f in range(3):
-        xp = jnp.where(row == FX - 1, dn[f][0], pltpu.roll(body[f][0], FX - 1, 0))
-        xm = jnp.where(row == 0, up[f][1], pltpu.roll(body[f][1], 1, 0))
-        yp = jnp.where(lane == FY - 1, hi[f][2], pltpu.roll(body[f][2], FY - 1, 1))
-        ym = jnp.where(lane == 0, lo[f][3], pltpu.roll(body[f][3], 1, 1))
-        out[f] = (xp + xm) + (yp + ym)
+        xp = jnp.where(row == FX - 1, 0.0, pltpu.roll(body[f][0], FX - 1, 0))
+        xm = jnp.where(row == 0, 0.0, pltpu.roll(body[f][1], 1, 0))
+        yp = jnp.where(lane == FY - 1, sides[1][f][2], pltpu.roll(body[f][2], FY - 1, 1))
+        ym = jnp.where(lane == 0, sides[0][f][3], pltpu.roll(body[f][3], 1, 1))
+        new = (xp + xm) + (yp + ym)
+        out[f] = new
+        head[f] = new[0:8]
+        tail[f] = new[FX - 8 : FX]
+
+
+def join_kernel(part, head, tail, above, below, out, new, sem):
+    px = lax.axis_index("px")
+    up = terms(above[0:1], above[1:2], above[2:3], px > 0)
+    dn = terms(below[0:1], below[1:2], below[2:3], px < lax.axis_size("px") - 1)
+    row = lax.broadcasted_iota(jnp.int32, (8, FY), 0)
+    for f in range(3):
+        new[0, f] = head[f] + jnp.where(row == 0, up[f][1], 0.0)
+        new[1, f] = tail[f] + jnp.where(row == 7, dn[f][0], 0.0)
+    first = pltpu.make_async_copy(new.at[0], out.at[:, 0:8], sem.at[0])
+    last = pltpu.make_async_copy(new.at[1], out.at[:, FX - 8 : FX], sem.at[1])
+    first.start()
+    last.start()
+    first.wait()
+    last.wait()
 
 
 def shape(*dims):
     return jax.ShapeDtypeStruct(dims, f32)
+
+
+def vmem(*dims):
+    return pltpu.VMEM(dims, f32)
+
+
+def cost(micros):
+    return pl.CostEstimate(flops=0, bytes_accessed=micros * 3_000_000, transcendentals=0)
 
 
 def local(near_state, column_owner, landing, far_depth, far_flows, wet_mask):
@@ -270,16 +357,30 @@
     back = [(i + 1, i) for i in range(n_px - 1)]
     owner = column_owner.reshape(4, 128)
     land = landing.reshape(4, 128)
-    send, xlo, xhi = pl.pallas_call(
+    given = (near_state, owner, land, far_depth, far_flows, wet_mask)
+    *given, xlo, xhi = pl.pallas_call(
+        load_kernel,
+        out_shape=[pltpu.VMEM(x.shape, x.dtype) for x in given]
+        + [vmem(3, CZ, CY)] * 2,
+        in_specs=[HBM] * 6,
+        out_specs=[VM] * 8,
+        scratch_shapes=[pltpu.SemaphoreType.DMA((8,))],
+        compiler_params=PARAMS,
+        cost_estimate=cost(1),
+        name="load",
+    )(*[pltpu.with_memory_space_constraint(x, pltpu.HBM) for x in given])
+    near_state, owner, land, far_depth, far_flows, wet_mask = given
+    xlow = lax.ppermute(xhi, "px", forth)
+    xhigh = lax.ppermute(xlo, "px", back)
+    send = pl.pallas_call(
         pack_kernel,
-        out_shape=(shape(GRP, BLK, 128), shape(3, CZ, CY), shape(3, CZ, CY)),
+        out_shape=shape(GRP, BLK, 128),
         in_specs=[VM] * 6,
-        out_specs=(VM,) * 3,
-        compiler_params=PARAMS,
+        out_specs=VM,
+        compiler_params=PARAMS,
+        cost_estimate=cost(2),
         name="pack",
     )(near_state, owner, land, far_depth, far_flows, wet_mask)
-    xlow = lax.ppermute(xhi, "px", forth)
-    xhigh = lax.ppermute(xlo, "px", back)
     got = lax.all_to_all(send, GROUP, split_axis=0, concat_axis=0, tiled=True)
     new_frac, sums = pl.pallas_call(
         near_kernel,
@@ -287,33 +388,50 @@
         in_specs=[VM] * 4,
         out_specs=(VM,) * 2,
         compiler_params=PARAMS,
+        cost_estimate=cost(2),
         name="near",
     )(near_state, got, xlow, xhigh)
     sums = lax.all_to_all(sums, GROUP, split_axis=0, concat_axis=0, tiled=True)
-    scale = column_height / (CZ * NDZ)
-    state, edges, top, bottom = pl.pallas_call(
-        functools.partial(scatter_kernel, scale),
-        out_shape=(shape(3, FX, FY), shape(FX, 128), shape(8, FY), shape(8, FY)),
+    total, top, bottom = pl.pallas_call(
+        functools.partial(edge_kernel, column_height / (CZ * NDZ)),
+        out_shape=(vmem(NPY, ROWS, 128), vmem(8, FY), vmem(8, FY)),
         in_specs=[VM] * 5,
-        out_specs=(VM,) * 4,
+        out_specs=(VM,) * 3,
+        scratch_shapes=[
+            pltpu.VMEM((FY, 1024), jnp.bfloat16),
+            pltpu.VMEM((16, 1024), jnp.bfloat16),
+        ],
+        compiler_params=PARAMS,
+        cost_estimate=cost(2),
+        name="edge",
+    )(got, sums, far_depth, far_flows, wet_mask)
+    above = lax.ppermute(bottom, "px", forth)
+    below = lax.ppermute(top, "px", back)
+    part, head, tail = pl.pallas_call(
+        far_kernel,
+        out_shape=(shape(3, FX, FY), vmem(3, 8, FY), vmem(3, 8, FY)),
+        in_specs=[VM] * 5,
+        out_specs=(VM,) * 3,
         scratch_shapes=[
             pltpu.VMEM((NROW, 1024), jnp.bfloat16),
             pltpu.VMEM((3 * FX, 1024), jnp.bfloat16),
             pltpu.VMEM((3 * FX, 1024), jnp.bfloat16),
         ],
         compiler_params=PARAMS,
-        name="scatter",
-    )(got, sums, far_depth, far_flows, wet_mask)
-    above = lax.ppermute(bottom, "px", forth)
-    below = lax.ppermute(top, "px", back)
+        cost_estimate=cost(5),
+        name="far",
+    )(got, total, far_depth, far_flows, wet_mask)
     far_new = pl.pallas_call(
-        far_kernel,
+        join_kernel,
         out_shape=shape(3, FX, FY),
-        in_specs=[VM] * 4,
-        out_specs=VM,
-        compiler_params=PARAMS,
-        name="far",
-    )(state, edges, above, below)
+        in_specs=[ANY] + [VM] * 4,
+        out_specs=ANY,
+        scratch_shapes=[pltpu.VMEM((2, 3, 8, FY), f32), pltpu.SemaphoreType.DMA((2,))],
+        input_output_aliases={0: 0},
+        compiler_params=PARAMS,
+        cost_estimate=cost(1),
+        name="join",
+    )(part, head, tail, above, below)
     return (new_frac, far_new)
 
 

time: 68.2 us -> 61.3 us (0.90)
  the two profiles are of different devices: /device:TPU:248 before, /device:TPU:256 now
where the time goes in v2:
time: 61.3 us; the launch traced here: 60.9 us
  starting transfers between devices  25.9 us (42%)
  blocking collectives  14.2 us (23%)
  Pallas kernels  12.6 us (21%)
  waiting for transfers between devices  7.62 us (12%)
  between operations  0.69 us (1%)
    all_to_all x1, blocking collectives, local(): sums = lax.all_to_all(sums, GROUP, split_axis=0, concat_axis=0, tiled=True)  14.2 us
    ppermute x1, starting transfers between devices, local(): below = lax.ppermute(top, 'px', back)  5.81 us
    all_to_all x1, starting transfers between devices, local(): got = lax.all_to_all(send, GROUP, split_axis=0, concat_axis=0, tiled=True)  5.74 us
    ppermute x1, starting transfers between devices, local(): xhigh = lax.ppermute(xlo, 'px', back)  5.56 us
    ppermute x1, waiting for transfers between devices, local(): xlow = lax.ppermute(xhi, 'px', forth)  5.48 us
    pallas_call x1, Pallas kernels, local(): pl.pallas_call(far_kernel, out_shape=(shape(3, FX, FY), vmem(3, 8, FY), v...  5.27 us
    ppermute x1, starting transfers between devices, local(): xlow = lax.ppermute(xhi, 'px', forth)  4.5 us
    ppermute x1, starting transfers between devices, local(): above = lax.ppermute(bottom, 'px', forth)  4.25 us
  transfers between devices with their start and end apart: 5, of which 2 were waited for; matrix products, arithmetic and copies ran while one was open for 0% of the time, Pallas kernels for 9%

profile of v2, /device:TPU:256, one launch (start us, length us, event | category | flops | bytes accessed | tf_op | source)
XLA Modules:
  0.0 60.9 jit_solution(13880310281292399799)
XLA Ops:
  0.6 1.5 %load.1 = (f32[3,8,48,256]{3,2,1,0:T(8,128)S(1)}, s32[4,128]{1,0:T(4,128)S(1)}, s32[4,128]{1,0:T(4,128)S(1)}, f32[64,256]{1,0:T(8,128)S(1)}, f32[2,64,256]{2,1,0...) custom-call(f32[3,8,48,256]{3,2,1,0:T(8,128)} %refs_0_.1, ...), custom_call_target="tpu_custom_call" | custom-call | bytes 3000000 | tf_op jit(solution)/shard_map/load/pallas_call | solution.py:361
  2.2 1.2 %pack.1 = f32[16,56,128]{2,1,0:T(8,128)} custom-call(f32[3,8,48,256]{3,2,1,0:T(8,128)S(1)} %get-tuple-element.18.near, s32[4,128]{1,0:T(4,128)S(1)} %get-tuple-element.19.owner, s32[4,128]{1,0:T(4,128)S(1)} %get-tuple-element.20.land, f32[64,256]{1,0:T(8,128)S(1)} %get-tuple-element.21.depth, f32[2,64,256]{2,1,0:T(8,128)S(1)} %get-tuple-element.22.flows, ...), custom_call_target="tpu_custom_call" | custom-call | bytes 6000000 | tf_op jit(solution)/shard_map/pack/pallas_call | solution.py:375
  3.4 5.7 %all-to-all-start = ((f32[16,56,128]{2,1,0:T(8,128)}), f32[16,56,128]{2,1,0:T(8,128)S(1)}, u32[]{:S(2)}, u32[]{:S(2)}) async-start(f32[16,56,128]{2,1,0:T(8,128)} %pack.1), calls=%async_computation | async-start | bytes 917504 | tf_op jit(solution)/shard_map/all_to_all | solution.py:384
  9.2 4.5 %collective-permute-start = (f32[3,48,256]{2,1,0:T(8,128)S(1)}, f32[3,48,256]{2,1,0:T(8,128)S(1)}, u32[]{:S(2)}, u32[]{:S(2)}) collective-permute-start(f32[3,48,256]{2,1,0:T(8,128)S(1)} %get-tuple-element.24), channel_id=1, source_target_pairs={{0,16},{16,32},{32,48},{48,64},{64,80},{80,96},{96,112},{112,128},... | collective-permute-start | bytes 442376 | tf_op jit(solution)/shard_map/ppermute | solution.py:373
  13.7 5.6 %collective-permute-start.1 = (f32[3,48,256]{2,1,0:T(8,128)S(1)}, f32[3,48,256]{2,1,0:T(8,128)S(1)}, u32[]{:S(2)}, u32[]{:S(2)}) collective-permute-start(f32[3,48,256]{2,1,0:T(8,128)S(1)} %get-tuple-element.25), channel_id=1, source_target_pairs={{16,0},{32,16},{48,32},{64,48},{80,64},{96,80},{112,96},{128,112},... | collective-permute-start | bytes 442376 | tf_op jit(solution)/shard_map/ppermute | solution.py:374
  19.2 5.5 %collective-permute-done.xlow = f32[3,48,256]{2,1,0:T(8,128)S(1)} collective-permute-done((f32[3,48,256]{2,1,0:T(8,128)S(1)}, f32[3,48,256]{2,1,0:T(8,128)S(1)}, u32[]{:S(2)}, u32[]{:S(2)}) %collective-permute-start) | collective-permute-done | bytes 147488 | tf_op jit(solution)/shard_map/ppermute | solution.py:373
  24.7 2.1 %collective-permute-done.1.xhigh = f32[3,48,256]{2,1,0:T(8,128)S(1)} collective-permute-done((f32[3,48,256]{2,1,0:T(8,128)S(1)}, f32[3,48,256]{2,1,0:T(8,128)S(1)}, u32[]{:S(2)}, u32[]{:S(2)}) %collective-permute-start.1) | collective-permute-done | bytes 147488 | tf_op jit(solution)/shard_map/ppermute | solution.py:374
  26.9 0.0 all-to-all-done.got
  26.9 1.9 %near.1 = (f32[8,48,256]{2,1,0:T(8,128)}, f32[16,48,128]{2,1,0:T(8,128)S(1)}) custom-call(f32[3,8,48,256]{3,2,1,0:T(8,128)S(1)} %get-tuple-element.18.near, f32[16,56,128]{2,1,0:T(8,128)S(1)} %all-to-all-done.got, f32[3,48,256]{2,1,0:T(8,128)S(1)} %collective-permute-done.xlow, f32[3,48,256]{2,1,0:T(8,128)S(1)} %collective-permute-done.1.xhigh), custom_call_target="tpu_custom_call" | custom-call | bytes 6000000 | tf_op jit(solution)/shard_map/near/pallas_call | solution.py:385
  28.8 14.2 %all_to_all.10.sums = f32[16,48,128]{2,1,0:T(8,128)S(1)} all-to-all(f32[16,48,128]{2,1,0:T(8,128)S(1)} %get-tuple-element.27), channel_id=1, replica_groups=mesh['px'=48,'py'=4,'dz'=4] {'py','dz'}, dimensions={0} | all-to-all | bytes 786432 | tf_op jit(solution)/shard_map/all_to_all | solution.py:394
  42.9 2.0 %edge.1 = (f32[4,48,128]{2,1,0:T(8,128)S(1)}, f32[8,256]{1,0:T(8,128)S(1)}, f32[8,256]{1,0:T(8,128)S(1)}) custom-call(f32[16,56,128]{2,1,0:T(8,128)S(1)} %all-to-all-done.got, f32[16,48,128]{2,1,0:T(8,128)S(1)} %all_to_all.10.sums, f32[64,256]{1,0:T(8,128)S(1)} %get-tuple-element.21.depth, f32[2,64,256]{2,1,0:T(8,128)S(1)} %get-tuple-element.22.flows, ...), custom_call_target="tpu_custom_call" | custom-call | bytes 6000000 | tf_op jit(solution)/shard_map/edge/pallas_call | solution.py:395
  44.9 4.3 %collective-permute-start.2 = (f32[8,256]{1,0:T(8,128)S(1)}, f32[8,256]{1,0:T(8,128)S(1)}, u32[]{:S(2)}, u32[]{:S(2)}) collective-permute-start(f32[8,256]{1,0:T(8,128)S(1)} %get-tuple-element.32), channel_id=1, source_target_pairs={{0,16},{16,32},{32,48},{48,64},{64,80},{80,96},{96,112},{112,128},... | collective-permute-start | bytes 24584 | tf_op jit(solution)/shard_map/ppermute | solution.py:408
  49.2 5.8 %collective-permute-start.3 = (f32[8,256]{1,0:T(8,128)S(1)}, f32[8,256]{1,0:T(8,128)S(1)}, u32[]{:S(2)}, u32[]{:S(2)}) collective-permute-start(f32[8,256]{1,0:T(8,128)S(1)} %get-tuple-element.33), channel_id=1, source_target_pairs={{16,0},{32,16},{48,32},{64,48},{80,64},{96,80},{112,96},{128,112},... | collective-permute-start | bytes 24584 | tf_op jit(solution)/shard_map/ppermute | solution.py:409
  55.0 5.3 %far.1 = (f32[3,64,256]{2,1,0:T(8,128)}, f32[3,8,256]{2,1,0:T(8,128)S(1)}, f32[3,8,256]{2,1,0:T(8,128)S(1)}) custom-call(f32[16,56,128]{2,1,0:T(8,128)S(1)} %all-to-all-done.got, f32[4,48,128]{2,1,0:T(8,128)S(1)} %get-tuple-element.28.total, f32[64,256]{1,0:T(8,128)S(1)} %get-tuple-element.21.depth, f32[2,64,256]{2,1,0:T(8,128)S(1)} %get-tuple-element.22.flows, ...), custom_call_target="tpu_custom_call" | custom-call | bytes 15000000 | tf_op jit(solution)/shard_map/far/pallas_call | solution.py:410
  60.2 0.0 collective-permute-done.2.above
  60.3 0.0 collective-permute-done.3.below
  60.3 0.7 %join.1 = f32[3,64,256]{2,1,0:T(8,128)} custom-call(f32[3,64,256]{2,1,0:T(8,128)} %get-tuple-element.29.part, f32[3,8,256]{2,1,0:T(8,128)S(1)} %get-tuple-element.30.head, f32[3,8,256]{2,1,0:T(8,128)S(1)} %get-tuple-element.31.tail, f32[8,256]{1,0:T(8,128)S(1)} %collective-permute-done.2.above, ...), custom_call_target="tpu_custom_call", output_to_operand_aliasing={{}: (0, {})} | custom-call | bytes 3000000 | tf_op jit(solution)/shard_map/join/pallas_call | solution.py:424
Async XLA Ops:
  3.4 23.4 %all-to-all-start = ((f32[16,56,128]{2,1,0:T(8,128)}), f32[16,56,128]{2,1,0:T(8,128)S(1)}, u32[]{:S(2)}, u32[]{:S(2)}) async-start(f32[16,56,128]{2,1,0:T(8,128)} %pack.1), calls=%async_computation | async-start | bytes 917504 | tf_op jit(solution)/shard_map/all_to_all | solution.py:384
  9.2 15.6 %collective-permute-start = (f32[3,48,256]{2,1,0:T(8,128)S(1)}, f32[3,48,256]{2,1,0:T(8,128)S(1)}, u32[]{:S(2)}, u32[]{:S(2)}) collective-permute-start(f32[3,48,256]{2,1,0:T(8,128)S(1)} %get-tuple-element.24), channel_id=1, source_target_pairs={{0,16},{16,32},{32,48},{48,64},{64,80},{80,96},{96,112},{112,128},... | collective-permute-start | bytes 442376 | tf_op jit(solution)/shard_map/ppermute | solution.py:373
  13.7 13.2 %collective-permute-start.1 = (f32[3,48,256]{2,1,0:T(8,128)S(1)}, f32[3,48,256]{2,1,0:T(8,128)S(1)}, u32[]{:S(2)}, u32[]{:S(2)}) collective-permute-start(f32[3,48,256]{2,1,0:T(8,128)S(1)} %get-tuple-element.25), channel_id=1, source_target_pairs={{16,0},{32,16},{48,32},{64,48},{80,64},{96,80},{112,96},{128,112},... | collective-permute-start | bytes 442376 | tf_op jit(solution)/shard_map/ppermute | solution.py:374
  44.9 15.4 %collective-permute-start.2 = (f32[8,256]{1,0:T(8,128)S(1)}, f32[8,256]{1,0:T(8,128)S(1)}, u32[]{:S(2)}, u32[]{:S(2)}) collective-permute-start(f32[8,256]{1,0:T(8,128)S(1)} %get-tuple-element.32), channel_id=1, source_target_pairs={{0,16},{16,32},{32,48},{48,64},{64,80},{80,96},{96,112},{112,128},... | collective-permute-start | bytes 24584 | tf_op jit(solution)/shard_map/ppermute | solution.py:408
  49.2 11.1 %collective-permute-start.3 = (f32[8,256]{1,0:T(8,128)S(1)}, f32[8,256]{1,0:T(8,128)S(1)}, u32[]{:S(2)}, u32[]{:S(2)}) collective-permute-start(f32[8,256]{1,0:T(8,128)S(1)} %get-tuple-element.33), channel_id=1, source_target_pairs={{16,0},{32,16},{48,32},{64,48},{80,64},{96,80},{112,96},{128,112},... | collective-permute-start | bytes 24584 | tf_op jit(solution)/shard_map/ppermute | solution.py:409

commit v3 on v2

--- a/solution.py
+++ b/solution.py
@@ -25,7 +25,6 @@
 FY = 256
 ROWS = CX * 3 * 2
 BLK = ROWS + 8
-NROW = FY + 16
 
 f32 = jnp.float32
 GROUP = ("py", "dz")
@@ -189,54 +188,59 @@
 
 
 def cell_rows(rows):
-    r = lax.broadcasted_iota(jnp.int32, (rows, 128), 0)
-    r = jnp.where(r > FY, FY - r, r)
-    return r.astype(f32).astype(jnp.bfloat16)
+    return lax.broadcasted_iota(jnp.int32, (rows, 128), 0).astype(f32).astype(jnp.bfloat16)
 
 
 OVER = (((1,), (1,)), ((), ()))
 
 
-def split(row, rows):
-    tile = jnp.broadcast_to(row, (16, 128))
-    high = tile.astype(jnp.bfloat16)
-    low = (tile - high.astype(f32)).astype(jnp.bfloat16)
-    return [jnp.concatenate([t] * (rows // 16), axis=0) for t in (high, low)]
-
-
-def edge_kernel(scale, got, sums, depth, flows, mask, total, top, bottom, bits, lhs):
+def spread(parts, wide):
+    for m, part in enumerate(parts):
+        wide[m * 8 : m * 8 + 8] = part
+
+
+def gathered(wide, p):
+    return wide[pl.ds(p, 16, stride=8), :].astype(jnp.bfloat16)
+
+
+def pairs(build):
+    for p in range(0, 8, 2):
+        yield [jnp.concatenate(two, axis=1) for two in zip(build(p), build(p + 1))]
+
+
+def edge_kernel(scale, got, sums, depth, flows, mask, pieces, top, bottom, wide):
     me = lax.axis_index("py") * NDZ + lax.axis_index("dz")
-    row = lax.broadcasted_iota(jnp.int32, (16, 128), 0)
-    part = row & 7
-    field = jnp.where(part >= 3, part - 3, part)
-    edge = jnp.where(part >= 3, FX - 1, 0)
-    edge = jnp.where(part >= 6, -1, edge)
-    edge = edge.astype(f32)
-    low = row >= 8
     ycell = cell_rows(FY)
     one = jnp.ones((FY, 128), jnp.bfloat16)
+    zero = jnp.zeros((8, 128), f32)
     acc = jnp.zeros((16, FY), f32)
     for a in range(NPY):
         t = sums[a * NDZ]
         for b in range(1, NDZ):
             t = t + sums[a * NDZ + b]
         t = t * scale
-        total[a] = t
+        high = t.astype(jnp.bfloat16).astype(f32)
+        low = t - high
+        pieces[0, a] = high
+        pieces[1, a] = low
         for h in range(2):
+            g = a * 2 + h
             y, x = decode(got, me, a, h)
-            for p in range(8):
-                at = slice(p * 128, (p + 1) * 128)
-                bits[:, at] = jnp.where(ycell == tall(y[p : p + 1], FY), one, one * 0)
-                value = None
-                for f in range(3):
-                    r = (f * 2 + h) * 8 + p
-                    whole = jnp.broadcast_to(t[r : r + 1], (16, 128))
-                    high = whole.astype(jnp.bfloat16).astype(f32)
-                    both = jnp.where(low, whole - high, high)
-                    value = both if f == 0 else jnp.where(field == f, both, value)
-                value = jnp.where(edge == x[p : p + 1], value, 0.0)
-                lhs[:, at] = value.astype(jnp.bfloat16)
-            acc = acc + lax.dot_general(lhs[...], bits[...], OVER, preferred_element_type=f32)
+            rows = []
+            for part in (high, low):
+                for cell in (0, FX - 1):
+                    for f in range(3):
+                        r = (f * 2 + h) * 8
+                        rows.append(jnp.where(x == cell, part[r : r + 8], 0.0))
+                rows += [zero, zero]
+            spread(rows, wide.at[g])
+
+            def build(p):
+                bits = jnp.where(ycell == tall(y[p : p + 1], FY), one, one * 0)
+                return gathered(wide.at[g], p), bits
+
+            for lhs, bits in pairs(build):
+                acc = acc + lax.dot_general(lhs, bits, OVER, preferred_element_type=f32)
     acc = acc[0:8] + acc[8:16]
     blank = jnp.zeros((5, FY), f32)
     for e, out in ((0, top), (1, bottom)):
@@ -266,47 +270,67 @@
     ]
 
 
-def far_kernel(got, total, depth, flows, mask, out, head, tail, bits, ah, al):
+def far_kernel(
+    got, pieces, depth, flows, mask, out, head, tail, wide
+):
     me = lax.axis_index("py") * NDZ + lax.axis_index("dz")
-    xcell = lax.broadcasted_iota(jnp.int32, (FX, 128), 0).astype(f32).astype(jnp.bfloat16)
-    ycell = cell_rows(NROW)
-    one = jnp.ones((NROW, 128), jnp.bfloat16)
-    zero = jnp.zeros((FX, 128), jnp.bfloat16)
-    acc = jnp.zeros((NROW, 3 * FX), f32)
+    xcell = cell_rows(FX)
+    ycell = cell_rows(FY)
+    one = jnp.ones((FY, 128), jnp.bfloat16)
+    none = jnp.zeros((FX, 128), jnp.bfloat16)
+    zero = jnp.zeros((8, 128), f32)
+    acc = jnp.zeros((6 * FX, FY), f32)
+    side = jnp.zeros((16, FX), f32)
     for a in range(NPY):
         for h in range(2):
+            g = a * 2 + h
             y, x = decode(got, me, a, h)
-            for p in range(8):
-                at = slice(p * 128, (p + 1) * 128)
-                bits[:, at] = jnp.where(ycell == tall(y[p : p + 1], NROW), one, one * 0)
+            rows = []
+            for n in range(2):
+                for cell in (-1, FY):
+                    for f in range(3):
+                        r = (f * 2 + h) * 8
+                        rows.append(jnp.where(y == cell, pieces[n, a, r : r + 8], 0.0))
+                rows += [zero, zero]
+            spread(rows, wide.at[g])
+
+            def build(p):
+                bits = jnp.where(ycell == tall(y[p : p + 1], FY), one, one * 0)
                 here = xcell == tall(x[p : p + 1], FX)
-                for f in range(3):
-                    r = (f * 2 + h) * 8 + p
-                    high, low = split(total[a, r : r + 1], FX)
-                    cells = slice(f * FX, (f + 1) * FX)
-                    ah[cells, at] = jnp.where(here, high, zero)
-                    al[cells, at] = jnp.where(here, low, zero)
-            for part in (ah, al):
-                acc = acc + lax.dot_general(bits[...], part[...], OVER, preferred_element_type=f32)
-    source = acc.T
+                parts = []
+                for n in range(2):
+                    for f in range(3):
+                        r = (f * 2 + h) * 8 + p
+                        value = tall(pieces[n, a, r : r + 1], FX)
+                        parts.append(jnp.where(here, value, none))
+                xbits = jnp.where(here, one[0:FX], none)
+                return jnp.concatenate(parts, axis=0), bits, gathered(wide.at[g], p), xbits
+
+            for lhs, bits, side_lhs, xbits in pairs(build):
+                acc = acc + lax.dot_general(lhs, bits, OVER, preferred_element_type=f32)
+                side = side + lax.dot_general(side_lhs, xbits, OVER, preferred_element_type=f32)
+    source = acc[0 : 3 * FX] + acc[3 * FX :]
+    side = side[0:8] + side[8:16]
+    side = jnp.concatenate([side] * 16, axis=0)
+    side = jnp.concatenate([side, side], axis=1).T
     wet = mask[...].astype(f32)
     raw = (depth[...], flows[0], flows[1])
     cells = []
     for f in range(3):
-        s = raw[f] + source[f * FX : (f + 1) * FX, 0:FY]
+        s = raw[f] + source[f * FX : (f + 1) * FX]
         cells.append(s if f == 0 else s * wet)
     body = terms(*cells, True)
     sides = []
-    for side in range(2):
-        other = jnp.maximum(me - 1, 0) if side == 0 else jnp.minimum(me + 1, GRP - 1)
+    for n in range(2):
+        other = jnp.maximum(me - 1, 0) if n == 0 else jnp.minimum(me + 1, GRP - 1)
         block = got[other, ROWS:BLK]
         block = jnp.where((other % 2) == 1, block, pltpu.roll(block, 64, 1))
         e = jnp.concatenate([block] * 16, axis=0).T[0:FX]
-        inside = (me > 0) if side == 0 else (me < GRP - 1)
-        col = FY + 1 if side == 0 else FY
+        inside = (me > 0) if n == 0 else (me < GRP - 1)
         s = []
         for f in range(3):
-            v = e[:, f : f + 1] + source[f * FX : (f + 1) * FX, col : col + 1]
+            col = n * 3 + f
+            v = e[:, f : f + 1] + side[0:FX, col : col + 1]
             v = v if f == 0 else v * e[:, 3:4]
             s.append(jnp.where(inside, v, 0.0))
         sides.append(terms(*s, inside))
@@ -392,15 +416,12 @@
         name="near",
     )(near_state, got, xlow, xhigh)
     sums = lax.all_to_all(sums, GROUP, split_axis=0, concat_axis=0, tiled=True)
-    total, top, bottom = pl.pallas_call(
+    pieces, top, bottom = pl.pallas_call(
         functools.partial(edge_kernel, column_height / (CZ * NDZ)),
-        out_shape=(vmem(NPY, ROWS, 128), vmem(8, FY), vmem(8, FY)),
+        out_shape=(vmem(2, NPY, ROWS, 128), vmem(8, FY), vmem(8, FY)),
         in_specs=[VM] * 5,
         out_specs=(VM,) * 3,
-        scratch_shapes=[
-            pltpu.VMEM((FY, 1024), jnp.bfloat16),
-            pltpu.VMEM((16, 1024), jnp.bfloat16),
-        ],
+        scratch_shapes=[vmem(8, 128, 128)],
         compiler_params=PARAMS,
         cost_estimate=cost(2),
         name="edge",
@@ -412,15 +433,11 @@
         out_shape=(shape(3, FX, FY), vmem(3, 8, FY), vmem(3, 8, FY)),
         in_specs=[VM] * 5,
         out_specs=(VM,) * 3,
-        scratch_shapes=[
-            pltpu.VMEM((NROW, 1024), jnp.bfloat16),
-            pltpu.VMEM((3 * FX, 1024), jnp.bfloat16),
-            pltpu.VMEM((3 * FX, 1024), jnp.bfloat16),
-        ],
-        compiler_params=PARAMS,
+        scratch_shapes=[vmem(8, 128, 128)],
+        compiler_params=pltpu.CompilerParams(vmem_limit_bytes=20 << 20),
         cost_estimate=cost(5),
         name="far",
-    )(got, total, far_depth, far_flows, wet_mask)
+    )(got, pieces, far_depth, far_flows, wet_mask)
     far_new = pl.pallas_call(
         join_kernel,
         out_shape=shape(3, FX, FY),

time: 61.3 us -> 59.9 us (0.977)
  the two profiles are of different devices: /device:TPU:256 before, /device:TPU:248 now
where the time goes in v3:
time: 59.9 us; the launch traced here: 59.5 us
  starting transfers between devices  20.4 us (34%)
  waiting for transfers between devices  14.3 us (24%)
  blocking collectives  14 us (23%)
  Pallas kernels  10.2 us (17%)
  between operations  0.68 us (1%)
    all_to_all x1, blocking collectives, local(): sums = lax.all_to_all(sums, GROUP, split_axis=0, concat_axis=0, tiled=True)  14 us
    ppermute x1, waiting for transfers between devices, local(): xhigh = lax.ppermute(xlo, 'px', back)  8.43 us
    all_to_all x1, starting transfers between devices, local(): got = lax.all_to_all(send, GROUP, split_axis=0, concat_axis=0, tiled=True)  5.99 us
    ppermute x1, starting transfers between devices, local(): xlow = lax.ppermute(xhi, 'px', forth)  5.7 us
    ppermute x1, starting transfers between devices, local(): below = lax.ppermute(top, 'px', back)  3.8 us
    pallas_call x1, Pallas kernels, local(): pl.pallas_call(far_kernel, out_shape=(shape(3, FX, FY), vmem(3, 8, FY), v...  3.54 us
    ppermute x1, waiting for transfers between devices, local(): xlow = lax.ppermute(xhi, 'px', forth)  3.43 us
    ppermute x1, starting transfers between devices, local(): above = lax.ppermute(bottom, 'px', forth)  2.94 us
  transfers between devices with their start and end apart: 5, of which 3 were waited for; matrix products, arithmetic and copies ran while one was open for 0% of the time, Pallas kernels for 6%

profile of v3, /device:TPU:248, one launch (start us, length us, event | category | flops | bytes accessed | tf_op | source)
XLA Modules:
  0.0 59.5 jit_solution(1145103052596130332)
XLA Ops:
  0.6 1.5 %load.1 = (f32[3,8,48,256]{3,2,1,0:T(8,128)S(1)}, s32[4,128]{1,0:T(4,128)S(1)}, s32[4,128]{1,0:T(4,128)S(1)}, f32[64,256]{1,0:T(8,128)S(1)}, f32[2,64,256]{2,1,0...) custom-call(f32[3,8,48,256]{3,2,1,0:T(8,128)} %refs_0_.1, ...), custom_call_target="tpu_custom_call" | custom-call | bytes 3000000 | tf_op jit(solution)/shard_map/load/pallas_call | solution.py:385
  2.2 1.3 %pack.1 = f32[16,56,128]{2,1,0:T(8,128)} custom-call(f32[3,8,48,256]{3,2,1,0:T(8,128)S(1)} %get-tuple-element.18.near, s32[4,128]{1,0:T(4,128)S(1)} %get-tuple-element.19.owner, s32[4,128]{1,0:T(4,128)S(1)} %get-tuple-element.20.land, f32[64,256]{1,0:T(8,128)S(1)} %get-tuple-element.21.depth, f32[2,64,256]{2,1,0:T(8,128)S(1)} %get-tuple-element.22.flows, ...), custom_call_target="tpu_custom_call" | custom-call | bytes 6000000 | tf_op jit(solution)/shard_map/pack/pallas_call | solution.py:399
  3.5 6.0 %all-to-all-start = ((f32[16,56,128]{2,1,0:T(8,128)}), f32[16,56,128]{2,1,0:T(8,128)S(1)}, u32[]{:S(2)}, u32[]{:S(2)}) async-start(f32[16,56,128]{2,1,0:T(8,128)} %pack.1), calls=%async_computation | async-start | bytes 917504 | tf_op jit(solution)/shard_map/all_to_all | solution.py:408
  9.5 5.7 %collective-permute-start = (f32[3,48,256]{2,1,0:T(8,128)S(1)}, f32[3,48,256]{2,1,0:T(8,128)S(1)}, u32[]{:S(2)}, u32[]{:S(2)}) collective-permute-start(f32[3,48,256]{2,1,0:T(8,128)S(1)} %get-tuple-element.24), channel_id=1, source_target_pairs={{0,16},{16,32},{32,48},{48,64},{64,80},{80,96},{96,112},{112,128},... | collective-permute-start | bytes 442376 | tf_op jit(solution)/shard_map/ppermute | solution.py:397
  15.2 1.9 %collective-permute-start.1 = (f32[3,48,256]{2,1,0:T(8,128)S(1)}, f32[3,48,256]{2,1,0:T(8,128)S(1)}, u32[]{:S(2)}, u32[]{:S(2)}) collective-permute-start(f32[3,48,256]{2,1,0:T(8,128)S(1)} %get-tuple-element.25), channel_id=1, source_target_pairs={{16,0},{32,16},{48,32},{64,48},{80,64},{96,80},{112,96},{128,112},... | collective-permute-start | bytes 442376 | tf_op jit(solution)/shard_map/ppermute | solution.py:398
  17.1 3.4 %collective-permute-done.xlow = f32[3,48,256]{2,1,0:T(8,128)S(1)} collective-permute-done((f32[3,48,256]{2,1,0:T(8,128)S(1)}, f32[3,48,256]{2,1,0:T(8,128)S(1)}, u32[]{:S(2)}, u32[]{:S(2)}) %collective-permute-start) | collective-permute-done | bytes 147488 | tf_op jit(solution)/shard_map/ppermute | solution.py:397
  20.6 8.4 %collective-permute-done.1.xhigh = f32[3,48,256]{2,1,0:T(8,128)S(1)} collective-permute-done((f32[3,48,256]{2,1,0:T(8,128)S(1)}, f32[3,48,256]{2,1,0:T(8,128)S(1)}, u32[]{:S(2)}, u32[]{:S(2)}) %collective-permute-start.1) | collective-permute-done | bytes 147488 | tf_op jit(solution)/shard_map/ppermute | solution.py:398
  29.0 0.0 all-to-all-done.got
  29.0 1.9 %near.1 = (f32[8,48,256]{2,1,0:T(8,128)}, f32[16,48,128]{2,1,0:T(8,128)S(1)}) custom-call(f32[3,8,48,256]{3,2,1,0:T(8,128)S(1)} %get-tuple-element.18.near, f32[16,56,128]{2,1,0:T(8,128)S(1)} %all-to-all-done.got, f32[3,48,256]{2,1,0:T(8,128)S(1)} %collective-permute-done.xlow, f32[3,48,256]{2,1,0:T(8,128)S(1)} %collective-permute-done.1.xhigh), custom_call_target="tpu_custom_call" | custom-call | bytes 6000000 | tf_op jit(solution)/shard_map/near/pallas_call | solution.py:409
  30.9 14.0 %all_to_all.10.sums = f32[16,48,128]{2,1,0:T(8,128)S(1)} all-to-all(f32[16,48,128]{2,1,0:T(8,128)S(1)} %get-tuple-element.27), channel_id=1, replica_groups=mesh['px'=48,'py'=4,'dz'=4] {'py','dz'}, dimensions={0} | all-to-all | bytes 786432 | tf_op jit(solution)/shard_map/all_to_all | solution.py:418
  44.9 1.2 %edge.1 = (f32[2,4,48,128]{3,2,1,0:T(8,128)S(1)}, f32[8,256]{1,0:T(8,128)S(1)}, f32[8,256]{1,0:T(8,128)S(1)}) custom-call(f32[16,56,128]{2,1,0:T(8,128)S(1)} %all-to-all-done.got, f32[16,48,128]{2,1,0:T(8,128)S(1)} %all_to_all.10.sums, f32[64,256]{1,0:T(8,128)S(1)} %get-tuple-element.21.depth, f32[2,64,256]{2,1,0:T(8,128)S(1)} %get-tuple-element.22.flows, ...), custom_call_target="tpu_custom_call" | custom-call | bytes 6000000 | tf_op jit(solution)/shard_map/edge/pallas_call | solution.py:419
  46.2 2.9 %collective-permute-start.2 = (f32[8,256]{1,0:T(8,128)S(1)}, f32[8,256]{1,0:T(8,128)S(1)}, u32[]{:S(2)}, u32[]{:S(2)}) collective-permute-start(f32[8,256]{1,0:T(8,128)S(1)} %get-tuple-element.32), channel_id=1, source_target_pairs={{0,16},{16,32},{32,48},{48,64},{64,80},{80,96},{96,112},{112,128},... | collective-permute-start | bytes 24584 | tf_op jit(solution)/shard_map/ppermute | solution.py:429
  49.1 3.8 %collective-permute-start.3 = (f32[8,256]{1,0:T(8,128)S(1)}, f32[8,256]{1,0:T(8,128)S(1)}, u32[]{:S(2)}, u32[]{:S(2)}) collective-permute-start(f32[8,256]{1,0:T(8,128)S(1)} %get-tuple-element.33), channel_id=1, source_target_pairs={{16,0},{32,16},{48,32},{64,48},{80,64},{96,80},{112,96},{128,112},... | collective-permute-start | bytes 24584 | tf_op jit(solution)/shard_map/ppermute | solution.py:430
  52.9 3.5 %far.1 = (f32[3,64,256]{2,1,0:T(8,128)}, f32[3,8,256]{2,1,0:T(8,128)S(1)}, f32[3,8,256]{2,1,0:T(8,128)S(1)}) custom-call(f32[16,56,128]{2,1,0:T(8,128)S(1)} %all-to-all-done.got, f32[2,4,48,128]{3,2,1,0:T(8,128)S(1)} %get-tuple-element.28.pieces, f32[64,256]{1,0:T(8,128)S(1)} %get-tuple-element.21.depth, f32[2,64,256]{2,1,0:T(8,128)S(1)} %get-tuple-element.22.flows, ...), custom_call_target="tpu_custom_call" | custom-call | bytes 15000000 | tf_op jit(solution)/shard_map/far/pallas_call | solution.py:431
  56.5 0.0 collective-permute-done.2.above
  56.5 2.4 %collective-permute-done.3.below = f32[8,256]{1,0:T(8,128)S(1)} collective-permute-done((f32[8,256]{1,0:T(8,128)S(1)}, f32[8,256]{1,0:T(8,128)S(1)}, u32[]{:S(2)}, u32[]{:S(2)}) %collective-permute-start.3) | collective-permute-done | bytes 8224 | tf_op jit(solution)/shard_map/ppermute | solution.py:430
  58.9 0.7 %join.1 = f32[3,64,256]{2,1,0:T(8,128)} custom-call(f32[3,64,256]{2,1,0:T(8,128)} %get-tuple-element.29.part, f32[3,8,256]{2,1,0:T(8,128)S(1)} %get-tuple-element.30.head, f32[3,8,256]{2,1,0:T(8,128)S(1)} %get-tuple-element.31.tail, f32[8,256]{1,0:T(8,128)S(1)} %collective-permute-done.2.above, ...), custom_call_target="tpu_custom_call", output_to_operand_aliasing={{}: (0, {})} | custom-call | bytes 3000000 | tf_op jit(solution)/shard_map/join/pallas_call | solution.py:441
Async XLA Ops:
  3.5 25.5 %all-to-all-start = ((f32[16,56,128]{2,1,0:T(8,128)}), f32[16,56,128]{2,1,0:T(8,128)S(1)}, u32[]{:S(2)}, u32[]{:S(2)}) async-start(f32[16,56,128]{2,1,0:T(8,128)} %pack.1), calls=%async_computation | async-start | bytes 917504 | tf_op jit(solution)/shard_map/all_to_all | solution.py:408
  9.5 11.1 %collective-permute-start = (f32[3,48,256]{2,1,0:T(8,128)S(1)}, f32[3,48,256]{2,1,0:T(8,128)S(1)}, u32[]{:S(2)}, u32[]{:S(2)}) collective-permute-start(f32[3,48,256]{2,1,0:T(8,128)S(1)} %get-tuple-element.24), channel_id=1, source_target_pairs={{0,16},{16,32},{32,48},{48,64},{64,80},{80,96},{96,112},{112,128},... | collective-permute-start | bytes 442376 | tf_op jit(solution)/shard_map/ppermute | solution.py:397
  15.2 13.8 %collective-permute-start.1 = (f32[3,48,256]{2,1,0:T(8,128)S(1)}, f32[3,48,256]{2,1,0:T(8,128)S(1)}, u32[]{:S(2)}, u32[]{:S(2)}) collective-permute-start(f32[3,48,256]{2,1,0:T(8,128)S(1)} %get-tuple-element.25), channel_id=1, source_target_pairs={{16,0},{32,16},{48,32},{64,48},{80,64},{96,80},{112,96},{128,112},... | collective-permute-start | bytes 442376 | tf_op jit(solution)/shard_map/ppermute | solution.py:398
  46.2 10.3 %collective-permute-start.2 = (f32[8,256]{1,0:T(8,128)S(1)}, f32[8,256]{1,0:T(8,128)S(1)}, u32[]{:S(2)}, u32[]{:S(2)}) collective-permute-start(f32[8,256]{1,0:T(8,128)S(1)} %get-tuple-element.32), channel_id=1, source_target_pairs={{0,16},{16,32},{32,48},{48,64},{64,80},{80,96},{96,112},{112,128},... | collective-permute-start | bytes 24584 | tf_op jit(solution)/shard_map/ppermute | solution.py:429
  49.1 9.8 %collective-permute-start.3 = (f32[8,256]{1,0:T(8,128)S(1)}, f32[8,256]{1,0:T(8,128)S(1)}, u32[]{:S(2)}, u32[]{:S(2)}) collective-permute-start(f32[8,256]{1,0:T(8,128)S(1)} %get-tuple-element.33), channel_id=1, source_target_pairs={{16,0},{32,16},{48,32},{64,48},{80,64},{96,80},{112,96},{128,112},... | collective-permute-start | bytes 24584 | tf_op jit(solution)/shard_map/ppermute | solution.py:430

commit v4 on v3

--- a/solution.py
+++ b/solution.py
@@ -24,7 +24,8 @@
 FX = 64
 FY = 256
 ROWS = CX * 3 * 2
-BLK = ROWS + 8
+SIDE = CZ // 3
+BLK = SIDE + 8
 
 f32 = jnp.float32
 GROUP = ("py", "dz")
@@ -52,7 +53,7 @@
         move.wait()
 
 
-def pack_kernel(near, owner, land, depth, flows, mask, out):
+def pack_kernel(near, owner, land, depth, flows, mask, out, zlo, zhi):
     py = lax.axis_index("py")
     dz = lax.axis_index("dz")
     me = py * NDZ + dz
@@ -63,10 +64,10 @@
     lanes = lane_iota((8, 128))
     mine = jnp.where(odd, lanes, 127 - lanes) >= 64
     codes = jnp.where(mine, codes, 0.0)
-    zero = jnp.zeros((ROWS, 128), f32)
+    zero = jnp.zeros((SIDE, 128), f32)
     for b in range(GRP):
-        out[b, 0:ROWS] = zero
-        out[b, ROWS:BLK] = codes
+        out[b, 0:SIDE] = zero
+        out[b, SIDE:BLK] = codes
 
     def edge(col):
         k = lane_iota((FX, 128))
@@ -78,18 +79,15 @@
 
     @pl.when(me > 0)
     def _():
-        out[me - 1, ROWS:BLK] = edge(0)
+        out[me - 1, SIDE:BLK] = edge(0)
 
     @pl.when(me < GRP - 1)
     def _():
-        out[me + 1, ROWS:BLK] = edge(FY - 1)
-
-    def zface(dst, z):
-        for f in range(3):
-            face = near[f, :, z, :]
-            for h in range(2):
-                r = (f * 2 + h) * 8
-                out[dst, r : r + 8] = face[:, h * 128 : (h + 1) * 128]
+        out[me + 1, SIDE:BLK] = edge(FY - 1)
+
+    for f in range(3):
+        zlo[f] = near[f, :, 0, :]
+        zhi[f] = near[f, :, CZ - 1, :]
 
     def yface(dst, y):
         k = lane_iota((CZ, 128))
@@ -97,15 +95,8 @@
         for f in range(3):
             for x in range(CX):
                 m = jnp.where(k == f * CX + x, near[f, x, :, y : y + 1], m)
-        out[dst, 0:ROWS] = m
-
-    @pl.when(dz > 0)
-    def _():
-        zface(me - 1, 0)
-
-    @pl.when(dz < NDZ - 1)
-    def _():
-        zface(me + 1, CZ - 1)
+        layers = [pltpu.roll(m[SIDE * n : SIDE * (n + 1)], 32 * n, 1) for n in range(3)]
+        out[dst, 0:SIDE] = layers[0] + layers[1] + layers[2]
 
     @pl.when(py > 0)
     def _():
@@ -116,25 +107,18 @@
         yface(me + NDZ, CY - 1)
 
 
-def near_kernel(near, got, xlow, xhigh, frac, sums):
+def near_kernel(near, got, xlow, xhigh, down, up, frac, sums):
     py = lax.axis_index("py")
-    dz = lax.axis_index("dz")
-    me = py * NDZ + dz
-    at_l = jnp.maximum(me - NDZ, 0)
-    at_r = jnp.minimum(me + NDZ, GRP - 1)
-    at_d = jnp.maximum(me - 1, 0)
-    at_u = jnp.minimum(me + 1, GRP - 1)
-    left = jnp.where(py > 0, got[at_l, 0:ROWS], 0.0)
-    right = jnp.where(py < NPY - 1, got[at_r, 0:ROWS], 0.0)
-    down = jnp.where(dz > 0, got[at_d, 0:ROWS], 0.0)
-    up = jnp.where(dz < NDZ - 1, got[at_u, 0:ROWS], 0.0)
+    me = py * NDZ + lax.axis_index("dz")
+
+    def yface(at, inside):
+        m = jnp.where(inside, got[at, 0:SIDE], 0.0)
+        return jnp.concatenate([m] + [pltpu.roll(m, 128 - 32 * n, 1) for n in (1, 2)], axis=0)
+
+    left = yface(jnp.maximum(me - NDZ, 0), py > 0)
+    right = yface(jnp.minimum(me + NDZ, GRP - 1), py < NPY - 1)
     lane = lane_iota((CZ, CY))
     row = lax.broadcasted_iota(jnp.int32, (CZ, CY), 0)
-
-    def face_row(face, f, x):
-        return jnp.concatenate(
-            [face[(f * 2 + h) * 8 + x : (f * 2 + h) * 8 + x + 1] for h in range(2)], axis=1
-        )
 
     for p in range(CX):
         x = x_order(p)
@@ -148,8 +132,8 @@
             xm = near[f, x - 1] if x > 0 else xlow[f]
             yp = jnp.where(lane == CY - 1, right[:, k : k + 1], pltpu.roll(q, CY - 1, 1))
             ym = jnp.where(lane == 0, left[:, k : k + 1], pltpu.roll(q, 1, 1))
-            zp = jnp.where(row == CZ - 1, face_row(up, f, x), pltpu.roll(q, CZ - 1, 0))
-            zm = jnp.where(row == 0, face_row(down, f, x), pltpu.roll(q, 1, 0))
+            zp = jnp.where(row == CZ - 1, up[f, x : x + 1], pltpu.roll(q, CZ - 1, 0))
+            zm = jnp.where(row == 0, down[f, x : x + 1], pltpu.roll(q, 1, 0))
             dx = xp - xm
             dy = yp - ym
             lap = xp + xm + yp + ym + zp + zm - 6.0 * q
@@ -176,7 +160,7 @@
 def decode(got, me, a, h):
     d = a * NDZ + 2 * h
     lanes = lane_iota((8, 128))
-    code = jnp.where(lanes < 64, got[d, ROWS:BLK], got[d + 1, ROWS:BLK]).astype(jnp.int32)
+    code = jnp.where(lanes < 64, got[d, SIDE:BLK], got[d + 1, SIDE:BLK]).astype(jnp.int32)
     y = (code >> 14) * FY + (code & (FY - 1)) - me * FY
     y = jnp.where((y < -1) | (y > FY), -128, y)
     return y.astype(f32), ((code >> 8) & (FX - 1)).astype(f32)
@@ -323,7 +307,7 @@
     sides = []
     for n in range(2):
         other = jnp.maximum(me - 1, 0) if n == 0 else jnp.minimum(me + 1, GRP - 1)
-        block = got[other, ROWS:BLK]
+        block = got[other, SIDE:BLK]
         block = jnp.where((other % 2) == 1, block, pltpu.roll(block, 64, 1))
         e = jnp.concatenate([block] * 16, axis=0).T[0:FX]
         inside = (me > 0) if n == 0 else (me < GRP - 1)
@@ -396,25 +380,27 @@
     near_state, owner, land, far_depth, far_flows, wet_mask = given
     xlow = lax.ppermute(xhi, "px", forth)
     xhigh = lax.ppermute(xlo, "px", back)
-    send = pl.pallas_call(
+    send, zlo, zhi = pl.pallas_call(
         pack_kernel,
-        out_shape=shape(GRP, BLK, 128),
+        out_shape=(shape(GRP, BLK, 128), vmem(3, CX, CY), vmem(3, CX, CY)),
         in_specs=[VM] * 6,
-        out_specs=VM,
+        out_specs=(VM,) * 3,
         compiler_params=PARAMS,
         cost_estimate=cost(2),
         name="pack",
     )(near_state, owner, land, far_depth, far_flows, wet_mask)
     got = lax.all_to_all(send, GROUP, split_axis=0, concat_axis=0, tiled=True)
+    down = lax.ppermute(zhi, "dz", [(i, i + 1) for i in range(NDZ - 1)])
+    up = lax.ppermute(zlo, "dz", [(i + 1, i) for i in range(NDZ - 1)])
     new_frac, sums = pl.pallas_call(
         near_kernel,
         out_shape=(shape(CX, CZ, CY), shape(GRP, ROWS, 128)),
-        in_specs=[VM] * 4,
+        in_specs=[VM] * 6,
         out_specs=(VM,) * 2,
         compiler_params=PARAMS,
         cost_estimate=cost(2),
         name="near",
-    )(near_state, got, xlow, xhigh)
+    )(near_state, got, xlow, xhigh, down, up)
     sums = lax.all_to_all(sums, GROUP, split_axis=0, concat_axis=0, tiled=True)
     pieces, top, bottom = pl.pallas_call(
         functools.partial(edge_kernel, column_height / (CZ * NDZ)),

time: 59.9 us -> 60.5 us (1.010)
  starting transfers between devices: 20.4 us -> 26 us
  waiting for transfers between devices: 14.3 us -> 9.21 us
    ppermute x0 -> x2, starting transfers between devices: none -> 5.56 us  [the longest x1 3.64 us: local(): up = lax.ppermute(zlo, 'dz', [(i + 1, i) for i in range(NDZ - 1)])]
    ppermute x1, waiting for transfers between devices: 8.43 us -> 4.78 us  [local(): xhigh = lax.ppermute(xlo, 'px', back)]
    ppermute x1, waiting for transfers between devices: 3.43 us -> 0.01 us  [local(): xlow = lax.ppermute(xhi, 'px', forth)]
    ppermute x0 -> x2, waiting for transfers between devices: none -> 1.49 us  [the longest x1 1.49 us: local(): up = lax.ppermute(zlo, 'dz', [(i + 1, i) for i in range(NDZ - 1)])]
  transfers between devices with their start and end apart: 5 -> 7, of which waited for: 3 -> 3; matrix products, arithmetic and copies ran while one was open for 0% -> 0% of each run, Pallas kernels for 6% -> 6%
where the time goes in v4:
time: 60.5 us; the launch traced here: 60.1 us
  starting transfers between devices  26 us (43%)
  blocking collectives  14 us (23%)
  Pallas kernels  10.2 us (17%)
  waiting for transfers between devices  9.21 us (15%)
  between operations  0.71 us (1%)
    all_to_all x1, blocking collectives, local(): sums = lax.all_to_all(sums, GROUP, split_axis=0, concat_axis=0, tiled=True)  14 us
    all_to_all x1, starting transfers between devices, local(): got = lax.all_to_all(send, GROUP, split_axis=0, concat_axis=0, tiled=True)  6.05 us
    ppermute x1, starting transfers between devices, local(): xlow = lax.ppermute(xhi, 'px', forth)  5.7 us
    ppermute x1, waiting for transfers between devices, local(): xhigh = lax.ppermute(xlo, 'px', back)  4.78 us
    ppermute x1, starting transfers between devices, local(): up = lax.ppermute(zlo, 'dz', [(i + 1, i) for i in range(NDZ - 1)])  3.64 us
    pallas_call x1, Pallas kernels, local(): pl.pallas_call(far_kernel, out_shape=(shape(3, FX, FY), vmem(3, 8, FY), v...  3.55 us
    ppermute x1, starting transfers between devices, local(): above = lax.ppermute(bottom, 'px', forth)  3.46 us
    ppermute x1, starting transfers between devices, local(): below = lax.ppermute(top, 'px', back)  3.28 us
  transfers between devices with their start and end apart: 7, of which 3 were waited for; matrix products, arithmetic and copies ran while one was open for 0% of the time, Pallas kernels for 6%

profile of v4, /device:TPU:248, one launch (start us, length us, event | category | flops | bytes accessed | tf_op | source)
XLA Modules:
  0.0 60.1 jit_solution(11226041200906927759)
XLA Ops:
  0.6 1.5 %load.1 = (f32[3,8,48,256]{3,2,1,0:T(8,128)S(1)}, s32[4,128]{1,0:T(4,128)S(1)}, s32[4,128]{1,0:T(4,128)S(1)}, f32[64,256]{1,0:T(8,128)S(1)}, f32[2,64,256]{2,1,0...) custom-call(f32[3,8,48,256]{3,2,1,0:T(8,128)} %refs_0_.1, ...), custom_call_target="tpu_custom_call" | custom-call | bytes 3000000 | tf_op jit(solution)/shard_map/load/pallas_call | solution.py:369
  2.2 1.3 %pack.1 = (f32[16,24,128]{2,1,0:T(8,128)}, f32[3,8,256]{2,1,0:T(8,128)S(1)}, f32[3,8,256]{2,1,0:T(8,128)S(1)}) custom-call(f32[3,8,48,256]{3,2,1,0:T(8,128)S(1)} %get-tuple-element.21.near, s32[4,128]{1,0:T(4,128)S(1)} %get-tuple-element.22.owner, s32[4,128]{1,0:T(4,128)S(1)} %get-tuple-element.23.land, f32[64,256]{1,0:T(8,128)S(1)} %get-tuple-element.24.depth, ...), custom_call_target="tpu_custom_call" | custom-call | bytes 6000000 | tf_op jit(solution)/shard_map/pack/pallas_call | solution.py:383
  3.5 6.0 %all-to-all-start = ((f32[16,24,128]{2,1,0:T(8,128)}), f32[16,24,128]{2,1,0:T(8,128)S(1)}, u32[]{:S(2)}, u32[]{:S(2)}) async-start(f32[16,24,128]{2,1,0:T(8,128)} %get-tuple-element.27), calls=%async_computation | async-start | bytes 393216 | tf_op jit(solution)/shard_map/all_to_all | solution.py:392
  9.5 5.7 %collective-permute-start = (f32[3,48,256]{2,1,0:T(8,128)S(1)}, f32[3,48,256]{2,1,0:T(8,128)S(1)}, u32[]{:S(2)}, u32[]{:S(2)}) collective-permute-start(f32[3,48,256]{2,1,0:T(8,128)S(1)} %get-tuple-element.28), channel_id=1, source_target_pairs={{0,16},{16,32},{32,48},{48,64},{64,80},{80,96},{96,112},{112,128},... | collective-permute-start | bytes 442376 | tf_op jit(solution)/shard_map/ppermute | solution.py:381
  15.2 1.9 %collective-permute-start.1 = (f32[3,48,256]{2,1,0:T(8,128)S(1)}, f32[3,48,256]{2,1,0:T(8,128)S(1)}, u32[]{:S(2)}, u32[]{:S(2)}) collective-permute-start(f32[3,48,256]{2,1,0:T(8,128)S(1)} %get-tuple-element.29), channel_id=1, source_target_pairs={{16,0},{32,16},{48,32},{64,48},{80,64},{96,80},{112,96},{128,112},... | collective-permute-start | bytes 442376 | tf_op jit(solution)/shard_map/ppermute | solution.py:382
  17.2 1.9 %collective-permute-start.2 = (f32[3,8,256]{2,1,0:T(8,128)S(1)}, f32[3,8,256]{2,1,0:T(8,128)S(1)}, u32[]{:S(2)}, u32[]{:S(2)}) collective-permute-start(f32[3,8,256]{2,1,0:T(8,128)S(1)} %get-tuple-element.30), channel_id=1, source_target_pairs={{0,1},{1,2},{2,3},{4,5},{5,6},{6,7},{8,9},{9,10},{10,11},{12,13},{... | collective-permute-start | bytes 73736 | tf_op jit(solution)/shard_map/ppermute | solution.py:393
  19.1 3.6 %collective-permute-start.3 = (f32[3,8,256]{2,1,0:T(8,128)S(1)}, f32[3,8,256]{2,1,0:T(8,128)S(1)}, u32[]{:S(2)}, u32[]{:S(2)}) collective-permute-start(f32[3,8,256]{2,1,0:T(8,128)S(1)} %get-tuple-element.31), channel_id=1, source_target_pairs={{1,0},{2,1},{3,2},{5,4},{6,5},{7,6},{9,8},{10,9},{11,10},{13,12},{... | collective-permute-start | bytes 73736 | tf_op jit(solution)/shard_map/ppermute | solution.py:394
  22.7 0.0 collective-permute-done.2.down
  22.7 1.5 %collective-permute-done.3.up = f32[3,8,256]{2,1,0:T(8,128)S(1)} collective-permute-done((f32[3,8,256]{2,1,0:T(8,128)S(1)}, f32[3,8,256]{2,1,0:T(8,128)S(1)}, u32[]{:S(2)}, u32[]{:S(2)}) %collective-permute-start.3) | collective-permute-done | bytes 24608 | tf_op jit(solution)/shard_map/ppermute | solution.py:394
  24.2 0.0 collective-permute-done.xlow
  24.2 4.8 %collective-permute-done.1.xhigh = f32[3,48,256]{2,1,0:T(8,128)S(1)} collective-permute-done((f32[3,48,256]{2,1,0:T(8,128)S(1)}, f32[3,48,256]{2,1,0:T(8,128)S(1)}, u32[]{:S(2)}, u32[]{:S(2)}) %collective-permute-start.1) | collective-permute-done | bytes 147488 | tf_op jit(solution)/shard_map/ppermute | solution.py:382
  29.0 0.0 all-to-all-done.got
  29.0 1.9 %near.1 = (f32[8,48,256]{2,1,0:T(8,128)}, f32[16,48,128]{2,1,0:T(8,128)S(1)}) custom-call(f32[3,8,48,256]{3,2,1,0:T(8,128)S(1)} %get-tuple-element.21.near, f32[16,24,128]{2,1,0:T(8,128)S(1)} %all-to-all-done.got, f32[3,48,256]{2,1,0:T(8,128)S(1)} %collective-permute-done.xlow, f32[3,48,256]{2,1,0:T(8,128)S(1)} %collective-permute-done.1.xhigh, ...), custom_call_target="tpu_custom_call" | custom-call | bytes 6000000 | tf_op jit(solution)/shard_map/near/pallas_call | solution.py:395
  31.0 14.0 %all_to_all.10.sums = f32[16,48,128]{2,1,0:T(8,128)S(1)} all-to-all(f32[16,48,128]{2,1,0:T(8,128)S(1)} %get-tuple-element.33), channel_id=1, replica_groups=mesh['px'=48,'py'=4,'dz'=4] {'py','dz'}, dimensions={0} | all-to-all | bytes 786432 | tf_op jit(solution)/shard_map/all_to_all | solution.py:404
  44.9 1.2 %edge.1 = (f32[2,4,48,128]{3,2,1,0:T(8,128)S(1)}, f32[8,256]{1,0:T(8,128)S(1)}, f32[8,256]{1,0:T(8,128)S(1)}) custom-call(f32[16,24,128]{2,1,0:T(8,128)S(1)} %all-to-all-done.got, f32[16,48,128]{2,1,0:T(8,128)S(1)} %all_to_all.10.sums, f32[64,256]{1,0:T(8,128)S(1)} %get-tuple-element.24.depth, f32[2,64,256]{2,1,0:T(8,128)S(1)} %get-tuple-element.25.flows, ...), custom_call_target="tpu_custom_call" | custom-call | bytes 6000000 | tf_op jit(solution)/shard_map/edge/pallas_call | solution.py:405
  46.2 3.5 %collective-permute-start.4 = (f32[8,256]{1,0:T(8,128)S(1)}, f32[8,256]{1,0:T(8,128)S(1)}, u32[]{:S(2)}, u32[]{:S(2)}) collective-permute-start(f32[8,256]{1,0:T(8,128)S(1)} %get-tuple-element.38), channel_id=1, source_target_pairs={{0,16},{16,32},{32,48},{48,64},{64,80},{80,96},{96,112},{112,128},... | collective-permute-start | bytes 24584 | tf_op jit(solution)/shard_map/ppermute | solution.py:415
  49.6 3.3 %collective-permute-start.5 = (f32[8,256]{1,0:T(8,128)S(1)}, f32[8,256]{1,0:T(8,128)S(1)}, u32[]{:S(2)}, u32[]{:S(2)}) collective-permute-start(f32[8,256]{1,0:T(8,128)S(1)} %get-tuple-element.39), channel_id=1, source_target_pairs={{16,0},{32,16},{48,32},{64,48},{80,64},{96,80},{112,96},{128,112},... | collective-permute-start | bytes 24584 | tf_op jit(solution)/shard_map/ppermute | solution.py:416
  52.9 3.5 %far.1 = (f32[3,64,256]{2,1,0:T(8,128)}, f32[3,8,256]{2,1,0:T(8,128)S(1)}, f32[3,8,256]{2,1,0:T(8,128)S(1)}) custom-call(f32[16,24,128]{2,1,0:T(8,128)S(1)} %all-to-all-done.got, f32[2,4,48,128]{3,2,1,0:T(8,128)S(1)} %get-tuple-element.34.pieces, f32[64,256]{1,0:T(8,128)S(1)} %get-tuple-element.24.depth, f32[2,64,256]{2,1,0:T(8,128)S(1)} %get-tuple-element.25.flows, ...), custom_call_target="tpu_custom_call" | custom-call | bytes 15000000 | tf_op jit(solution)/shard_map/far/pallas_call | solution.py:417
  56.5 0.0 collective-permute-done.4.above
  56.5 2.9 %collective-permute-done.5.below = f32[8,256]{1,0:T(8,128)S(1)} collective-permute-done((f32[8,256]{1,0:T(8,128)S(1)}, f32[8,256]{1,0:T(8,128)S(1)}, u32[]{:S(2)}, u32[]{:S(2)}) %collective-permute-start.5) | collective-permute-done | bytes 8224 | tf_op jit(solution)/shard_map/ppermute | solution.py:416
  59.4 0.7 %join.1 = f32[3,64,256]{2,1,0:T(8,128)} custom-call(f32[3,64,256]{2,1,0:T(8,128)} %get-tuple-element.35.part, f32[3,8,256]{2,1,0:T(8,128)S(1)} %get-tuple-element.36.head, f32[3,8,256]{2,1,0:T(8,128)S(1)} %get-tuple-element.37.tail, f32[8,256]{1,0:T(8,128)S(1)} %collective-permute-done.4.above, ...), custom_call_target="tpu_custom_call", output_to_operand_aliasing={{}: (0, {})} | custom-call | bytes 3000000 | tf_op jit(solution)/shard_map/join/pallas_call | solution.py:427
Async XLA Ops:
  3.5 25.5 %all-to-all-start = ((f32[16,24,128]{2,1,0:T(8,128)}), f32[16,24,128]{2,1,0:T(8,128)S(1)}, u32[]{:S(2)}, u32[]{:S(2)}) async-start(f32[16,24,128]{2,1,0:T(8,128)} %get-tuple-element.27), calls=%async_computation | async-start | bytes 393216 | tf_op jit(solution)/shard_map/all_to_all | solution.py:392
  9.5 14.7 %collective-permute-start = (f32[3,48,256]{2,1,0:T(8,128)S(1)}, f32[3,48,256]{2,1,0:T(8,128)S(1)}, u32[]{:S(2)}, u32[]{:S(2)}) collective-permute-start(f32[3,48,256]{2,1,0:T(8,128)S(1)} %get-tuple-element.28), channel_id=1, source_target_pairs={{0,16},{16,32},{32,48},{48,64},{64,80},{80,96},{96,112},{112,128},... | collective-permute-start | bytes 442376 | tf_op jit(solution)/shard_map/ppermute | solution.py:381
  15.2 13.8 %collective-permute-start.1 = (f32[3,48,256]{2,1,0:T(8,128)S(1)}, f32[3,48,256]{2,1,0:T(8,128)S(1)}, u32[]{:S(2)}, u32[]{:S(2)}) collective-permute-start(f32[3,48,256]{2,1,0:T(8,128)S(1)} %get-tuple-element.29), channel_id=1, source_target_pairs={{16,0},{32,16},{48,32},{64,48},{80,64},{96,80},{112,96},{128,112},... | collective-permute-start | bytes 442376 | tf_op jit(solution)/shard_map/ppermute | solution.py:382
  17.2 5.6 %collective-permute-start.2 = (f32[3,8,256]{2,1,0:T(8,128)S(1)}, f32[3,8,256]{2,1,0:T(8,128)S(1)}, u32[]{:S(2)}, u32[]{:S(2)}) collective-permute-start(f32[3,8,256]{2,1,0:T(8,128)S(1)} %get-tuple-element.30), channel_id=1, source_target_pairs={{0,1},{1,2},{2,3},{4,5},{5,6},{6,7},{8,9},{9,10},{10,11},{12,13},{... | collective-permute-start | bytes 73736 | tf_op jit(solution)/shard_map/ppermute | solution.py:393
  19.1 5.1 %collective-permute-start.3 = (f32[3,8,256]{2,1,0:T(8,128)S(1)}, f32[3,8,256]{2,1,0:T(8,128)S(1)}, u32[]{:S(2)}, u32[]{:S(2)}) collective-permute-start(f32[3,8,256]{2,1,0:T(8,128)S(1)} %get-tuple-element.31), channel_id=1, source_target_pairs={{1,0},{2,1},{3,2},{5,4},{6,5},{7,6},{9,8},{10,9},{11,10},{13,12},{... | collective-permute-start | bytes 73736 | tf_op jit(solution)/shard_map/ppermute | solution.py:394
  46.2 10.3 %collective-permute-start.4 = (f32[8,256]{1,0:T(8,128)S(1)}, f32[8,256]{1,0:T(8,128)S(1)}, u32[]{:S(2)}, u32[]{:S(2)}) collective-permute-start(f32[8,256]{1,0:T(8,128)S(1)} %get-tuple-element.38), channel_id=1, source_target_pairs={{0,16},{16,32},{32,48},{48,64},{64,80},{80,96},{96,112},{112,128},... | collective-permute-start | bytes 24584 | tf_op jit(solution)/shard_map/ppermute | solution.py:415
  49.6 9.8 %collective-permute-start.5 = (f32[8,256]{1,0:T(8,128)S(1)}, f32[8,256]{1,0:T(8,128)S(1)}, u32[]{:S(2)}, u32[]{:S(2)}) collective-permute-start(f32[8,256]{1,0:T(8,128)S(1)} %get-tuple-element.39), channel_id=1, source_target_pairs={{16,0},{32,16},{48,32},{64,48},{80,64},{96,80},{112,96},{128,112},... | collective-permute-start | bytes 24584 | tf_op jit(solution)/shard_map/ppermute | solution.py:416

commit v5 on v4

--- a/solution.py
+++ b/solution.py
@@ -44,16 +44,20 @@
 
 
 def load_kernel(*refs):
-    sources, copies, (xlo, xhi), sem = refs[:6], refs[6:12], refs[12:14], refs[14]
+    sources, copies, (xlo, xhi, zlo, zhi), sem = refs[:6], refs[6:12], refs[12:16], refs[16]
     moves = [(sources[0].at[:, 0], xlo), (sources[0].at[:, CX - 1], xhi), *zip(sources, copies)]
     moves = [pltpu.make_async_copy(a, b, sem.at[n]) for n, (a, b) in enumerate(moves)]
     for move in moves:
         move.start()
     for move in moves:
         move.wait()
-
-
-def pack_kernel(near, owner, land, depth, flows, mask, out, zlo, zhi):
+    near = copies[0]
+    for f in range(3):
+        zlo[f] = near[f, :, 0, :]
+        zhi[f] = near[f, :, CZ - 1, :]
+
+
+def pack_kernel(near, owner, land, depth, flows, mask, out):
     py = lax.axis_index("py")
     dz = lax.axis_index("dz")
     me = py * NDZ + dz
@@ -84,10 +88,6 @@
     @pl.when(me < GRP - 1)
     def _():
         out[me + 1, SIDE:BLK] = edge(FY - 1)
-
-    for f in range(3):
-        zlo[f] = near[f, :, 0, :]
-        zhi[f] = near[f, :, CZ - 1, :]
 
     def yface(dst, y):
         k = lane_iota((CZ, 128))
@@ -366,12 +366,13 @@
     owner = column_owner.reshape(4, 128)
     land = landing.reshape(4, 128)
     given = (near_state, owner, land, far_depth, far_flows, wet_mask)
-    *given, xlo, xhi = pl.pallas_call(
+    *given, xlo, xhi, zlo, zhi = pl.pallas_call(
         load_kernel,
         out_shape=[pltpu.VMEM(x.shape, x.dtype) for x in given]
-        + [vmem(3, CZ, CY)] * 2,
+        + [vmem(3, CZ, CY)] * 2
+        + [vmem(3, CX, CY)] * 2,
         in_specs=[HBM] * 6,
-        out_specs=[VM] * 8,
+        out_specs=[VM] * 10,
         scratch_shapes=[pltpu.SemaphoreType.DMA((8,))],
         compiler_params=PARAMS,
         cost_estimate=cost(1),
@@ -380,18 +381,18 @@
     near_state, owner, land, far_depth, far_flows, wet_mask = given
     xlow = lax.ppermute(xhi, "px", forth)
     xhigh = lax.ppermute(xlo, "px", back)
-    send, zlo, zhi = pl.pallas_call(
+    down = lax.ppermute(zhi, "dz", [(i, i + 1) for i in range(NDZ - 1)])
+    up = lax.ppermute(zlo, "dz", [(i + 1, i) for i in range(NDZ - 1)])
+    send = pl.pallas_call(
         pack_kernel,
-        out_shape=(shape(GRP, BLK, 128), vmem(3, CX, CY), vmem(3, CX, CY)),
+        out_shape=shape(GRP, BLK, 128),
         in_specs=[VM] * 6,
-        out_specs=(VM,) * 3,
+        out_specs=VM,
         compiler_params=PARAMS,
         cost_estimate=cost(2),
         name="pack",
     )(near_state, owner, land, far_depth, far_flows, wet_mask)
     got = lax.all_to_all(send, GROUP, split_axis=0, concat_axis=0, tiled=True)
-    down = lax.ppermute(zhi, "dz", [(i, i + 1) for i in range(NDZ - 1)])
-    up = lax.ppermute(zlo, "dz", [(i + 1, i) for i in range(NDZ - 1)])
     new_frac, sums = pl.pallas_call(
         near_kernel,
         out_shape=(shape(CX, CZ, CY), shape(GRP, ROWS, 128)),

time: 60.5 us -> 60.5 us (level)
  no operation moved by 1% of the time
where the time goes in v5:
time: 60.5 us; the launch traced here: 60.1 us
  starting transfers between devices  26 us (43%)
  blocking collectives  14 us (23%)
  Pallas kernels  10.2 us (17%)
  waiting for transfers between devices  9.21 us (15%)
  between operations  0.71 us (1%)
    all_to_all x1, blocking collectives, local(): sums = lax.all_to_all(sums, GROUP, split_axis=0, concat_axis=0, tiled=True)  14 us
    all_to_all x1, starting transfers between devices, local(): got = lax.all_to_all(send, GROUP, split_axis=0, concat_axis=0, tiled=True)  6.05 us
    ppermute x1, starting transfers between devices, local(): xlow = lax.ppermute(xhi, 'px', forth)  5.7 us
    ppermute x1, waiting for transfers between devices, local(): xhigh = lax.ppermute(xlo, 'px', back)  4.78 us
    ppermute x1, starting transfers between devices, local(): up = lax.ppermute(zlo, 'dz', [(i + 1, i) for i in range(NDZ - 1)])  3.64 us
    pallas_call x1, Pallas kernels, local(): pl.pallas_call(far_kernel, out_shape=(shape(3, FX, FY), vmem(3, 8, FY), v...  3.55 us
    ppermute x1, starting transfers between devices, local(): above = lax.ppermute(bottom, 'px', forth)  3.46 us
    ppermute x1, starting transfers between devices, local(): below = lax.ppermute(top, 'px', back)  3.28 us
  transfers between devices with their start and end apart: 7, of which 3 were waited for; matrix products, arithmetic and copies ran while one was open for 0% of the time, Pallas kernels for 6%

profile of v5, /device:TPU:248, one launch (start us, length us, event | category | flops | bytes accessed | tf_op | source)
XLA Modules:
  0.0 60.1 jit_solution(15813496596853691361)
XLA Ops:
  0.6 1.6 %load.1 = (f32[3,8,48,256]{3,2,1,0:T(8,128)S(1)}, s32[4,128]{1,0:T(4,128)S(1)}, s32[4,128]{1,0:T(4,128)S(1)}, f32[64,256]{1,0:T(8,128)S(1)}, f32[2,64,256]{2,1,0...) custom-call(f32[3,8,48,256]{3,2,1,0:T(8,128)} %refs_0_.1, ...), custom_call_target="tpu_custom_call" | custom-call | bytes 3000000 | tf_op jit(solution)/shard_map/load/pallas_call | solution.py:369
  2.2 1.3 %pack.1 = f32[16,24,128]{2,1,0:T(8,128)} custom-call(f32[3,8,48,256]{3,2,1,0:T(8,128)S(1)} %get-tuple-element.20.near, s32[4,128]{1,0:T(4,128)S(1)} %get-tuple-element.21.owner, s32[4,128]{1,0:T(4,128)S(1)} %get-tuple-element.22.land, f32[64,256]{1,0:T(8,128)S(1)} %get-tuple-element.23.depth, f32[2,64,256]{2,1,0:T(8,128)S(1)} %get-tuple-element.24.flows, ...), custom_call_target="tpu_custom_call" | custom-call | bytes 6000000 | tf_op jit(solution)/shard_map/pack/pallas_call | solution.py:386
  3.5 6.1 %all-to-all-start = ((f32[16,24,128]{2,1,0:T(8,128)}), f32[16,24,128]{2,1,0:T(8,128)S(1)}, u32[]{:S(2)}, u32[]{:S(2)}) async-start(f32[16,24,128]{2,1,0:T(8,128)} %pack.1), calls=%async_computation | async-start | bytes 393216 | tf_op jit(solution)/shard_map/all_to_all | solution.py:395
  9.5 5.7 %collective-permute-start = (f32[3,48,256]{2,1,0:T(8,128)S(1)}, f32[3,48,256]{2,1,0:T(8,128)S(1)}, u32[]{:S(2)}, u32[]{:S(2)}) collective-permute-start(f32[3,48,256]{2,1,0:T(8,128)S(1)} %get-tuple-element.26), channel_id=1, source_target_pairs={{0,16},{16,32},{32,48},{48,64},{64,80},{80,96},{96,112},{112,128},... | collective-permute-start | bytes 442376 | tf_op jit(solution)/shard_map/ppermute | solution.py:382
  15.2 1.9 %collective-permute-start.1 = (f32[3,48,256]{2,1,0:T(8,128)S(1)}, f32[3,48,256]{2,1,0:T(8,128)S(1)}, u32[]{:S(2)}, u32[]{:S(2)}) collective-permute-start(f32[3,48,256]{2,1,0:T(8,128)S(1)} %get-tuple-element.27), channel_id=1, source_target_pairs={{16,0},{32,16},{48,32},{64,48},{80,64},{96,80},{112,96},{128,112},... | collective-permute-start | bytes 442376 | tf_op jit(solution)/shard_map/ppermute | solution.py:383
  17.2 1.9 %collective-permute-start.2 = (f32[3,8,256]{2,1,0:T(8,128)S(1)}, f32[3,8,256]{2,1,0:T(8,128)S(1)}, u32[]{:S(2)}, u32[]{:S(2)}) collective-permute-start(f32[3,8,256]{2,1,0:T(8,128)S(1)} %get-tuple-element.28), channel_id=1, source_target_pairs={{0,1},{1,2},{2,3},{4,5},{5,6},{6,7},{8,9},{9,10},{10,11},{12,13},{... | collective-permute-start | bytes 73736 | tf_op jit(solution)/shard_map/ppermute | solution.py:384
  19.1 3.6 %collective-permute-start.3 = (f32[3,8,256]{2,1,0:T(8,128)S(1)}, f32[3,8,256]{2,1,0:T(8,128)S(1)}, u32[]{:S(2)}, u32[]{:S(2)}) collective-permute-start(f32[3,8,256]{2,1,0:T(8,128)S(1)} %get-tuple-element.29), channel_id=1, source_target_pairs={{1,0},{2,1},{3,2},{5,4},{6,5},{7,6},{9,8},{10,9},{11,10},{13,12},{... | collective-permute-start | bytes 73736 | tf_op jit(solution)/shard_map/ppermute | solution.py:385
  22.7 0.0 collective-permute-done.2.down
  22.7 1.5 %collective-permute-done.3.up = f32[3,8,256]{2,1,0:T(8,128)S(1)} collective-permute-done((f32[3,8,256]{2,1,0:T(8,128)S(1)}, f32[3,8,256]{2,1,0:T(8,128)S(1)}, u32[]{:S(2)}, u32[]{:S(2)}) %collective-permute-start.3) | collective-permute-done | bytes 24608 | tf_op jit(solution)/shard_map/ppermute | solution.py:385
  24.2 0.0 collective-permute-done.xlow
  24.2 4.8 %collective-permute-done.1.xhigh = f32[3,48,256]{2,1,0:T(8,128)S(1)} collective-permute-done((f32[3,48,256]{2,1,0:T(8,128)S(1)}, f32[3,48,256]{2,1,0:T(8,128)S(1)}, u32[]{:S(2)}, u32[]{:S(2)}) %collective-permute-start.1) | collective-permute-done | bytes 147488 | tf_op jit(solution)/shard_map/ppermute | solution.py:383
  29.0 0.0 all-to-all-done.got
  29.0 1.9 %near.1 = (f32[8,48,256]{2,1,0:T(8,128)}, f32[16,48,128]{2,1,0:T(8,128)S(1)}) custom-call(f32[3,8,48,256]{3,2,1,0:T(8,128)S(1)} %get-tuple-element.20.near, f32[16,24,128]{2,1,0:T(8,128)S(1)} %all-to-all-done.got, f32[3,48,256]{2,1,0:T(8,128)S(1)} %collective-permute-done.xlow, f32[3,48,256]{2,1,0:T(8,128)S(1)} %collective-permute-done.1.xhigh, ...), custom_call_target="tpu_custom_call" | custom-call | bytes 6000000 | tf_op jit(solution)/shard_map/near/pallas_call | solution.py:396
  31.0 14.0 %all_to_all.10.sums = f32[16,48,128]{2,1,0:T(8,128)S(1)} all-to-all(f32[16,48,128]{2,1,0:T(8,128)S(1)} %get-tuple-element.31), channel_id=1, replica_groups=mesh['px'=48,'py'=4,'dz'=4] {'py','dz'}, dimensions={0} | all-to-all | bytes 786432 | tf_op jit(solution)/shard_map/all_to_all | solution.py:405
  44.9 1.2 %edge.1 = (f32[2,4,48,128]{3,2,1,0:T(8,128)S(1)}, f32[8,256]{1,0:T(8,128)S(1)}, f32[8,256]{1,0:T(8,128)S(1)}) custom-call(f32[16,24,128]{2,1,0:T(8,128)S(1)} %all-to-all-done.got, f32[16,48,128]{2,1,0:T(8,128)S(1)} %all_to_all.10.sums, f32[64,256]{1,0:T(8,128)S(1)} %get-tuple-element.23.depth, f32[2,64,256]{2,1,0:T(8,128)S(1)} %get-tuple-element.24.flows, ...), custom_call_target="tpu_custom_call" | custom-call | bytes 6000000 | tf_op jit(solution)/shard_map/edge/pallas_call | solution.py:406
  46.2 3.5 %collective-permute-start.4 = (f32[8,256]{1,0:T(8,128)S(1)}, f32[8,256]{1,0:T(8,128)S(1)}, u32[]{:S(2)}, u32[]{:S(2)}) collective-permute-start(f32[8,256]{1,0:T(8,128)S(1)} %get-tuple-element.36), channel_id=1, source_target_pairs={{0,16},{16,32},{32,48},{48,64},{64,80},{80,96},{96,112},{112,128},... | collective-permute-start | bytes 24584 | tf_op jit(solution)/shard_map/ppermute | solution.py:416
  49.6 3.3 %collective-permute-start.5 = (f32[8,256]{1,0:T(8,128)S(1)}, f32[8,256]{1,0:T(8,128)S(1)}, u32[]{:S(2)}, u32[]{:S(2)}) collective-permute-start(f32[8,256]{1,0:T(8,128)S(1)} %get-tuple-element.37), channel_id=1, source_target_pairs={{16,0},{32,16},{48,32},{64,48},{80,64},{96,80},{112,96},{128,112},... | collective-permute-start | bytes 24584 | tf_op jit(solution)/shard_map/ppermute | solution.py:417
  52.9 3.5 %far.1 = (f32[3,64,256]{2,1,0:T(8,128)}, f32[3,8,256]{2,1,0:T(8,128)S(1)}, f32[3,8,256]{2,1,0:T(8,128)S(1)}) custom-call(f32[16,24,128]{2,1,0:T(8,128)S(1)} %all-to-all-done.got, f32[2,4,48,128]{3,2,1,0:T(8,128)S(1)} %get-tuple-element.32.pieces, f32[64,256]{1,0:T(8,128)S(1)} %get-tuple-element.23.depth, f32[2,64,256]{2,1,0:T(8,128)S(1)} %get-tuple-element.24.flows, ...), custom_call_target="tpu_custom_call" | custom-call | bytes 15000000 | tf_op jit(solution)/shard_map/far/pallas_call | solution.py:418
  56.5 0.0 collective-permute-done.4.above
  56.5 2.9 %collective-permute-done.5.below = f32[8,256]{1,0:T(8,128)S(1)} collective-permute-done((f32[8,256]{1,0:T(8,128)S(1)}, f32[8,256]{1,0:T(8,128)S(1)}, u32[]{:S(2)}, u32[]{:S(2)}) %collective-permute-start.5) | collective-permute-done | bytes 8224 | tf_op jit(solution)/shard_map/ppermute | solution.py:417
  59.4 0.7 %join.1 = f32[3,64,256]{2,1,0:T(8,128)} custom-call(f32[3,64,256]{2,1,0:T(8,128)} %get-tuple-element.33.part, f32[3,8,256]{2,1,0:T(8,128)S(1)} %get-tuple-element.34.head, f32[3,8,256]{2,1,0:T(8,128)S(1)} %get-tuple-element.35.tail, f32[8,256]{1,0:T(8,128)S(1)} %collective-permute-done.4.above, ...), custom_call_target="tpu_custom_call", output_to_operand_aliasing={{}: (0, {})} | custom-call | bytes 3000000 | tf_op jit(solution)/shard_map/join/pallas_call | solution.py:428
Async XLA Ops:
  3.5 25.6 %all-to-all-start = ((f32[16,24,128]{2,1,0:T(8,128)}), f32[16,24,128]{2,1,0:T(8,128)S(1)}, u32[]{:S(2)}, u32[]{:S(2)}) async-start(f32[16,24,128]{2,1,0:T(8,128)} %pack.1), calls=%async_computation | async-start | bytes 393216 | tf_op jit(solution)/shard_map/all_to_all | solution.py:395
  9.5 14.7 %collective-permute-start = (f32[3,48,256]{2,1,0:T(8,128)S(1)}, f32[3,48,256]{2,1,0:T(8,128)S(1)}, u32[]{:S(2)}, u32[]{:S(2)}) collective-permute-start(f32[3,48,256]{2,1,0:T(8,128)S(1)} %get-tuple-element.26), channel_id=1, source_target_pairs={{0,16},{16,32},{32,48},{48,64},{64,80},{80,96},{96,112},{112,128},... | collective-permute-start | bytes 442376 | tf_op jit(solution)/shard_map/ppermute | solution.py:382
  15.2 13.8 %collective-permute-start.1 = (f32[3,48,256]{2,1,0:T(8,128)S(1)}, f32[3,48,256]{2,1,0:T(8,128)S(1)}, u32[]{:S(2)}, u32[]{:S(2)}) collective-permute-start(f32[3,48,256]{2,1,0:T(8,128)S(1)} %get-tuple-element.27), channel_id=1, source_target_pairs={{16,0},{32,16},{48,32},{64,48},{80,64},{96,80},{112,96},{128,112},... | collective-permute-start | bytes 442376 | tf_op jit(solution)/shard_map/ppermute | solution.py:383
  17.2 5.6 %collective-permute-start.2 = (f32[3,8,256]{2,1,0:T(8,128)S(1)}, f32[3,8,256]{2,1,0:T(8,128)S(1)}, u32[]{:S(2)}, u32[]{:S(2)}) collective-permute-start(f32[3,8,256]{2,1,0:T(8,128)S(1)} %get-tuple-element.28), channel_id=1, source_target_pairs={{0,1},{1,2},{2,3},{4,5},{5,6},{6,7},{8,9},{9,10},{10,11},{12,13},{... | collective-permute-start | bytes 73736 | tf_op jit(solution)/shard_map/ppermute | solution.py:384
  19.1 5.1 %collective-permute-start.3 = (f32[3,8,256]{2,1,0:T(8,128)S(1)}, f32[3,8,256]{2,1,0:T(8,128)S(1)}, u32[]{:S(2)}, u32[]{:S(2)}) collective-permute-start(f32[3,8,256]{2,1,0:T(8,128)S(1)} %get-tuple-element.29), channel_id=1, source_target_pairs={{1,0},{2,1},{3,2},{5,4},{6,5},{7,6},{9,8},{10,9},{11,10},{13,12},{... | collective-permute-start | bytes 73736 | tf_op jit(solution)/shard_map/ppermute | solution.py:385
  46.2 10.3 %collective-permute-start.4 = (f32[8,256]{1,0:T(8,128)S(1)}, f32[8,256]{1,0:T(8,128)S(1)}, u32[]{:S(2)}, u32[]{:S(2)}) collective-permute-start(f32[8,256]{1,0:T(8,128)S(1)} %get-tuple-element.36), channel_id=1, source_target_pairs={{0,16},{16,32},{32,48},{48,64},{64,80},{80,96},{96,112},{112,128},... | collective-permute-start | bytes 24584 | tf_op jit(solution)/shard_map/ppermute | solution.py:416
  49.6 9.8 %collective-permute-start.5 = (f32[8,256]{1,0:T(8,128)S(1)}, f32[8,256]{1,0:T(8,128)S(1)}, u32[]{:S(2)}, u32[]{:S(2)}) collective-permute-start(f32[8,256]{1,0:T(8,128)S(1)} %get-tuple-element.37), channel_id=1, source_target_pairs={{16,0},{32,16},{48,32},{64,48},{80,64},{96,80},{112,96},{128,112},... | collective-permute-start | bytes 24584 | tf_op jit(solution)/shard_map/ppermute | solution.py:417

commit v6 on v3

--- a/solution.py
+++ b/solution.py
@@ -116,58 +116,66 @@
         yface(me + NDZ, CY - 1)
 
 
-def near_kernel(near, got, xlow, xhigh, frac, sums):
+def inner_kernel(near, xlow, xhigh, mid, vely):
+    lane = lane_iota((CZ, CY))
+    row = lax.broadcasted_iota(jnp.int32, (CZ, CY), 0)
+    for x in range(CX):
+        velx = near[1, x]
+        velv = near[2, x]
+        vely[x] = jnp.where(lane[:, 0:128] == 127, velv[:, 128:], velv[:, 0:128])
+        for f in range(3):
+            q = near[f, x]
+            xp = near[f, x + 1] if x < CX - 1 else xhigh[f]
+            xm = near[f, x - 1] if x > 0 else xlow[f]
+            yp = jnp.where(lane == CY - 1, 0.0, pltpu.roll(q, CY - 1, 1))
+            ym = jnp.where(lane == 0, 0.0, pltpu.roll(q, 1, 1))
+            zp = jnp.where(row == CZ - 1, 0.0, pltpu.roll(q, CZ - 1, 0))
+            zm = jnp.where(row == 0, 0.0, pltpu.roll(q, 1, 0))
+            dx = xp - xm
+            dy = yp - ym
+            lap = xp + xm + yp + ym + zp + zm - 6.0 * q
+            moved = q - advect_coef * (velx * dx + velv * dy) + diffuse_coef * lap
+            if f == 0:
+                fdx, fdy = dx, dy
+            elif f == 1:
+                moved = moved - slope_coef * fdx
+            else:
+                moved = moved - slope_coef * fdy
+            mid[f, x] = moved
+
+
+def near_kernel(mid, vely, got, frac, sums):
     py = lax.axis_index("py")
     dz = lax.axis_index("dz")
     me = py * NDZ + dz
-    at_l = jnp.maximum(me - NDZ, 0)
-    at_r = jnp.minimum(me + NDZ, GRP - 1)
-    at_d = jnp.maximum(me - 1, 0)
-    at_u = jnp.minimum(me + 1, GRP - 1)
-    left = jnp.where(py > 0, got[at_l, 0:ROWS], 0.0)
-    right = jnp.where(py < NPY - 1, got[at_r, 0:ROWS], 0.0)
-    down = jnp.where(dz > 0, got[at_d, 0:ROWS], 0.0)
-    up = jnp.where(dz < NDZ - 1, got[at_u, 0:ROWS], 0.0)
-    lane = lane_iota((CZ, CY))
-    row = lax.broadcasted_iota(jnp.int32, (CZ, CY), 0)
-
-    def face_row(face, f, x):
-        return jnp.concatenate(
-            [face[(f * 2 + h) * 8 + x : (f * 2 + h) * 8 + x + 1] for h in range(2)], axis=1
-        )
-
+    left = jnp.where(py > 0, got[jnp.maximum(me - NDZ, 0), 0:ROWS], 0.0)
+    right = jnp.where(py < NPY - 1, got[jnp.minimum(me + NDZ, GRP - 1), 0:ROWS], 0.0)
+    down = jnp.where(dz > 0, got[jnp.maximum(me - 1, 0), 0:ROWS], 0.0) * diffuse_coef
+    up = jnp.where(dz < NDZ - 1, got[jnp.minimum(me + 1, GRP - 1), 0:ROWS], 0.0) * diffuse_coef
+    lane = lane_iota((CZ, 128))
+    row = lax.broadcasted_iota(jnp.int32, (8, 128), 0)
     for p in range(CX):
         x = x_order(p)
-        velx = near[1, x]
-        vely = near[2, x]
-        new = []
-        for f in range(3):
-            q = near[f, x]
-            k = f * CX + x
-            xp = near[f, x + 1] if x < CX - 1 else xhigh[f]
-            xm = near[f, x - 1] if x > 0 else xlow[f]
-            yp = jnp.where(lane == CY - 1, right[:, k : k + 1], pltpu.roll(q, CY - 1, 1))
-            ym = jnp.where(lane == 0, left[:, k : k + 1], pltpu.roll(q, 1, 1))
-            zp = jnp.where(row == CZ - 1, face_row(up, f, x), pltpu.roll(q, CZ - 1, 0))
-            zm = jnp.where(row == 0, face_row(down, f, x), pltpu.roll(q, 1, 0))
-            dx = xp - xm
-            dy = yp - ym
-            lap = xp + xm + yp + ym + zp + zm - 6.0 * q
-            moved = q - advect_coef * (velx * dx + vely * dy) + diffuse_coef * lap
-            if f == 0:
-                fdx, fdy = dx, dy
-            new.append(moved)
-        frac[x] = new[0]
-        parts = (
-            new[0],
-            new[0] * (new[1] - slope_coef * fdx),
-            new[0] * (new[2] - slope_coef * fdy),
-        )
-        for f in range(3):
-            total = jnp.sum(parts[f], axis=0, keepdims=True)
-            for h in range(2):
+        for h in range(2):
+            lanes = slice(h * 128, (h + 1) * 128)
+            side, sign, edge = (left, 1.0, 0) if h == 0 else (right, -1.0, 127)
+            coef = diffuse_coef + (sign * advect_coef) * vely[x]
+            new = []
+            for f in range(3):
+                face = side[:, f * CX + x : f * CX + x + 1]
+                term = face * coef
+                if f == 2:
+                    term = term + (sign * slope_coef) * side[:, x : x + 1]
+                n = mid[f, x, :, lanes] + jnp.where(lane == edge, term, 0.0)
+                r = (f * 2 + h) * 8 + x
+                first = n[0:8] + jnp.where(row == 0, down[r : r + 1], 0.0)
+                last = n[CZ - 8 : CZ] + jnp.where(row == 7, up[r : r + 1], 0.0)
+                new.append(jnp.concatenate([first, n[8 : CZ - 8], last], axis=0))
+            frac[x, :, lanes] = new[0]
+            for f in range(3):
+                part = new[0] if f == 0 else new[0] * new[f]
                 r = (f * 2 + h) * 8 + p
-                sums[0, r : r + 1] = total[:, h * 128 : (h + 1) * 128]
+                sums[0, r : r + 1] = jnp.sum(part, axis=0, keepdims=True)
     whole = sums[0]
     for b in range(1, GRP):
         sums[b] = whole
@@ -406,15 +414,24 @@
         name="pack",
     )(near_state, owner, land, far_depth, far_flows, wet_mask)
     got = lax.all_to_all(send, GROUP, split_axis=0, concat_axis=0, tiled=True)
+    mid, vely = pl.pallas_call(
+        inner_kernel,
+        out_shape=(vmem(3, CX, CZ, CY), vmem(CX, CZ, 128)),
+        in_specs=[VM] * 3,
+        out_specs=(VM,) * 2,
+        compiler_params=PARAMS,
+        cost_estimate=cost(2),
+        name="inner",
+    )(near_state, xlow, xhigh)
     new_frac, sums = pl.pallas_call(
         near_kernel,
         out_shape=(shape(CX, CZ, CY), shape(GRP, ROWS, 128)),
-        in_specs=[VM] * 4,
+        in_specs=[VM] * 3,
         out_specs=(VM,) * 2,
         compiler_params=PARAMS,
         cost_estimate=cost(2),
         name="near",
-    )(near_state, got, xlow, xhigh)
+    )(mid, vely, got)
     sums = lax.all_to_all(sums, GROUP, split_axis=0, concat_axis=0, tiled=True)
     pieces, top, bottom = pl.pallas_call(
         functools.partial(edge_kernel, column_height / (CZ * NDZ)),

time: 59.9 us -> 60.4 us (level)
    pallas_call x0 -> x1, Pallas kernels: none -> 1.06 us  [local(): pl.pallas_call(inner_kernel, out_shape=(vmem(3, CX, CZ, CY), vmem(CX, CZ,...]
  transfers between devices with their start and end apart: 5 -> 5, of which waited for: 3 -> 3; matrix products, arithmetic and copies ran while one was open for 0% -> 0% of each run, Pallas kernels for 6% -> 8%
where the time goes in v6:
time: 60.4 us; the launch traced here: 60 us
  starting transfers between devices  20.4 us (34%)
  waiting for transfers between devices  14.3 us (24%)
  blocking collectives  14 us (23%)
  Pallas kernels  10.7 us (18%)
  between operations  0.7 us (1%)
    all_to_all x1, blocking collectives, local(): sums = lax.all_to_all(sums, GROUP, split_axis=0, concat_axis=0, tiled=True)  14 us
    ppermute x1, waiting for transfers between devices, local(): xhigh = lax.ppermute(xlo, 'px', back)  8.43 us
    all_to_all x1, starting transfers between devices, local(): got = lax.all_to_all(send, GROUP, split_axis=0, concat_axis=0, tiled=True)  5.99 us
    ppermute x1, starting transfers between devices, local(): xlow = lax.ppermute(xhi, 'px', forth)  5.7 us
    ppermute x1, starting transfers between devices, local(): below = lax.ppermute(top, 'px', back)  3.78 us
    pallas_call x1, Pallas kernels, local(): pl.pallas_call(far_kernel, out_shape=(shape(3, FX, FY), vmem(3, 8, FY), v...  3.54 us
    ppermute x1, waiting for transfers between devices, local(): xlow = lax.ppermute(xhi, 'px', forth)  3.43 us
    ppermute x1, starting transfers between devices, local(): above = lax.ppermute(bottom, 'px', forth)  2.96 us
  transfers between devices with their start and end apart: 5, of which 3 were waited for; matrix products, arithmetic and copies ran while one was open for 0% of the time, Pallas kernels for 8%

profile of v6, /device:TPU:248, one launch (start us, length us, event | category | flops | bytes accessed | tf_op | source)
XLA Modules:
  0.0 60.0 jit_solution(7866411975818352527)
XLA Ops:
  0.6 1.5 %load.1 = (f32[3,8,48,256]{3,2,1,0:T(8,128)S(1)}, s32[4,128]{1,0:T(4,128)S(1)}, s32[4,128]{1,0:T(4,128)S(1)}, f32[64,256]{1,0:T(8,128)S(1)}, f32[2,64,256]{2,1,0...) custom-call(f32[3,8,48,256]{3,2,1,0:T(8,128)} %refs_0_.1, ...), custom_call_target="tpu_custom_call" | custom-call | bytes 3000000 | tf_op jit(solution)/shard_map/load/pallas_call | solution.py:393
  2.2 1.3 %pack.1 = f32[16,56,128]{2,1,0:T(8,128)} custom-call(f32[3,8,48,256]{3,2,1,0:T(8,128)S(1)} %get-tuple-element.20.near, s32[4,128]{1,0:T(4,128)S(1)} %get-tuple-element.25.owner, s32[4,128]{1,0:T(4,128)S(1)} %get-tuple-element.26.land, f32[64,256]{1,0:T(8,128)S(1)} %get-tuple-element.27.depth, f32[2,64,256]{2,1,0:T(8,128)S(1)} %get-tuple-element.28.flows, ...), custom_call_target="tpu_custom_call" | custom-call | bytes 6000000 | tf_op jit(solution)/shard_map/pack/pallas_call | solution.py:407
  3.5 6.0 %all-to-all-start = ((f32[16,56,128]{2,1,0:T(8,128)}), f32[16,56,128]{2,1,0:T(8,128)S(1)}, u32[]{:S(2)}, u32[]{:S(2)}) async-start(f32[16,56,128]{2,1,0:T(8,128)} %pack.1), calls=%async_computation | async-start | bytes 917504 | tf_op jit(solution)/shard_map/all_to_all | solution.py:416
  9.5 5.7 %collective-permute-start = (f32[3,48,256]{2,1,0:T(8,128)S(1)}, f32[3,48,256]{2,1,0:T(8,128)S(1)}, u32[]{:S(2)}, u32[]{:S(2)}) collective-permute-start(f32[3,48,256]{2,1,0:T(8,128)S(1)} %get-tuple-element.21), channel_id=1, source_target_pairs={{0,16},{16,32},{32,48},{48,64},{64,80},{80,96},{96,112},{112,128},... | collective-permute-start | bytes 442376 | tf_op jit(solution)/shard_map/ppermute | solution.py:405
  15.2 1.9 %collective-permute-start.1 = (f32[3,48,256]{2,1,0:T(8,128)S(1)}, f32[3,48,256]{2,1,0:T(8,128)S(1)}, u32[]{:S(2)}, u32[]{:S(2)}) collective-permute-start(f32[3,48,256]{2,1,0:T(8,128)S(1)} %get-tuple-element.22), channel_id=1, source_target_pairs={{16,0},{32,16},{48,32},{64,48},{80,64},{96,80},{112,96},{128,112},... | collective-permute-start | bytes 442376 | tf_op jit(solution)/shard_map/ppermute | solution.py:406
  17.1 3.4 %collective-permute-done.xlow = f32[3,48,256]{2,1,0:T(8,128)S(1)} collective-permute-done((f32[3,48,256]{2,1,0:T(8,128)S(1)}, f32[3,48,256]{2,1,0:T(8,128)S(1)}, u32[]{:S(2)}, u32[]{:S(2)}) %collective-permute-start) | collective-permute-done | bytes 147488 | tf_op jit(solution)/shard_map/ppermute | solution.py:405
  20.6 8.4 %collective-permute-done.1.xhigh = f32[3,48,256]{2,1,0:T(8,128)S(1)} collective-permute-done((f32[3,48,256]{2,1,0:T(8,128)S(1)}, f32[3,48,256]{2,1,0:T(8,128)S(1)}, u32[]{:S(2)}, u32[]{:S(2)}) %collective-permute-start.1) | collective-permute-done | bytes 147488 | tf_op jit(solution)/shard_map/ppermute | solution.py:406
  29.0 1.1 %inner.1 = (f32[3,8,48,256]{3,2,1,0:T(8,128)S(1)}, f32[8,48,128]{2,1,0:T(8,128)S(1)}) custom-call(f32[3,8,48,256]{3,2,1,0:T(8,128)S(1)} %get-tuple-element.20.near, f32[3,48,256]{2,1,0:T(8,128)S(1)} %collective-permute-done.xlow, f32[3,48,256]{2,1,0:T(8,128)S(1)} %collective-permute-done.1.xhigh), custom_call_target="tpu_custom_call" | custom-call | bytes 6000000 | tf_op jit(solution)/shard_map/inner/pallas_call | solution.py:417
  30.1 0.0 all-to-all-done.got
  30.1 1.3 %near.1 = (f32[8,48,256]{2,1,0:T(8,128)}, f32[16,48,128]{2,1,0:T(8,128)S(1)}) custom-call(f32[3,8,48,256]{3,2,1,0:T(8,128)S(1)} %get-tuple-element.23.mid, f32[8,48,128]{2,1,0:T(8,128)S(1)} %get-tuple-element.24.vely, f32[16,56,128]{2,1,0:T(8,128)S(1)} %all-to-all-done.got), custom_call_target="tpu_custom_call" | custom-call | bytes 6000000 | tf_op jit(solution)/shard_map/near/pallas_call | solution.py:426
  31.4 14.0 %all_to_all.10.sums = f32[16,48,128]{2,1,0:T(8,128)S(1)} all-to-all(f32[16,48,128]{2,1,0:T(8,128)S(1)} %get-tuple-element.31), channel_id=1, replica_groups=mesh['px'=48,'py'=4,'dz'=4] {'py','dz'}, dimensions={0} | all-to-all | bytes 786432 | tf_op jit(solution)/shard_map/all_to_all | solution.py:435
  45.4 1.2 %edge.1 = (f32[2,4,48,128]{3,2,1,0:T(8,128)S(1)}, f32[8,256]{1,0:T(8,128)S(1)}, f32[8,256]{1,0:T(8,128)S(1)}) custom-call(f32[16,56,128]{2,1,0:T(8,128)S(1)} %all-to-all-done.got, f32[16,48,128]{2,1,0:T(8,128)S(1)} %all_to_all.10.sums, f32[64,256]{1,0:T(8,128)S(1)} %get-tuple-element.27.depth, f32[2,64,256]{2,1,0:T(8,128)S(1)} %get-tuple-element.28.flows, ...), custom_call_target="tpu_custom_call" | custom-call | bytes 6000000 | tf_op jit(solution)/shard_map/edge/pallas_call | solution.py:436
  46.6 3.0 %collective-permute-start.2 = (f32[8,256]{1,0:T(8,128)S(1)}, f32[8,256]{1,0:T(8,128)S(1)}, u32[]{:S(2)}, u32[]{:S(2)}) collective-permute-start(f32[8,256]{1,0:T(8,128)S(1)} %get-tuple-element.36), channel_id=1, source_target_pairs={{0,16},{16,32},{32,48},{48,64},{64,80},{80,96},{96,112},{112,128},... | collective-permute-start | bytes 24584 | tf_op jit(solution)/shard_map/ppermute | solution.py:446
  49.6 3.8 %collective-permute-start.3 = (f32[8,256]{1,0:T(8,128)S(1)}, f32[8,256]{1,0:T(8,128)S(1)}, u32[]{:S(2)}, u32[]{:S(2)}) collective-permute-start(f32[8,256]{1,0:T(8,128)S(1)} %get-tuple-element.37), channel_id=1, source_target_pairs={{16,0},{32,16},{48,32},{64,48},{80,64},{96,80},{112,96},{128,112},... | collective-permute-start | bytes 24584 | tf_op jit(solution)/shard_map/ppermute | solution.py:447
  53.4 3.5 %far.1 = (f32[3,64,256]{2,1,0:T(8,128)}, f32[3,8,256]{2,1,0:T(8,128)S(1)}, f32[3,8,256]{2,1,0:T(8,128)S(1)}) custom-call(f32[16,56,128]{2,1,0:T(8,128)S(1)} %all-to-all-done.got, f32[2,4,48,128]{3,2,1,0:T(8,128)S(1)} %get-tuple-element.32.pieces, f32[64,256]{1,0:T(8,128)S(1)} %get-tuple-element.27.depth, f32[2,64,256]{2,1,0:T(8,128)S(1)} %get-tuple-element.28.flows, ...), custom_call_target="tpu_custom_call" | custom-call | bytes 15000000 | tf_op jit(solution)/shard_map/far/pallas_call | solution.py:448
  56.9 0.0 collective-permute-done.2.above
  56.9 2.4 %collective-permute-done.3.below = f32[8,256]{1,0:T(8,128)S(1)} collective-permute-done((f32[8,256]{1,0:T(8,128)S(1)}, f32[8,256]{1,0:T(8,128)S(1)}, u32[]{:S(2)}, u32[]{:S(2)}) %collective-permute-start.3) | collective-permute-done | bytes 8224 | tf_op jit(solution)/shard_map/ppermute | solution.py:447
  59.4 0.7 %join.1 = f32[3,64,256]{2,1,0:T(8,128)} custom-call(f32[3,64,256]{2,1,0:T(8,128)} %get-tuple-element.33.part, f32[3,8,256]{2,1,0:T(8,128)S(1)} %get-tuple-element.34.head, f32[3,8,256]{2,1,0:T(8,128)S(1)} %get-tuple-element.35.tail, f32[8,256]{1,0:T(8,128)S(1)} %collective-permute-done.2.above, ...), custom_call_target="tpu_custom_call", output_to_operand_aliasing={{}: (0, {})} | custom-call | bytes 3000000 | tf_op jit(solution)/shard_map/join/pallas_call | solution.py:458
Async XLA Ops:
  3.5 26.6 %all-to-all-start = ((f32[16,56,128]{2,1,0:T(8,128)}), f32[16,56,128]{2,1,0:T(8,128)S(1)}, u32[]{:S(2)}, u32[]{:S(2)}) async-start(f32[16,56,128]{2,1,0:T(8,128)} %pack.1), calls=%async_computation | async-start | bytes 917504 | tf_op jit(solution)/shard_map/all_to_all | solution.py:416
  9.5 11.1 %collective-permute-start = (f32[3,48,256]{2,1,0:T(8,128)S(1)}, f32[3,48,256]{2,1,0:T(8,128)S(1)}, u32[]{:S(2)}, u32[]{:S(2)}) collective-permute-start(f32[3,48,256]{2,1,0:T(8,128)S(1)} %get-tuple-element.21), channel_id=1, source_target_pairs={{0,16},{16,32},{32,48},{48,64},{64,80},{80,96},{96,112},{112,128},... | collective-permute-start | bytes 442376 | tf_op jit(solution)/shard_map/ppermute | solution.py:405
  15.2 13.8 %collective-permute-start.1 = (f32[3,48,256]{2,1,0:T(8,128)S(1)}, f32[3,48,256]{2,1,0:T(8,128)S(1)}, u32[]{:S(2)}, u32[]{:S(2)}) collective-permute-start(f32[3,48,256]{2,1,0:T(8,128)S(1)} %get-tuple-element.22), channel_id=1, source_target_pairs={{16,0},{32,16},{48,32},{64,48},{80,64},{96,80},{112,96},{128,112},... | collective-permute-start | bytes 442376 | tf_op jit(solution)/shard_map/ppermute | solution.py:406
  46.6 10.3 %collective-permute-start.2 = (f32[8,256]{1,0:T(8,128)S(1)}, f32[8,256]{1,0:T(8,128)S(1)}, u32[]{:S(2)}, u32[]{:S(2)}) collective-permute-start(f32[8,256]{1,0:T(8,128)S(1)} %get-tuple-element.36), channel_id=1, source_target_pairs={{0,16},{16,32},{32,48},{48,64},{64,80},{80,96},{96,112},{112,128},... | collective-permute-start | bytes 24584 | tf_op jit(solution)/shard_map/ppermute | solution.py:446
  49.6 9.8 %collective-permute-start.3 = (f32[8,256]{1,0:T(8,128)S(1)}, f32[8,256]{1,0:T(8,128)S(1)}, u32[]{:S(2)}, u32[]{:S(2)}) collective-permute-start(f32[8,256]{1,0:T(8,128)S(1)} %get-tuple-element.37), channel_id=1, source_target_pairs={{16,0},{32,16},{48,32},{64,48},{80,64},{96,80},{112,96},{128,112},... | collective-permute-start | bytes 24584 | tf_op jit(solution)/shard_map/ppermute | solution.py:447

commit v7 on v6

--- a/solution.py
+++ b/solution.py
@@ -42,9 +42,20 @@
     return 2 * row if row < 4 else 2 * (row - 4) + 1
 
 
+def odd_px():
+    return lax.rem(lax.axis_index("px"), 2) == 1
+
+
+def swaps(count, first):
+    low = range(first, count - 1, 2)
+    return [(i, i + 1) for i in low] + [(i + 1, i) for i in low]
+
+
 def load_kernel(*refs):
-    sources, copies, (xlo, xhi), sem = refs[:6], refs[6:12], refs[12:14], refs[14]
-    moves = [(sources[0].at[:, 0], xlo), (sources[0].at[:, CX - 1], xhi), *zip(sources, copies)]
+    sources, copies, (first, second), sem = refs[:6], refs[6:12], refs[12:14], refs[14]
+    up = jnp.where(odd_px(), CX - 1, 0)
+    near = sources[0]
+    moves = [(near.at[:, up], first), (near.at[:, CX - 1 - up], second), *zip(sources, copies)]
     moves = [pltpu.make_async_copy(a, b, sem.at[n]) for n, (a, b) in enumerate(moves)]
     for move in moves:
         move.start()
@@ -116,7 +127,8 @@
         yface(me + NDZ, CY - 1)
 
 
-def inner_kernel(near, xlow, xhigh, mid, vely):
+def inner_kernel(near, first, second, mid, vely):
+    odd = odd_px()
     lane = lane_iota((CZ, CY))
     row = lax.broadcasted_iota(jnp.int32, (CZ, CY), 0)
     for x in range(CX):
@@ -125,8 +137,8 @@
         vely[x] = jnp.where(lane[:, 0:128] == 127, velv[:, 128:], velv[:, 0:128])
         for f in range(3):
             q = near[f, x]
-            xp = near[f, x + 1] if x < CX - 1 else xhigh[f]
-            xm = near[f, x - 1] if x > 0 else xlow[f]
+            xp = near[f, x + 1] if x < CX - 1 else jnp.where(odd, first[f], second[f])
+            xm = near[f, x - 1] if x > 0 else jnp.where(odd, second[f], first[f])
             yp = jnp.where(lane == CY - 1, 0.0, pltpu.roll(q, CY - 1, 1))
             ym = jnp.where(lane == 0, 0.0, pltpu.roll(q, 1, 1))
             zp = jnp.where(row == CZ - 1, 0.0, pltpu.roll(q, CZ - 1, 0))
@@ -216,7 +228,7 @@
         yield [jnp.concatenate(two, axis=1) for two in zip(build(p), build(p + 1))]
 
 
-def edge_kernel(scale, got, sums, depth, flows, mask, pieces, top, bottom, wide):
+def edge_kernel(scale, got, sums, depth, flows, mask, pieces, send1, send2, wide):
     me = lax.axis_index("py") * NDZ + lax.axis_index("dz")
     ycell = cell_rows(FY)
     one = jnp.ones((FY, 128), jnp.bfloat16)
@@ -251,13 +263,17 @@
                 acc = acc + lax.dot_general(lhs, bits, OVER, preferred_element_type=f32)
     acc = acc[0:8] + acc[8:16]
     blank = jnp.zeros((5, FY), f32)
-    for e, out in ((0, top), (1, bottom)):
+    ends = []
+    for e in range(2):
         at = 0 if e == 0 else FX - 1
         wet = mask[at : at + 1].astype(f32)
         h = depth[at : at + 1] + acc[e * 3 : e * 3 + 1]
         hu = (flows[0, at : at + 1] + acc[e * 3 + 1 : e * 3 + 2]) * wet
         hv = (flows[1, at : at + 1] + acc[e * 3 + 2 : e * 3 + 3]) * wet
-        out[...] = jnp.concatenate([h, hu, hv, blank], axis=0)
+        ends.append(jnp.concatenate([h, hu, hv, blank], axis=0))
+    odd = odd_px()
+    send1[...] = jnp.where(odd, ends[1], ends[0])
+    send2[...] = jnp.where(odd, ends[0], ends[1])
 
 
 def terms(h, hu, hv, ok):
@@ -355,8 +371,11 @@
         tail[f] = new[FX - 8 : FX]
 
 
-def join_kernel(part, head, tail, above, below, out, new, sem):
+def join_kernel(part, head, tail, got1, got2, out, new, sem):
     px = lax.axis_index("px")
+    odd = odd_px()
+    above = jnp.where(odd, got2[...], got1[...])
+    below = jnp.where(odd, got1[...], got2[...])
     up = terms(above[0:1], above[1:2], above[2:3], px > 0)
     dn = terms(below[0:1], below[1:2], below[2:3], px < lax.axis_size("px") - 1)
     row = lax.broadcasted_iota(jnp.int32, (8, FY), 0)
@@ -385,12 +404,10 @@
 
 def local(near_state, column_owner, landing, far_depth, far_flows, wet_mask):
     n_px = lax.axis_size("px")
-    forth = [(i, i + 1) for i in range(n_px - 1)]
-    back = [(i + 1, i) for i in range(n_px - 1)]
     owner = column_owner.reshape(4, 128)
     land = landing.reshape(4, 128)
     given = (near_state, owner, land, far_depth, far_flows, wet_mask)
-    *given, xlo, xhi = pl.pallas_call(
+    *given, face1, face2 = pl.pallas_call(
         load_kernel,
         out_shape=[pltpu.VMEM(x.shape, x.dtype) for x in given]
         + [vmem(3, CZ, CY)] * 2,
@@ -402,8 +419,8 @@
         name="load",
     )(*[pltpu.with_memory_space_constraint(x, pltpu.HBM) for x in given])
     near_state, owner, land, far_depth, far_flows, wet_mask = given
-    xlow = lax.ppermute(xhi, "px", forth)
-    xhigh = lax.ppermute(xlo, "px", back)
+    face1 = lax.ppermute(face1, "px", swaps(n_px, 1))
+    face2 = lax.ppermute(face2, "px", swaps(n_px, 0))
     send = pl.pallas_call(
         pack_kernel,
         out_shape=shape(GRP, BLK, 128),
@@ -422,7 +439,7 @@
         compiler_params=PARAMS,
         cost_estimate=cost(2),
         name="inner",
-    )(near_state, xlow, xhigh)
+    )(near_state, face1, face2)
     new_frac, sums = pl.pallas_call(
         near_kernel,
         out_shape=(shape(CX, CZ, CY), shape(GRP, ROWS, 128)),
@@ -433,7 +450,7 @@
         name="near",
     )(mid, vely, got)
     sums = lax.all_to_all(sums, GROUP, split_axis=0, concat_axis=0, tiled=True)
-    pieces, top, bottom = pl.pallas_call(
+    pieces, end1, end2 = pl.pallas_call(
         functools.partial(edge_kernel, column_height / (CZ * NDZ)),
         out_shape=(vmem(2, NPY, ROWS, 128), vmem(8, FY), vmem(8, FY)),
         in_specs=[VM] * 5,
@@ -443,8 +460,8 @@
         cost_estimate=cost(2),
         name="edge",
     )(got, sums, far_depth, far_flows, wet_mask)
-    above = lax.ppermute(bottom, "px", forth)
-    below = lax.ppermute(top, "px", back)
+    end1 = lax.ppermute(end1, "px", swaps(n_px, 1))
+    end2 = lax.ppermute(end2, "px", swaps(n_px, 0))
     part, head, tail = pl.pallas_call(
         far_kernel,
         out_shape=(shape(3, FX, FY), vmem(3, 8, FY), vmem(3, 8, FY)),
@@ -465,7 +482,7 @@
         compiler_params=PARAMS,
         cost_estimate=cost(1),
         name="join",
-    )(part, head, tail, above, below)
+    )(part, head, tail, end1, end2)
     return (new_frac, far_new)
 
 

time: 60.4 us -> 56.8 us (0.940)
  the two profiles are of different devices: /device:TPU:248 before, /device:TPU:512 now
where the time goes in v7:
time: 56.8 us; the launch traced here: 56.5 us
  starting transfers between devices  21.5 us (38%)
  blocking collectives  13.7 us (24%)
  Pallas kernels  10.6 us (19%)
  waiting for transfers between devices  10 us (18%)
  between operations  0.71 us (1%)
    all_to_all x1, blocking collectives, local(): sums = lax.all_to_all(sums, GROUP, split_axis=0, concat_axis=0, tiled=True)  13.7 us
    ppermute x1, starting transfers between devices, local(): face1 = lax.ppermute(face1, 'px', swaps(n_px, 1))  6.46 us
    ppermute x1, waiting for transfers between devices, local(): face1 = lax.ppermute(face1, 'px', swaps(n_px, 1))  6.2 us
    all_to_all x1, starting transfers between devices, local(): got = lax.all_to_all(send, GROUP, split_axis=0, concat_axis=0, tiled=True)  5.74 us
    ppermute x1, starting transfers between devices, local(): end1 = lax.ppermute(end1, 'px', swaps(n_px, 1))  4.5 us
    pallas_call x1, Pallas kernels, local(): pl.pallas_call(far_kernel, out_shape=(shape(3, FX, FY), vmem(3, 8, FY), v...  3.54 us
    ppermute x1, starting transfers between devices, local(): face2 = lax.ppermute(face2, 'px', swaps(n_px, 0))  2.84 us
    ppermute x1, waiting for transfers between devices, local(): face2 = lax.ppermute(face2, 'px', swaps(n_px, 0))  2.83 us
  transfers between devices with their start and end apart: 5, of which 3 were waited for; matrix products, arithmetic and copies ran while one was open for 0% of the time, Pallas kernels for 8%

profile of v7, /device:TPU:512, one launch (start us, length us, event | category | flops | bytes accessed | tf_op | source)
XLA Modules:
  0.0 56.5 jit_solution(2564410141380862022)
XLA Ops:
  0.6 1.6 %load.1 = (f32[3,8,48,256]{3,2,1,0:T(8,128)S(1)}, s32[4,128]{1,0:T(4,128)S(1)}, s32[4,128]{1,0:T(4,128)S(1)}, f32[64,256]{1,0:T(8,128)S(1)}, f32[2,64,256]{2,1,0...) custom-call(f32[3,8,48,256]{3,2,1,0:T(8,128)} %refs_0_.1, ...), custom_call_target="tpu_custom_call" | custom-call | bytes 3000000 | tf_op jit(solution)/shard_map/load/pallas_call | solution.py:410
  2.2 1.2 %pack.1 = f32[16,56,128]{2,1,0:T(8,128)} custom-call(f32[3,8,48,256]{3,2,1,0:T(8,128)S(1)} %get-tuple-element.20.near, s32[4,128]{1,0:T(4,128)S(1)} %get-tuple-element.25.owner, s32[4,128]{1,0:T(4,128)S(1)} %get-tuple-element.26.land, f32[64,256]{1,0:T(8,128)S(1)} %get-tuple-element.27.depth, f32[2,64,256]{2,1,0:T(8,128)S(1)} %get-tuple-element.28.flows, ...), custom_call_target="tpu_custom_call" | custom-call | bytes 6000000 | tf_op jit(solution)/shard_map/pack/pallas_call | solution.py:424
  3.4 5.7 %all-to-all-start = ((f32[16,56,128]{2,1,0:T(8,128)}), f32[16,56,128]{2,1,0:T(8,128)S(1)}, u32[]{:S(2)}, u32[]{:S(2)}) async-start(f32[16,56,128]{2,1,0:T(8,128)} %pack.1), calls=%async_computation | async-start | bytes 917504 | tf_op jit(solution)/shard_map/all_to_all | solution.py:433
  9.2 6.5 %collective-permute-start = (f32[3,48,256]{2,1,0:T(8,128)S(1)}, f32[3,48,256]{2,1,0:T(8,128)S(1)}, u32[]{:S(2)}, u32[]{:S(2)}) collective-permute-start(f32[3,48,256]{2,1,0:T(8,128)S(1)} %get-tuple-element.21), channel_id=1, source_target_pairs={{16,32},{48,64},{80,96},{112,128},{144,160},{176,192},{208,224},{2... | collective-permute-start | bytes 442376 | tf_op jit(solution)/shard_map/ppermute | solution.py:422
  15.7 2.8 %collective-permute-start.1 = (f32[3,48,256]{2,1,0:T(8,128)S(1)}, f32[3,48,256]{2,1,0:T(8,128)S(1)}, u32[]{:S(2)}, u32[]{:S(2)}) collective-permute-start(f32[3,48,256]{2,1,0:T(8,128)S(1)} %get-tuple-element.22), channel_id=1, source_target_pairs={{0,16},{32,48},{64,80},{96,112},{128,144},{160,176},{192,208},{224... | collective-permute-start | bytes 442376 | tf_op jit(solution)/shard_map/ppermute | solution.py:423
  18.5 6.2 %collective-permute-done.first = f32[3,48,256]{2,1,0:T(8,128)S(1)} collective-permute-done((f32[3,48,256]{2,1,0:T(8,128)S(1)}, f32[3,48,256]{2,1,0:T(8,128)S(1)}, u32[]{:S(2)}, u32[]{:S(2)}) %collective-permute-start) | collective-permute-done | bytes 147488 | tf_op jit(solution)/shard_map/ppermute | solution.py:422
  24.7 2.8 %collective-permute-done.1.second = f32[3,48,256]{2,1,0:T(8,128)S(1)} collective-permute-done((f32[3,48,256]{2,1,0:T(8,128)S(1)}, f32[3,48,256]{2,1,0:T(8,128)S(1)}, u32[]{:S(2)}, u32[]{:S(2)}) %collective-permute-start.1) | collective-permute-done | bytes 147488 | tf_op jit(solution)/shard_map/ppermute | solution.py:423
  27.5 1.1 %inner.1 = (f32[3,8,48,256]{3,2,1,0:T(8,128)S(1)}, f32[8,48,128]{2,1,0:T(8,128)S(1)}) custom-call(f32[3,8,48,256]{3,2,1,0:T(8,128)S(1)} %get-tuple-element.20.near, f32[3,48,256]{2,1,0:T(8,128)S(1)} %collective-permute-done.first, f32[3,48,256]{2,1,0:T(8,128)S(1)} %collective-permute-done.1.second), custom_call_target="tpu_custom_call" | custom-call | bytes 6000000 | tf_op jit(solution)/shard_map/inner/pallas_call | solution.py:434
  28.6 0.0 all-to-all-done.got
  28.6 1.3 %near.1 = (f32[8,48,256]{2,1,0:T(8,128)}, f32[16,48,128]{2,1,0:T(8,128)S(1)}) custom-call(f32[3,8,48,256]{3,2,1,0:T(8,128)S(1)} %get-tuple-element.23.mid, f32[8,48,128]{2,1,0:T(8,128)S(1)} %get-tuple-element.24.vely, f32[16,56,128]{2,1,0:T(8,128)S(1)} %all-to-all-done.got), custom_call_target="tpu_custom_call" | custom-call | bytes 6000000 | tf_op jit(solution)/shard_map/near/pallas_call | solution.py:443
  30.0 13.7 %all_to_all.10.sums = f32[16,48,128]{2,1,0:T(8,128)S(1)} all-to-all(f32[16,48,128]{2,1,0:T(8,128)S(1)} %get-tuple-element.31), channel_id=1, replica_groups=mesh['px'=48,'py'=4,'dz'=4] {'py','dz'}, dimensions={0} | all-to-all | bytes 786432 | tf_op jit(solution)/shard_map/all_to_all | solution.py:452
  43.6 1.2 %edge.1 = (f32[2,4,48,128]{3,2,1,0:T(8,128)S(1)}, f32[8,256]{1,0:T(8,128)S(1)}, f32[8,256]{1,0:T(8,128)S(1)}) custom-call(f32[16,56,128]{2,1,0:T(8,128)S(1)} %all-to-all-done.got, f32[16,48,128]{2,1,0:T(8,128)S(1)} %all_to_all.10.sums, f32[64,256]{1,0:T(8,128)S(1)} %get-tuple-element.27.depth, f32[2,64,256]{2,1,0:T(8,128)S(1)} %get-tuple-element.28.flows, ...), custom_call_target="tpu_custom_call" | custom-call | bytes 6000000 | tf_op jit(solution)/shard_map/edge/pallas_call | solution.py:453
  44.9 4.5 %collective-permute-start.2 = (f32[8,256]{1,0:T(8,128)S(1)}, f32[8,256]{1,0:T(8,128)S(1)}, u32[]{:S(2)}, u32[]{:S(2)}) collective-permute-start(f32[8,256]{1,0:T(8,128)S(1)} %get-tuple-element.36), channel_id=1, source_target_pairs={{16,32},{48,64},{80,96},{112,128},{144,160},{176,192},{208,224},{2... | collective-permute-start | bytes 24584 | tf_op jit(solution)/shard_map/ppermute | solution.py:463
  49.4 1.9 %collective-permute-start.3 = (f32[8,256]{1,0:T(8,128)S(1)}, f32[8,256]{1,0:T(8,128)S(1)}, u32[]{:S(2)}, u32[]{:S(2)}) collective-permute-start(f32[8,256]{1,0:T(8,128)S(1)} %get-tuple-element.37), channel_id=1, source_target_pairs={{0,16},{32,48},{64,80},{96,112},{128,144},{160,176},{192,208},{224... | collective-permute-start | bytes 24584 | tf_op jit(solution)/shard_map/ppermute | solution.py:464
  51.3 3.5 %far.1 = (f32[3,64,256]{2,1,0:T(8,128)}, f32[3,8,256]{2,1,0:T(8,128)S(1)}, f32[3,8,256]{2,1,0:T(8,128)S(1)}) custom-call(f32[16,56,128]{2,1,0:T(8,128)S(1)} %all-to-all-done.got, f32[2,4,48,128]{3,2,1,0:T(8,128)S(1)} %get-tuple-element.32.pieces, f32[64,256]{1,0:T(8,128)S(1)} %get-tuple-element.27.depth, f32[2,64,256]{2,1,0:T(8,128)S(1)} %get-tuple-element.28.flows, ...), custom_call_target="tpu_custom_call" | custom-call | bytes 15000000 | tf_op jit(solution)/shard_map/far/pallas_call | solution.py:465
  54.8 0.0 collective-permute-done.2.got1
  54.8 1.0 %collective-permute-done.3.got2 = f32[8,256]{1,0:T(8,128)S(1)} collective-permute-done((f32[8,256]{1,0:T(8,128)S(1)}, f32[8,256]{1,0:T(8,128)S(1)}, u32[]{:S(2)}, u32[]{:S(2)}) %collective-permute-start.3) | collective-permute-done | bytes 8224 | tf_op jit(solution)/shard_map/ppermute | solution.py:464
  55.8 0.7 %join.1 = f32[3,64,256]{2,1,0:T(8,128)} custom-call(f32[3,64,256]{2,1,0:T(8,128)} %get-tuple-element.33.part, f32[3,8,256]{2,1,0:T(8,128)S(1)} %get-tuple-element.34.head, f32[3,8,256]{2,1,0:T(8,128)S(1)} %get-tuple-element.35.tail, f32[8,256]{1,0:T(8,128)S(1)} %collective-permute-done.2.got1, ...), custom_call_target="tpu_custom_call", output_to_operand_aliasing={{}: (0, {})} | custom-call | bytes 3000000 | tf_op jit(solution)/shard_map/join/pallas_call | solution.py:475
Async XLA Ops:
  3.4 25.2 %all-to-all-start = ((f32[16,56,128]{2,1,0:T(8,128)}), f32[16,56,128]{2,1,0:T(8,128)S(1)}, u32[]{:S(2)}, u32[]{:S(2)}) async-start(f32[16,56,128]{2,1,0:T(8,128)} %pack.1), calls=%async_computation | async-start | bytes 917504 | tf_op jit(solution)/shard_map/all_to_all | solution.py:433
  9.2 15.5 %collective-permute-start = (f32[3,48,256]{2,1,0:T(8,128)S(1)}, f32[3,48,256]{2,1,0:T(8,128)S(1)}, u32[]{:S(2)}, u32[]{:S(2)}) collective-permute-start(f32[3,48,256]{2,1,0:T(8,128)S(1)} %get-tuple-element.21), channel_id=1, source_target_pairs={{16,32},{48,64},{80,96},{112,128},{144,160},{176,192},{208,224},{2... | collective-permute-start | bytes 442376 | tf_op jit(solution)/shard_map/ppermute | solution.py:422
  15.7 11.9 %collective-permute-start.1 = (f32[3,48,256]{2,1,0:T(8,128)S(1)}, f32[3,48,256]{2,1,0:T(8,128)S(1)}, u32[]{:S(2)}, u32[]{:S(2)}) collective-permute-start(f32[3,48,256]{2,1,0:T(8,128)S(1)} %get-tuple-element.22), channel_id=1, source_target_pairs={{0,16},{32,48},{64,80},{96,112},{128,144},{160,176},{192,208},{224... | collective-permute-start | bytes 442376 | tf_op jit(solution)/shard_map/ppermute | solution.py:423
  44.9 10.0 %collective-permute-start.2 = (f32[8,256]{1,0:T(8,128)S(1)}, f32[8,256]{1,0:T(8,128)S(1)}, u32[]{:S(2)}, u32[]{:S(2)}) collective-permute-start(f32[8,256]{1,0:T(8,128)S(1)} %get-tuple-element.36), channel_id=1, source_target_pairs={{16,32},{48,64},{80,96},{112,128},{144,160},{176,192},{208,224},{2... | collective-permute-start | bytes 24584 | tf_op jit(solution)/shard_map/ppermute | solution.py:463
  49.4 6.4 %collective-permute-start.3 = (f32[8,256]{1,0:T(8,128)S(1)}, f32[8,256]{1,0:T(8,128)S(1)}, u32[]{:S(2)}, u32[]{:S(2)}) collective-permute-start(f32[8,256]{1,0:T(8,128)S(1)} %get-tuple-element.37), channel_id=1, source_target_pairs={{0,16},{32,48},{64,80},{96,112},{128,144},{160,176},{192,208},{224... | collective-permute-start | bytes 24584 | tf_op jit(solution)/shard_map/ppermute | solution.py:464

commit v8 on v7

--- a/solution.py
+++ b/solution.py
@@ -295,7 +295,7 @@
 
 
 def far_kernel(
-    got, pieces, depth, flows, mask, out, head, tail, wide
+    got, pieces, depth, flows, mask, out, wide
 ):
     me = lax.axis_index("py") * NDZ + lax.axis_index("dz")
     xcell = cell_rows(FX)
@@ -335,8 +335,21 @@
                 side = side + lax.dot_general(side_lhs, xbits, OVER, preferred_element_type=f32)
     source = acc[0 : 3 * FX] + acc[3 * FX :]
     side = side[0:8] + side[8:16]
-    side = jnp.concatenate([side] * 16, axis=0)
-    side = jnp.concatenate([side, side], axis=1).T
+    side = jnp.concatenate([side, side], axis=1)
+    sides = []
+    for n in range(2):
+        other = jnp.maximum(me - 1, 0) if n == 0 else jnp.minimum(me + 1, GRP - 1)
+        e = got[other, ROWS:BLK]
+        e = jnp.where((other % 2) == 1, e, pltpu.roll(e, 64, 1))
+        inside = (me > 0) if n == 0 else (me < GRP - 1)
+        s = []
+        for f in range(3):
+            v = e[f : f + 1] + side[n * 3 + f : n * 3 + f + 1]
+            v = v if f == 0 else v * e[3:4]
+            s.append(jnp.where(inside, v, 0.0))
+        sides += [t[3 - n] for t in terms(*s, inside)]
+    sides = jnp.concatenate(sides + [jnp.zeros((2, 128), f32)], axis=0)
+    sides = jnp.concatenate([sides] * 16, axis=0).T[0:FX]
     wet = mask[...].astype(f32)
     raw = (depth[...], flows[0], flows[1])
     cells = []
@@ -344,34 +357,20 @@
         s = raw[f] + source[f * FX : (f + 1) * FX]
         cells.append(s if f == 0 else s * wet)
     body = terms(*cells, True)
-    sides = []
-    for n in range(2):
-        other = jnp.maximum(me - 1, 0) if n == 0 else jnp.minimum(me + 1, GRP - 1)
-        block = got[other, ROWS:BLK]
-        block = jnp.where((other % 2) == 1, block, pltpu.roll(block, 64, 1))
-        e = jnp.concatenate([block] * 16, axis=0).T[0:FX]
-        inside = (me > 0) if n == 0 else (me < GRP - 1)
-        s = []
-        for f in range(3):
-            col = n * 3 + f
-            v = e[:, f : f + 1] + side[0:FX, col : col + 1]
-            v = v if f == 0 else v * e[:, 3:4]
-            s.append(jnp.where(inside, v, 0.0))
-        sides.append(terms(*s, inside))
     lane = lane_iota((FX, FY))
     row = lax.broadcasted_iota(jnp.int32, (FX, FY), 0)
     for f in range(3):
         xp = jnp.where(row == FX - 1, 0.0, pltpu.roll(body[f][0], FX - 1, 0))
         xm = jnp.where(row == 0, 0.0, pltpu.roll(body[f][1], 1, 0))
-        yp = jnp.where(lane == FY - 1, sides[1][f][2], pltpu.roll(body[f][2], FY - 1, 1))
-        ym = jnp.where(lane == 0, sides[0][f][3], pltpu.roll(body[f][3], 1, 1))
+        yp = jnp.where(lane == FY - 1, sides[:, 3 + f : 4 + f], pltpu.roll(body[f][2], FY - 1, 1))
+        ym = jnp.where(lane == 0, sides[:, f : f + 1], pltpu.roll(body[f][3], 1, 1))
         new = (xp + xm) + (yp + ym)
         out[f] = new
-        head[f] = new[0:8]
-        tail[f] = new[FX - 8 : FX]
-
-
-def join_kernel(part, head, tail, got1, got2, out, new, sem):
+
+
+def join_kernel(part, got1, got2, out, new, sem):
+    inner = pltpu.make_async_copy(part.at[:, 8 : FX - 8], out.at[:, 8 : FX - 8], sem.at[2])
+    inner.start()
     px = lax.axis_index("px")
     odd = odd_px()
     above = jnp.where(odd, got2[...], got1[...])
@@ -380,14 +379,15 @@
     dn = terms(below[0:1], below[1:2], below[2:3], px < lax.axis_size("px") - 1)
     row = lax.broadcasted_iota(jnp.int32, (8, FY), 0)
     for f in range(3):
-        new[0, f] = head[f] + jnp.where(row == 0, up[f][1], 0.0)
-        new[1, f] = tail[f] + jnp.where(row == 7, dn[f][0], 0.0)
+        new[0, f] = part[f, 0:8] + jnp.where(row == 0, up[f][1], 0.0)
+        new[1, f] = part[f, FX - 8 : FX] + jnp.where(row == 7, dn[f][0], 0.0)
     first = pltpu.make_async_copy(new.at[0], out.at[:, 0:8], sem.at[0])
     last = pltpu.make_async_copy(new.at[1], out.at[:, FX - 8 : FX], sem.at[1])
     first.start()
     last.start()
     first.wait()
     last.wait()
+    inner.wait()
 
 
 def shape(*dims):
@@ -462,11 +462,11 @@
     )(got, sums, far_depth, far_flows, wet_mask)
     end1 = lax.ppermute(end1, "px", swaps(n_px, 1))
     end2 = lax.ppermute(end2, "px", swaps(n_px, 0))
-    part, head, tail = pl.pallas_call(
+    part = pl.pallas_call(
         far_kernel,
-        out_shape=(shape(3, FX, FY), vmem(3, 8, FY), vmem(3, 8, FY)),
+        out_shape=vmem(3, FX, FY),
         in_specs=[VM] * 5,
-        out_specs=(VM,) * 3,
+        out_specs=VM,
         scratch_shapes=[vmem(8, 128, 128)],
         compiler_params=pltpu.CompilerParams(vmem_limit_bytes=20 << 20),
         cost_estimate=cost(5),
@@ -475,14 +475,13 @@
     far_new = pl.pallas_call(
         join_kernel,
         out_shape=shape(3, FX, FY),
-        in_specs=[ANY] + [VM] * 4,
+        in_specs=[VM] * 3,
         out_specs=ANY,
-        scratch_shapes=[pltpu.VMEM((2, 3, 8, FY), f32), pltpu.SemaphoreType.DMA((2,))],
-        input_output_aliases={0: 0},
+        scratch_shapes=[pltpu.VMEM((2, 3, 8, FY), f32), pltpu.SemaphoreType.DMA((3,))],
         compiler_params=PARAMS,
         cost_estimate=cost(1),
         name="join",
-    )(part, head, tail, end1, end2)
+    )(part, end1, end2)
     return (new_frac, far_new)
 
 

time: 56.8 us -> 56.9 us (level)
  waiting for transfers between devices: 10 us -> 10.9 us
  Pallas kernels: 10.6 us -> 9.79 us
    pallas_call x2, Pallas kernels: 4.2 us -> 3.37 us  [the longest x1 2.68 us: local(): pl.pallas_call(far_kernel, out_shape=vmem(3, FX, FY), in_specs=[VM] * 5,...]
    ppermute x1, waiting for transfers between devices: 0.01 us -> 0.64 us  [local(): end1 = lax.ppermute(end1, 'px', swaps(n_px, 1))]
  transfers between devices with their start and end apart: 5 -> 5, of which waited for: 3 -> 4; matrix products, arithmetic and copies ran while one was open for 0% -> 0% of each run, Pallas kernels for 8% -> 7%
where the time goes in v8:
time: 56.9 us; the launch traced here: 56.5 us
  starting transfers between devices  21.5 us (38%)
  blocking collectives  13.7 us (24%)
  waiting for transfers between devices  10.9 us (19%)
  Pallas kernels  9.79 us (17%)
  between operations  0.71 us (1%)
    all_to_all x1, blocking collectives, local(): sums = lax.all_to_all(sums, GROUP, split_axis=0, concat_axis=0, tiled=True)  13.7 us
    ppermute x1, starting transfers between devices, local(): face1 = lax.ppermute(face1, 'px', swaps(n_px, 1))  6.46 us
    ppermute x1, waiting for transfers between devices, local(): face1 = lax.ppermute(face1, 'px', swaps(n_px, 1))  6.2 us
    all_to_all x1, starting transfers between devices, local(): got = lax.all_to_all(send, GROUP, split_axis=0, concat_axis=0, tiled=True)  5.74 us
    ppermute x1, starting transfers between devices, local(): end1 = lax.ppermute(end1, 'px', swaps(n_px, 1))  4.5 us
    ppermute x1, starting transfers between devices, local(): face2 = lax.ppermute(face2, 'px', swaps(n_px, 0))  2.84 us
    ppermute x1, waiting for transfers between devices, local(): face2 = lax.ppermute(face2, 'px', swaps(n_px, 0))  2.83 us
    pallas_call x1, Pallas kernels, local(): pl.pallas_call(far_kernel, out_shape=vmem(3, FX, FY), in_specs=[VM] * 5,...  2.68 us
  transfers between devices with their start and end apart: 5, of which 4 were waited for; matrix products, arithmetic and copies ran while one was open for 0% of the time, Pallas kernels for 7%

profile of v8, /device:TPU:512, one launch (start us, length us, event | category | flops | bytes accessed | tf_op | source)
XLA Modules:
  0.0 56.5 jit_solution(15339206518742352851)
XLA Ops:
  0.6 1.6 %load.1 = (f32[3,8,48,256]{3,2,1,0:T(8,128)S(1)}, s32[4,128]{1,0:T(4,128)S(1)}, s32[4,128]{1,0:T(4,128)S(1)}, f32[64,256]{1,0:T(8,128)S(1)}, f32[2,64,256]{2,1,0...) custom-call(f32[3,8,48,256]{3,2,1,0:T(8,128)} %refs_0_.1, ...), custom_call_target="tpu_custom_call" | custom-call | bytes 3000000 | tf_op jit(solution)/shard_map/load/pallas_call | solution.py:410
  2.2 1.2 %pack.1 = f32[16,56,128]{2,1,0:T(8,128)} custom-call(f32[3,8,48,256]{3,2,1,0:T(8,128)S(1)} %get-tuple-element.17.near, s32[4,128]{1,0:T(4,128)S(1)} %get-tuple-element.22.owner, s32[4,128]{1,0:T(4,128)S(1)} %get-tuple-element.23.land, f32[64,256]{1,0:T(8,128)S(1)} %get-tuple-element.24.depth, f32[2,64,256]{2,1,0:T(8,128)S(1)} %get-tuple-element.25.flows, ...), custom_call_target="tpu_custom_call" | custom-call | bytes 6000000 | tf_op jit(solution)/shard_map/pack/pallas_call | solution.py:424
  3.4 5.7 %all-to-all-start = ((f32[16,56,128]{2,1,0:T(8,128)}), f32[16,56,128]{2,1,0:T(8,128)S(1)}, u32[]{:S(2)}, u32[]{:S(2)}) async-start(f32[16,56,128]{2,1,0:T(8,128)} %pack.1), calls=%async_computation | async-start | bytes 917504 | tf_op jit(solution)/shard_map/all_to_all | solution.py:433
  9.2 6.5 %collective-permute-start = (f32[3,48,256]{2,1,0:T(8,128)S(1)}, f32[3,48,256]{2,1,0:T(8,128)S(1)}, u32[]{:S(2)}, u32[]{:S(2)}) collective-permute-start(f32[3,48,256]{2,1,0:T(8,128)S(1)} %get-tuple-element.18), channel_id=1, source_target_pairs={{16,32},{48,64},{80,96},{112,128},{144,160},{176,192},{208,224},{2... | collective-permute-start | bytes 442376 | tf_op jit(solution)/shard_map/ppermute | solution.py:422
  15.7 2.8 %collective-permute-start.1 = (f32[3,48,256]{2,1,0:T(8,128)S(1)}, f32[3,48,256]{2,1,0:T(8,128)S(1)}, u32[]{:S(2)}, u32[]{:S(2)}) collective-permute-start(f32[3,48,256]{2,1,0:T(8,128)S(1)} %get-tuple-element.19), channel_id=1, source_target_pairs={{0,16},{32,48},{64,80},{96,112},{128,144},{160,176},{192,208},{224... | collective-permute-start | bytes 442376 | tf_op jit(solution)/shard_map/ppermute | solution.py:423
  18.5 6.2 %collective-permute-done.first = f32[3,48,256]{2,1,0:T(8,128)S(1)} collective-permute-done((f32[3,48,256]{2,1,0:T(8,128)S(1)}, f32[3,48,256]{2,1,0:T(8,128)S(1)}, u32[]{:S(2)}, u32[]{:S(2)}) %collective-permute-start) | collective-permute-done | bytes 147488 | tf_op jit(solution)/shard_map/ppermute | solution.py:422
  24.7 2.8 %collective-permute-done.1.second = f32[3,48,256]{2,1,0:T(8,128)S(1)} collective-permute-done((f32[3,48,256]{2,1,0:T(8,128)S(1)}, f32[3,48,256]{2,1,0:T(8,128)S(1)}, u32[]{:S(2)}, u32[]{:S(2)}) %collective-permute-start.1) | collective-permute-done | bytes 147488 | tf_op jit(solution)/shard_map/ppermute | solution.py:423
  27.5 1.1 %inner.1 = (f32[3,8,48,256]{3,2,1,0:T(8,128)S(1)}, f32[8,48,128]{2,1,0:T(8,128)S(1)}) custom-call(f32[3,8,48,256]{3,2,1,0:T(8,128)S(1)} %get-tuple-element.17.near, f32[3,48,256]{2,1,0:T(8,128)S(1)} %collective-permute-done.first, f32[3,48,256]{2,1,0:T(8,128)S(1)} %collective-permute-done.1.second), custom_call_target="tpu_custom_call" | custom-call | bytes 6000000 | tf_op jit(solution)/shard_map/inner/pallas_call | solution.py:434
  28.6 0.0 all-to-all-done.got
  28.6 1.3 %near.1 = (f32[8,48,256]{2,1,0:T(8,128)}, f32[16,48,128]{2,1,0:T(8,128)S(1)}) custom-call(f32[3,8,48,256]{3,2,1,0:T(8,128)S(1)} %get-tuple-element.20.mid, f32[8,48,128]{2,1,0:T(8,128)S(1)} %get-tuple-element.21.vely, f32[16,56,128]{2,1,0:T(8,128)S(1)} %all-to-all-done.got), custom_call_target="tpu_custom_call" | custom-call | bytes 6000000 | tf_op jit(solution)/shard_map/near/pallas_call | solution.py:443
  29.9 13.7 %all_to_all.10.sums = f32[16,48,128]{2,1,0:T(8,128)S(1)} all-to-all(f32[16,48,128]{2,1,0:T(8,128)S(1)} %get-tuple-element.28), channel_id=1, replica_groups=mesh['px'=48,'py'=4,'dz'=4] {'py','dz'}, dimensions={0} | all-to-all | bytes 786432 | tf_op jit(solution)/shard_map/all_to_all | solution.py:452
  43.6 1.2 %edge.1 = (f32[2,4,48,128]{3,2,1,0:T(8,128)S(1)}, f32[8,256]{1,0:T(8,128)S(1)}, f32[8,256]{1,0:T(8,128)S(1)}) custom-call(f32[16,56,128]{2,1,0:T(8,128)S(1)} %all-to-all-done.got, f32[16,48,128]{2,1,0:T(8,128)S(1)} %all_to_all.10.sums, f32[64,256]{1,0:T(8,128)S(1)} %get-tuple-element.24.depth, f32[2,64,256]{2,1,0:T(8,128)S(1)} %get-tuple-element.25.flows, ...), custom_call_target="tpu_custom_call" | custom-call | bytes 6000000 | tf_op jit(solution)/shard_map/edge/pallas_call | solution.py:453
  44.9 4.5 %collective-permute-start.2 = (f32[8,256]{1,0:T(8,128)S(1)}, f32[8,256]{1,0:T(8,128)S(1)}, u32[]{:S(2)}, u32[]{:S(2)}) collective-permute-start(f32[8,256]{1,0:T(8,128)S(1)} %get-tuple-element.30), channel_id=1, source_target_pairs={{16,32},{48,64},{80,96},{112,128},{144,160},{176,192},{208,224},{2... | collective-permute-start | bytes 24584 | tf_op jit(solution)/shard_map/ppermute | solution.py:463
  49.4 1.9 %collective-permute-start.3 = (f32[8,256]{1,0:T(8,128)S(1)}, f32[8,256]{1,0:T(8,128)S(1)}, u32[]{:S(2)}, u32[]{:S(2)}) collective-permute-start(f32[8,256]{1,0:T(8,128)S(1)} %get-tuple-element.31), channel_id=1, source_target_pairs={{0,16},{32,48},{64,80},{96,112},{128,144},{160,176},{192,208},{224... | collective-permute-start | bytes 24584 | tf_op jit(solution)/shard_map/ppermute | solution.py:464
  51.3 2.7 %far.1.part = f32[3,64,256]{2,1,0:T(8,128)S(1)} custom-call(f32[16,56,128]{2,1,0:T(8,128)S(1)} %all-to-all-done.got, f32[2,4,48,128]{3,2,1,0:T(8,128)S(1)} %get-tuple-element.29.pieces, f32[64,256]{1,0:T(8,128)S(1)} %get-tuple-element.24.depth, f32[2,64,256]{2,1,0:T(8,128)S(1)} %get-tuple-element.25.flows, s32[64,256]{1,0:T(8,128)S(1)} %get-tuple-element.26.mask), custom_call_target="tpu_custom_call" | custom-call | bytes 15000000 | tf_op jit(solution)/shard_map/far/pallas_call | solution.py:465
  54.0 0.6 %collective-permute-done.2.got1 = f32[8,256]{1,0:T(8,128)S(1)} collective-permute-done((f32[8,256]{1,0:T(8,128)S(1)}, f32[8,256]{1,0:T(8,128)S(1)}, u32[]{:S(2)}, u32[]{:S(2)}) %collective-permute-start.2) | collective-permute-done | bytes 8224 | tf_op jit(solution)/shard_map/ppermute | solution.py:463
  54.6 1.2 %collective-permute-done.3.got2 = f32[8,256]{1,0:T(8,128)S(1)} collective-permute-done((f32[8,256]{1,0:T(8,128)S(1)}, f32[8,256]{1,0:T(8,128)S(1)}, u32[]{:S(2)}, u32[]{:S(2)}) %collective-permute-start.3) | collective-permute-done | bytes 8224 | tf_op jit(solution)/shard_map/ppermute | solution.py:464
  55.8 0.7 %join.1 = f32[3,64,256]{2,1,0:T(8,128)} custom-call(f32[3,64,256]{2,1,0:T(8,128)S(1)} %far.1.part, f32[8,256]{1,0:T(8,128)S(1)} %collective-permute-done.2.got1, f32[8,256]{1,0:T(8,128)S(1)} %collective-permute-done.3.got2), custom_call_target="tpu_custom_call" | custom-call | bytes 3000000 | tf_op jit(solution)/shard_map/join/pallas_call | solution.py:475
Async XLA Ops:
  3.4 25.2 %all-to-all-start = ((f32[16,56,128]{2,1,0:T(8,128)}), f32[16,56,128]{2,1,0:T(8,128)S(1)}, u32[]{:S(2)}, u32[]{:S(2)}) async-start(f32[16,56,128]{2,1,0:T(8,128)} %pack.1), calls=%async_computation | async-start | bytes 917504 | tf_op jit(solution)/shard_map/all_to_all | solution.py:433
  9.2 15.5 %collective-permute-start = (f32[3,48,256]{2,1,0:T(8,128)S(1)}, f32[3,48,256]{2,1,0:T(8,128)S(1)}, u32[]{:S(2)}, u32[]{:S(2)}) collective-permute-start(f32[3,48,256]{2,1,0:T(8,128)S(1)} %get-tuple-element.18), channel_id=1, source_target_pairs={{16,32},{48,64},{80,96},{112,128},{144,160},{176,192},{208,224},{2... | collective-permute-start | bytes 442376 | tf_op jit(solution)/shard_map/ppermute | solution.py:422
  15.7 11.9 %collective-permute-start.1 = (f32[3,48,256]{2,1,0:T(8,128)S(1)}, f32[3,48,256]{2,1,0:T(8,128)S(1)}, u32[]{:S(2)}, u32[]{:S(2)}) collective-permute-start(f32[3,48,256]{2,1,0:T(8,128)S(1)} %get-tuple-element.19), channel_id=1, source_target_pairs={{0,16},{32,48},{64,80},{96,112},{128,144},{160,176},{192,208},{224... | collective-permute-start | bytes 442376 | tf_op jit(solution)/shard_map/ppermute | solution.py:423
  44.9 9.8 %collective-permute-start.2 = (f32[8,256]{1,0:T(8,128)S(1)}, f32[8,256]{1,0:T(8,128)S(1)}, u32[]{:S(2)}, u32[]{:S(2)}) collective-permute-start(f32[8,256]{1,0:T(8,128)S(1)} %get-tuple-element.30), channel_id=1, source_target_pairs={{16,32},{48,64},{80,96},{112,128},{144,160},{176,192},{208,224},{2... | collective-permute-start | bytes 24584 | tf_op jit(solution)/shard_map/ppermute | solution.py:463
  49.4 6.4 %collective-permute-start.3 = (f32[8,256]{1,0:T(8,128)S(1)}, f32[8,256]{1,0:T(8,128)S(1)}, u32[]{:S(2)}, u32[]{:S(2)}) collective-permute-start(f32[8,256]{1,0:T(8,128)S(1)} %get-tuple-element.31), channel_id=1, source_target_pairs={{0,16},{32,48},{64,80},{96,112},{128,144},{160,176},{192,208},{224... | collective-permute-start | bytes 24584 | tf_op jit(solution)/shard_map/ppermute | solution.py:464

commit v9 on v8

--- a/solution.py
+++ b/solution.py
@@ -24,7 +24,8 @@
 FX = 64
 FY = 256
 ROWS = CX * 3 * 2
-BLK = ROWS + 8
+SIDE = CZ // 3
+BLK = SIDE + 8
 
 f32 = jnp.float32
 GROUP = ("py", "dz")
@@ -63,7 +64,7 @@
         move.wait()
 
 
-def pack_kernel(near, owner, land, depth, flows, mask, out):
+def pack_kernel(near, owner, land, depth, flows, mask, out, z1, z2):
     py = lax.axis_index("py")
     dz = lax.axis_index("dz")
     me = py * NDZ + dz
@@ -74,10 +75,10 @@
     lanes = lane_iota((8, 128))
     mine = jnp.where(odd, lanes, 127 - lanes) >= 64
     codes = jnp.where(mine, codes, 0.0)
-    zero = jnp.zeros((ROWS, 128), f32)
+    zero = jnp.zeros((SIDE, 128), f32)
     for b in range(GRP):
-        out[b, 0:ROWS] = zero
-        out[b, ROWS:BLK] = codes
+        out[b, 0:SIDE] = zero
+        out[b, SIDE:BLK] = codes
 
     def edge(col):
         k = lane_iota((FX, 128))
@@ -89,18 +90,18 @@
 
     @pl.when(me > 0)
     def _():
-        out[me - 1, ROWS:BLK] = edge(0)
+        out[me - 1, SIDE:BLK] = edge(0)
 
     @pl.when(me < GRP - 1)
     def _():
-        out[me + 1, ROWS:BLK] = edge(FY - 1)
-
-    def zface(dst, z):
-        for f in range(3):
-            face = near[f, :, z, :]
-            for h in range(2):
-                r = (f * 2 + h) * 8
-                out[dst, r : r + 8] = face[:, h * 128 : (h + 1) * 128]
+        out[me + 1, SIDE:BLK] = edge(FY - 1)
+
+    odd_dz = lax.rem(dz, 2) == 1
+    for f in range(3):
+        low = near[f, :, 0, :]
+        high = near[f, :, CZ - 1, :]
+        z1[f] = jnp.where(odd_dz, high, low)
+        z2[f] = jnp.where(odd_dz, low, high)
 
     def yface(dst, y):
         k = lane_iota((CZ, 128))
@@ -108,15 +109,8 @@
         for f in range(3):
             for x in range(CX):
                 m = jnp.where(k == f * CX + x, near[f, x, :, y : y + 1], m)
-        out[dst, 0:ROWS] = m
-
-    @pl.when(dz > 0)
-    def _():
-        zface(me - 1, 0)
-
-    @pl.when(dz < NDZ - 1)
-    def _():
-        zface(me + 1, CZ - 1)
+        layers = [pltpu.roll(m[SIDE * n : SIDE * (n + 1)], 32 * n, 1) for n in range(3)]
+        out[dst, 0:SIDE] = layers[0] + layers[1] + layers[2]
 
     @pl.when(py > 0)
     def _():
@@ -156,14 +150,20 @@
             mid[f, x] = moved
 
 
-def near_kernel(mid, vely, got, frac, sums):
+def near_kernel(mid, vely, got, z1, z2, frac, sums):
     py = lax.axis_index("py")
     dz = lax.axis_index("dz")
     me = py * NDZ + dz
-    left = jnp.where(py > 0, got[jnp.maximum(me - NDZ, 0), 0:ROWS], 0.0)
-    right = jnp.where(py < NPY - 1, got[jnp.minimum(me + NDZ, GRP - 1), 0:ROWS], 0.0)
-    down = jnp.where(dz > 0, got[jnp.maximum(me - 1, 0), 0:ROWS], 0.0) * diffuse_coef
-    up = jnp.where(dz < NDZ - 1, got[jnp.minimum(me + 1, GRP - 1), 0:ROWS], 0.0) * diffuse_coef
+    odd_dz = lax.rem(dz, 2) == 1
+    up = [jnp.where(odd_dz, z1[f], z2[f]) * diffuse_coef for f in range(3)]
+    down = [jnp.where(odd_dz, z2[f], z1[f]) * diffuse_coef for f in range(3)]
+
+    def yface(at, inside):
+        m = jnp.where(inside, got[at, 0:SIDE], 0.0)
+        return jnp.concatenate([m] + [pltpu.roll(m, 128 - 32 * n, 1) for n in (1, 2)], axis=0)
+
+    left = yface(jnp.maximum(me - NDZ, 0), py > 0)
+    right = yface(jnp.minimum(me + NDZ, GRP - 1), py < NPY - 1)
     lane = lane_iota((CZ, 128))
     row = lax.broadcasted_iota(jnp.int32, (8, 128), 0)
     for p in range(CX):
@@ -179,9 +179,8 @@
                 if f == 2:
                     term = term + (sign * slope_coef) * side[:, x : x + 1]
                 n = mid[f, x, :, lanes] + jnp.where(lane == edge, term, 0.0)
-                r = (f * 2 + h) * 8 + x
-                first = n[0:8] + jnp.where(row == 0, down[r : r + 1], 0.0)
-                last = n[CZ - 8 : CZ] + jnp.where(row == 7, up[r : r + 1], 0.0)
+                first = n[0:8] + jnp.where(row == 0, down[f][x : x + 1, lanes], 0.0)
+                last = n[CZ - 8 : CZ] + jnp.where(row == 7, up[f][x : x + 1, lanes], 0.0)
                 new.append(jnp.concatenate([first, n[8 : CZ - 8], last], axis=0))
             frac[x, :, lanes] = new[0]
             for f in range(3):
@@ -196,7 +195,7 @@
 def decode(got, me, a, h):
     d = a * NDZ + 2 * h
     lanes = lane_iota((8, 128))
-    code = jnp.where(lanes < 64, got[d, ROWS:BLK], got[d + 1, ROWS:BLK]).astype(jnp.int32)
+    code = jnp.where(lanes < 64, got[d, SIDE:BLK], got[d + 1, SIDE:BLK]).astype(jnp.int32)
     y = (code >> 14) * FY + (code & (FY - 1)) - me * FY
     y = jnp.where((y < -1) | (y > FY), -128, y)
     return y.astype(f32), ((code >> 8) & (FX - 1)).astype(f32)
@@ -339,7 +338,7 @@
     sides = []
     for n in range(2):
         other = jnp.maximum(me - 1, 0) if n == 0 else jnp.minimum(me + 1, GRP - 1)
-        e = got[other, ROWS:BLK]
+        e = got[other, SIDE:BLK]
         e = jnp.where((other % 2) == 1, e, pltpu.roll(e, 64, 1))
         inside = (me > 0) if n == 0 else (me < GRP - 1)
         s = []
@@ -421,16 +420,18 @@
     near_state, owner, land, far_depth, far_flows, wet_mask = given
     face1 = lax.ppermute(face1, "px", swaps(n_px, 1))
     face2 = lax.ppermute(face2, "px", swaps(n_px, 0))
-    send = pl.pallas_call(
+    send, z1, z2 = pl.pallas_call(
         pack_kernel,
-        out_shape=shape(GRP, BLK, 128),
+        out_shape=(shape(GRP, BLK, 128), vmem(3, CX, CY), vmem(3, CX, CY)),
         in_specs=[VM] * 6,
-        out_specs=VM,
+        out_specs=(VM,) * 3,
         compiler_params=PARAMS,
         cost_estimate=cost(2),
         name="pack",
     )(near_state, owner, land, far_depth, far_flows, wet_mask)
     got = lax.all_to_all(send, GROUP, split_axis=0, concat_axis=0, tiled=True)
+    z1 = lax.ppermute(z1, "dz", swaps(NDZ, 1))
+    z2 = lax.ppermute(z2, "dz", swaps(NDZ, 0))
     mid, vely = pl.pallas_call(
         inner_kernel,
         out_shape=(vmem(3, CX, CZ, CY), vmem(CX, CZ, 128)),
@@ -443,12 +444,12 @@
     new_frac, sums = pl.pallas_call(
         near_kernel,
         out_shape=(shape(CX, CZ, CY), shape(GRP, ROWS, 128)),
-        in_specs=[VM] * 3,
+        in_specs=[VM] * 5,
         out_specs=(VM,) * 2,
         compiler_params=PARAMS,
         cost_estimate=cost(2),
         name="near",
-    )(mid, vely, got)
+    )(mid, vely, got, z1, z2)
     sums = lax.all_to_all(sums, GROUP, split_axis=0, concat_axis=0, tiled=True)
     pieces, end1, end2 = pl.pallas_call(
         functools.partial(edge_kernel, column_height / (CZ * NDZ)),

time: 56.9 us -> 56.7 us (level)
  waiting for transfers between devices: 10.9 us -> 5.6 us
  starting transfers between devices: 21.5 us -> 26.6 us
    ppermute x1, waiting for transfers between devices: 6.2 us -> 0.24 us  [local(): face1 = lax.ppermute(face1, 'px', swaps(n_px, 1))]
    ppermute x0 -> x2, starting transfers between devices: none -> 5.85 us  [the longest x1 5.18 us: local(): z2 = lax.ppermute(z2, 'dz', swaps(NDZ, 0))]
    ppermute x1, starting transfers between devices: 4.5 us -> 3.76 us  [local(): end1 = lax.ppermute(end1, 'px', swaps(n_px, 1))]
    ppermute x1, waiting for transfers between devices: 1.19 us -> 0.45 us  [local(): end2 = lax.ppermute(end2, 'px', swaps(n_px, 0))]
    ppermute x1, waiting for transfers between devices: 0.64 us -> 1.38 us  [local(): end1 = lax.ppermute(end1, 'px', swaps(n_px, 1))]
    ppermute x1, waiting for transfers between devices: 2.83 us -> 3.52 us  [local(): face2 = lax.ppermute(face2, 'px', swaps(n_px, 0))]
  transfers between devices with their start and end apart: 5 -> 7, of which waited for: 4 -> 4; matrix products, arithmetic and copies ran while one was open for 0% -> 0% of each run, Pallas kernels for 7% -> 7%
where the time goes in v9:
time: 56.7 us; the launch traced here: 56.3 us
  starting transfers between devices  26.6 us (47%)
  blocking collectives  13.5 us (24%)
  Pallas kernels  9.82 us (17%)
  waiting for transfers between devices  5.6 us (10%)
  between operations  0.74 us (1%)
    all_to_all x1, blocking collectives, local(): sums = lax.all_to_all(sums, GROUP, split_axis=0, concat_axis=0, tiled=True)  13.5 us
    ppermute x1, starting transfers between devices, local(): face1 = lax.ppermute(face1, 'px', swaps(n_px, 1))  6.46 us
    all_to_all x1, starting transfers between devices, local(): got = lax.all_to_all(send, GROUP, split_axis=0, concat_axis=0, tiled=True)  5.78 us
    ppermute x1, starting transfers between devices, local(): z2 = lax.ppermute(z2, 'dz', swaps(NDZ, 0))  5.18 us
    ppermute x1, starting transfers between devices, local(): end1 = lax.ppermute(end1, 'px', swaps(n_px, 1))  3.76 us
    ppermute x1, waiting for transfers between devices, local(): face2 = lax.ppermute(face2, 'px', swaps(n_px, 0))  3.52 us
    ppermute x1, starting transfers between devices, local(): face2 = lax.ppermute(face2, 'px', swaps(n_px, 0))  2.84 us
    pallas_call x1, Pallas kernels, local(): pl.pallas_call(far_kernel, out_shape=vmem(3, FX, FY), in_specs=[VM] * 5,...  2.68 us
  transfers between devices with their start and end apart: 7, of which 4 were waited for; matrix products, arithmetic and copies ran while one was open for 0% of the time, Pallas kernels for 7%

profile of v9, /device:TPU:512, one launch (start us, length us, event | category | flops | bytes accessed | tf_op | source)
XLA Modules:
  0.0 56.3 jit_solution(10584851221282561279)
XLA Ops:
  0.6 1.6 %load.1 = (f32[3,8,48,256]{3,2,1,0:T(8,128)S(1)}, s32[4,128]{1,0:T(4,128)S(1)}, s32[4,128]{1,0:T(4,128)S(1)}, f32[64,256]{1,0:T(8,128)S(1)}, f32[2,64,256]{2,1,0...) custom-call(f32[3,8,48,256]{3,2,1,0:T(8,128)} %refs_0_.1, ...), custom_call_target="tpu_custom_call" | custom-call | bytes 3000000 | tf_op jit(solution)/shard_map/load/pallas_call | solution.py:409
  2.2 1.2 %pack.1 = (f32[16,24,128]{2,1,0:T(8,128)}, f32[3,8,256]{2,1,0:T(8,128)S(1)}, f32[3,8,256]{2,1,0:T(8,128)S(1)}) custom-call(f32[3,8,48,256]{3,2,1,0:T(8,128)S(1)} %get-tuple-element.20.near, s32[4,128]{1,0:T(4,128)S(1)} %get-tuple-element.25.owner, s32[4,128]{1,0:T(4,128)S(1)} %get-tuple-element.26.land, f32[64,256]{1,0:T(8,128)S(1)} %get-tuple-element.27.depth, ...), custom_call_target="tpu_custom_call" | custom-call | bytes 6000000 | tf_op jit(solution)/shard_map/pack/pallas_call | solution.py:423
  3.4 5.8 %all-to-all-start = ((f32[16,24,128]{2,1,0:T(8,128)}), f32[16,24,128]{2,1,0:T(8,128)S(1)}, u32[]{:S(2)}, u32[]{:S(2)}) async-start(f32[16,24,128]{2,1,0:T(8,128)} %get-tuple-element.30), calls=%async_computation | async-start | bytes 393216 | tf_op jit(solution)/shard_map/all_to_all | solution.py:432
  9.2 6.5 %collective-permute-start = (f32[3,48,256]{2,1,0:T(8,128)S(1)}, f32[3,48,256]{2,1,0:T(8,128)S(1)}, u32[]{:S(2)}, u32[]{:S(2)}) collective-permute-start(f32[3,48,256]{2,1,0:T(8,128)S(1)} %get-tuple-element.21), channel_id=1, source_target_pairs={{16,32},{48,64},{80,96},{112,128},{144,160},{176,192},{208,224},{2... | collective-permute-start | bytes 442376 | tf_op jit(solution)/shard_map/ppermute | solution.py:421
  15.7 2.8 %collective-permute-start.1 = (f32[3,48,256]{2,1,0:T(8,128)S(1)}, f32[3,48,256]{2,1,0:T(8,128)S(1)}, u32[]{:S(2)}, u32[]{:S(2)}) collective-permute-start(f32[3,48,256]{2,1,0:T(8,128)S(1)} %get-tuple-element.22), channel_id=1, source_target_pairs={{0,16},{32,48},{64,80},{96,112},{128,144},{160,176},{192,208},{224... | collective-permute-start | bytes 442376 | tf_op jit(solution)/shard_map/ppermute | solution.py:422
  18.5 0.7 %collective-permute-start.2 = (f32[3,8,256]{2,1,0:T(8,128)S(1)}, f32[3,8,256]{2,1,0:T(8,128)S(1)}, u32[]{:S(2)}, u32[]{:S(2)}) collective-permute-start(f32[3,8,256]{2,1,0:T(8,128)S(1)} %get-tuple-element.31), channel_id=1, source_target_pairs={{1,2},{2,1},{5,6},{6,5},{9,10},{10,9},{13,14},{14,13},{17,18},{18,... | collective-permute-start | bytes 73736 | tf_op jit(solution)/shard_map/ppermute | solution.py:433
  19.2 5.2 %collective-permute-start.3 = (f32[3,8,256]{2,1,0:T(8,128)S(1)}, f32[3,8,256]{2,1,0:T(8,128)S(1)}, u32[]{:S(2)}, u32[]{:S(2)}) collective-permute-start(f32[3,8,256]{2,1,0:T(8,128)S(1)} %get-tuple-element.32), channel_id=1, source_target_pairs={{0,1},{2,3},{1,0},{3,2},{4,5},{6,7},{5,4},{7,6},{8,9},{10,11},{9,8... | collective-permute-start | bytes 73736 | tf_op jit(solution)/shard_map/ppermute | solution.py:434
  24.4 0.2 collective-permute-done.first
  24.6 3.5 %collective-permute-done.1.second = f32[3,48,256]{2,1,0:T(8,128)S(1)} collective-permute-done((f32[3,48,256]{2,1,0:T(8,128)S(1)}, f32[3,48,256]{2,1,0:T(8,128)S(1)}, u32[]{:S(2)}, u32[]{:S(2)}) %collective-permute-start.1) | collective-permute-done | bytes 147488 | tf_op jit(solution)/shard_map/ppermute | solution.py:422
  28.1 1.1 %inner.1 = (f32[3,8,48,256]{3,2,1,0:T(8,128)S(1)}, f32[8,48,128]{2,1,0:T(8,128)S(1)}) custom-call(f32[3,8,48,256]{3,2,1,0:T(8,128)S(1)} %get-tuple-element.20.near, f32[3,48,256]{2,1,0:T(8,128)S(1)} %collective-permute-done.first, f32[3,48,256]{2,1,0:T(8,128)S(1)} %collective-permute-done.1.second), custom_call_target="tpu_custom_call" | custom-call | bytes 6000000 | tf_op jit(solution)/shard_map/inner/pallas_call | solution.py:435
  29.2 0.0 collective-permute-done.2.z1
  29.2 0.0 collective-permute-done.3.z2
  29.2 0.0 all-to-all-done.got
  29.3 1.4 %near.1 = (f32[8,48,256]{2,1,0:T(8,128)}, f32[16,48,128]{2,1,0:T(8,128)S(1)}) custom-call(f32[3,8,48,256]{3,2,1,0:T(8,128)S(1)} %get-tuple-element.23.mid, f32[8,48,128]{2,1,0:T(8,128)S(1)} %get-tuple-element.24.vely, f32[16,24,128]{2,1,0:T(8,128)S(1)} %all-to-all-done.got, f32[3,8,256]{2,1,0:T(8,128)S(1)} %collective-permute-done.2.z1, ...), custom_call_target="tpu_custom_call" | custom-call | bytes 6000000 | tf_op jit(solution)/shard_map/near/pallas_call | solution.py:444
  30.6 13.5 %all_to_all.10.sums = f32[16,48,128]{2,1,0:T(8,128)S(1)} all-to-all(f32[16,48,128]{2,1,0:T(8,128)S(1)} %get-tuple-element.34), channel_id=1, replica_groups=mesh['px'=48,'py'=4,'dz'=4] {'py','dz'}, dimensions={0} | all-to-all | bytes 786432 | tf_op jit(solution)/shard_map/all_to_all | solution.py:453
  44.2 1.2 %edge.1 = (f32[2,4,48,128]{3,2,1,0:T(8,128)S(1)}, f32[8,256]{1,0:T(8,128)S(1)}, f32[8,256]{1,0:T(8,128)S(1)}) custom-call(f32[16,24,128]{2,1,0:T(8,128)S(1)} %all-to-all-done.got, f32[16,48,128]{2,1,0:T(8,128)S(1)} %all_to_all.10.sums, f32[64,256]{1,0:T(8,128)S(1)} %get-tuple-element.27.depth, f32[2,64,256]{2,1,0:T(8,128)S(1)} %get-tuple-element.28.flows, ...), custom_call_target="tpu_custom_call" | custom-call | bytes 6000000 | tf_op jit(solution)/shard_map/edge/pallas_call | solution.py:454
  45.4 3.8 %collective-permute-start.4 = (f32[8,256]{1,0:T(8,128)S(1)}, f32[8,256]{1,0:T(8,128)S(1)}, u32[]{:S(2)}, u32[]{:S(2)}) collective-permute-start(f32[8,256]{1,0:T(8,128)S(1)} %get-tuple-element.36), channel_id=1, source_target_pairs={{16,32},{48,64},{80,96},{112,128},{144,160},{176,192},{208,224},{2... | collective-permute-start | bytes 24584 | tf_op jit(solution)/shard_map/ppermute | solution.py:464
  49.2 1.9 %collective-permute-start.5 = (f32[8,256]{1,0:T(8,128)S(1)}, f32[8,256]{1,0:T(8,128)S(1)}, u32[]{:S(2)}, u32[]{:S(2)}) collective-permute-start(f32[8,256]{1,0:T(8,128)S(1)} %get-tuple-element.37), channel_id=1, source_target_pairs={{0,16},{32,48},{64,80},{96,112},{128,144},{160,176},{192,208},{224... | collective-permute-start | bytes 24584 | tf_op jit(solution)/shard_map/ppermute | solution.py:465
  51.1 2.7 %far.1.part = f32[3,64,256]{2,1,0:T(8,128)S(1)} custom-call(f32[16,24,128]{2,1,0:T(8,128)S(1)} %all-to-all-done.got, f32[2,4,48,128]{3,2,1,0:T(8,128)S(1)} %get-tuple-element.35.pieces, f32[64,256]{1,0:T(8,128)S(1)} %get-tuple-element.27.depth, f32[2,64,256]{2,1,0:T(8,128)S(1)} %get-tuple-element.28.flows, s32[64,256]{1,0:T(8,128)S(1)} %get-tuple-element.29.mask), custom_call_target="tpu_custom_call" | custom-call | bytes 15000000 | tf_op jit(solution)/shard_map/far/pallas_call | solution.py:466
  53.8 1.4 %collective-permute-done.4.got1 = f32[8,256]{1,0:T(8,128)S(1)} collective-permute-done((f32[8,256]{1,0:T(8,128)S(1)}, f32[8,256]{1,0:T(8,128)S(1)}, u32[]{:S(2)}, u32[]{:S(2)}) %collective-permute-start.4) | collective-permute-done | bytes 8224 | tf_op jit(solution)/shard_map/ppermute | solution.py:464
  55.2 0.4 collective-permute-done.5.got2
  55.6 0.7 %join.1 = f32[3,64,256]{2,1,0:T(8,128)} custom-call(f32[3,64,256]{2,1,0:T(8,128)S(1)} %far.1.part, f32[8,256]{1,0:T(8,128)S(1)} %collective-permute-done.4.got1, f32[8,256]{1,0:T(8,128)S(1)} %collective-permute-done.5.got2), custom_call_target="tpu_custom_call" | custom-call | bytes 3000000 | tf_op jit(solution)/shard_map/join/pallas_call | solution.py:476
Async XLA Ops:
  3.4 25.8 %all-to-all-start = ((f32[16,24,128]{2,1,0:T(8,128)}), f32[16,24,128]{2,1,0:T(8,128)S(1)}, u32[]{:S(2)}, u32[]{:S(2)}) async-start(f32[16,24,128]{2,1,0:T(8,128)} %get-tuple-element.30), calls=%async_computation | async-start | bytes 393216 | tf_op jit(solution)/shard_map/all_to_all | solution.py:432
  9.2 15.4 %collective-permute-start = (f32[3,48,256]{2,1,0:T(8,128)S(1)}, f32[3,48,256]{2,1,0:T(8,128)S(1)}, u32[]{:S(2)}, u32[]{:S(2)}) collective-permute-start(f32[3,48,256]{2,1,0:T(8,128)S(1)} %get-tuple-element.21), channel_id=1, source_target_pairs={{16,32},{48,64},{80,96},{112,128},{144,160},{176,192},{208,224},{2... | collective-permute-start | bytes 442376 | tf_op jit(solution)/shard_map/ppermute | solution.py:421
  15.7 12.5 %collective-permute-start.1 = (f32[3,48,256]{2,1,0:T(8,128)S(1)}, f32[3,48,256]{2,1,0:T(8,128)S(1)}, u32[]{:S(2)}, u32[]{:S(2)}) collective-permute-start(f32[3,48,256]{2,1,0:T(8,128)S(1)} %get-tuple-element.22), channel_id=1, source_target_pairs={{0,16},{32,48},{64,80},{96,112},{128,144},{160,176},{192,208},{224... | collective-permute-start | bytes 442376 | tf_op jit(solution)/shard_map/ppermute | solution.py:422
  18.5 10.7 %collective-permute-start.2 = (f32[3,8,256]{2,1,0:T(8,128)S(1)}, f32[3,8,256]{2,1,0:T(8,128)S(1)}, u32[]{:S(2)}, u32[]{:S(2)}) collective-permute-start(f32[3,8,256]{2,1,0:T(8,128)S(1)} %get-tuple-element.31), channel_id=1, source_target_pairs={{1,2},{2,1},{5,6},{6,5},{9,10},{10,9},{13,14},{14,13},{17,18},{18,... | collective-permute-start | bytes 73736 | tf_op jit(solution)/shard_map/ppermute | solution.py:433
  19.2 10.0 %collective-permute-start.3 = (f32[3,8,256]{2,1,0:T(8,128)S(1)}, f32[3,8,256]{2,1,0:T(8,128)S(1)}, u32[]{:S(2)}, u32[]{:S(2)}) collective-permute-start(f32[3,8,256]{2,1,0:T(8,128)S(1)} %get-tuple-element.32), channel_id=1, source_target_pairs={{0,1},{2,3},{1,0},{3,2},{4,5},{6,7},{5,4},{7,6},{8,9},{10,11},{9,8... | collective-permute-start | bytes 73736 | tf_op jit(solution)/shard_map/ppermute | solution.py:434
  45.4 9.8 %collective-permute-start.4 = (f32[8,256]{1,0:T(8,128)S(1)}, f32[8,256]{1,0:T(8,128)S(1)}, u32[]{:S(2)}, u32[]{:S(2)}) collective-permute-start(f32[8,256]{1,0:T(8,128)S(1)} %get-tuple-element.36), channel_id=1, source_target_pairs={{16,32},{48,64},{80,96},{112,128},{144,160},{176,192},{208,224},{2... | collective-permute-start | bytes 24584 | tf_op jit(solution)/shard_map/ppermute | solution.py:464
  49.2 6.4 %collective-permute-start.5 = (f32[8,256]{1,0:T(8,128)S(1)}, f32[8,256]{1,0:T(8,128)S(1)}, u32[]{:S(2)}, u32[]{:S(2)}) collective-permute-start(f32[8,256]{1,0:T(8,128)S(1)} %get-tuple-element.37), channel_id=1, source_target_pairs={{0,16},{32,48},{64,80},{96,112},{128,144},{160,176},{192,208},{224... | collective-permute-start | bytes 24584 | tf_op jit(solution)/shard_map/ppermute | solution.py:465

commit v10 on v9

--- a/solution.py
+++ b/solution.py
@@ -294,8 +294,10 @@
 
 
 def far_kernel(
-    got, pieces, depth, flows, mask, out, wide
+    got, pieces, depth, flows, mask, frac, out, frac_out, wide, sem
 ):
+    keep = pltpu.make_async_copy(frac, frac_out, sem)
+    keep.start()
     me = lax.axis_index("py") * NDZ + lax.axis_index("dz")
     xcell = cell_rows(FX)
     ycell = cell_rows(FY)
@@ -365,6 +367,7 @@
         ym = jnp.where(lane == 0, sides[:, f : f + 1], pltpu.roll(body[f][3], 1, 1))
         new = (xp + xm) + (yp + ym)
         out[f] = new
+    keep.wait()
 
 
 def join_kernel(part, got1, got2, out, new, sem):
@@ -443,7 +446,7 @@
     )(near_state, face1, face2)
     new_frac, sums = pl.pallas_call(
         near_kernel,
-        out_shape=(shape(CX, CZ, CY), shape(GRP, ROWS, 128)),
+        out_shape=(vmem(CX, CZ, CY), shape(GRP, ROWS, 128)),
         in_specs=[VM] * 5,
         out_specs=(VM,) * 2,
         compiler_params=PARAMS,
@@ -463,16 +466,16 @@
     )(got, sums, far_depth, far_flows, wet_mask)
     end1 = lax.ppermute(end1, "px", swaps(n_px, 1))
     end2 = lax.ppermute(end2, "px", swaps(n_px, 0))
-    part = pl.pallas_call(
+    part, new_frac = pl.pallas_call(
         far_kernel,
-        out_shape=vmem(3, FX, FY),
-        in_specs=[VM] * 5,
-        out_specs=VM,
-        scratch_shapes=[vmem(8, 128, 128)],
+        out_shape=(vmem(3, FX, FY), shape(CX, CZ, CY)),
+        in_specs=[VM] * 6,
+        out_specs=(VM, ANY),
+        scratch_shapes=[vmem(8, 128, 128), pltpu.SemaphoreType.DMA(())],
         compiler_params=pltpu.CompilerParams(vmem_limit_bytes=20 << 20),
         cost_estimate=cost(5),
         name="far",
-    )(got, pieces, far_depth, far_flows, wet_mask)
+    )(got, pieces, far_depth, far_flows, wet_mask, new_frac)
     far_new = pl.pallas_call(
         join_kernel,
         out_shape=shape(3, FX, FY),

time: 56.7 us -> 56 us (0.988)
  Pallas kernels: 9.82 us -> 9.12 us
    pallas_call x2, Pallas kernels: 4.05 us -> 3.35 us  [the longest x1 2.69 us: local(): pl.pallas_call(far_kernel, out_shape=(vmem(3, FX, FY), shape(CX, CZ, CY))...]
where the time goes in v10:
time: 56 us; the launch traced here: 55.6 us
  starting transfers between devices  26.6 us (48%)
  blocking collectives  13.6 us (24%)
  Pallas kernels  9.12 us (16%)
  waiting for transfers between devices  5.59 us (10%)
  between operations  0.75 us (1%)
    all_to_all x1, blocking collectives, local(): sums = lax.all_to_all(sums, GROUP, split_axis=0, concat_axis=0, tiled=True)  13.6 us
    ppermute x1, starting transfers between devices, local(): face1 = lax.ppermute(face1, 'px', swaps(n_px, 1))  6.46 us
    all_to_all x1, starting transfers between devices, local(): got = lax.all_to_all(send, GROUP, split_axis=0, concat_axis=0, tiled=True)  5.78 us
    ppermute x1, starting transfers between devices, local(): z2 = lax.ppermute(z2, 'dz', swaps(NDZ, 0))  5.18 us
    ppermute x1, starting transfers between devices, local(): end1 = lax.ppermute(end1, 'px', swaps(n_px, 1))  3.76 us
    ppermute x1, waiting for transfers between devices, local(): face2 = lax.ppermute(face2, 'px', swaps(n_px, 0))  3.52 us
    ppermute x1, starting transfers between devices, local(): face2 = lax.ppermute(face2, 'px', swaps(n_px, 0))  2.84 us
    pallas_call x1, Pallas kernels, local(): pl.pallas_call(far_kernel, out_shape=(vmem(3, FX, FY), shape(CX, CZ, CY))...  2.69 us
  transfers between devices with their start and end apart: 7, of which 4 were waited for; matrix products, arithmetic and copies ran while one was open for 0% of the time, Pallas kernels for 7%

profile of v10, /device:TPU:512, one launch (start us, length us, event | category | flops | bytes accessed | tf_op | source)
XLA Modules:
  0.0 55.6 jit_solution(1806212005156901841)
XLA Ops:
  0.6 1.6 %load.1 = (f32[3,8,48,256]{3,2,1,0:T(8,128)S(1)}, s32[4,128]{1,0:T(4,128)S(1)}, s32[4,128]{1,0:T(4,128)S(1)}, f32[64,256]{1,0:T(8,128)S(1)}, f32[2,64,256]{2,1,0...) custom-call(f32[3,8,48,256]{3,2,1,0:T(8,128)} %refs_0_.1, ...), custom_call_target="tpu_custom_call" | custom-call | bytes 3000000 | tf_op jit(solution)/shard_map/load/pallas_call | solution.py:412
  2.2 1.2 %pack.1 = (f32[16,24,128]{2,1,0:T(8,128)}, f32[3,8,256]{2,1,0:T(8,128)S(1)}, f32[3,8,256]{2,1,0:T(8,128)S(1)}) custom-call(f32[3,8,48,256]{3,2,1,0:T(8,128)S(1)} %get-tuple-element.22.near, s32[4,128]{1,0:T(4,128)S(1)} %get-tuple-element.23.owner, s32[4,128]{1,0:T(4,128)S(1)} %get-tuple-element.24.land, f32[64,256]{1,0:T(8,128)S(1)} %get-tuple-element.25.depth, ...), custom_call_target="tpu_custom_call" | custom-call | bytes 6000000 | tf_op jit(solution)/shard_map/pack/pallas_call | solution.py:426
  3.4 5.8 %all-to-all-start = ((f32[16,24,128]{2,1,0:T(8,128)}), f32[16,24,128]{2,1,0:T(8,128)S(1)}, u32[]{:S(2)}, u32[]{:S(2)}) async-start(f32[16,24,128]{2,1,0:T(8,128)} %get-tuple-element.28), calls=%async_computation | async-start | bytes 393216 | tf_op jit(solution)/shard_map/all_to_all | solution.py:435
  9.2 6.5 %collective-permute-start = (f32[3,48,256]{2,1,0:T(8,128)S(1)}, f32[3,48,256]{2,1,0:T(8,128)S(1)}, u32[]{:S(2)}, u32[]{:S(2)}) collective-permute-start(f32[3,48,256]{2,1,0:T(8,128)S(1)} %get-tuple-element.29), channel_id=1, source_target_pairs={{16,32},{48,64},{80,96},{112,128},{144,160},{176,192},{208,224},{2... | collective-permute-start | bytes 442376 | tf_op jit(solution)/shard_map/ppermute | solution.py:424
  15.7 2.8 %collective-permute-start.1 = (f32[3,48,256]{2,1,0:T(8,128)S(1)}, f32[3,48,256]{2,1,0:T(8,128)S(1)}, u32[]{:S(2)}, u32[]{:S(2)}) collective-permute-start(f32[3,48,256]{2,1,0:T(8,128)S(1)} %get-tuple-element.30), channel_id=1, source_target_pairs={{0,16},{32,48},{64,80},{96,112},{128,144},{160,176},{192,208},{224... | collective-permute-start | bytes 442376 | tf_op jit(solution)/shard_map/ppermute | solution.py:425
  18.5 0.7 %collective-permute-start.2 = (f32[3,8,256]{2,1,0:T(8,128)S(1)}, f32[3,8,256]{2,1,0:T(8,128)S(1)}, u32[]{:S(2)}, u32[]{:S(2)}) collective-permute-start(f32[3,8,256]{2,1,0:T(8,128)S(1)} %get-tuple-element.33), channel_id=1, source_target_pairs={{1,2},{2,1},{5,6},{6,5},{9,10},{10,9},{13,14},{14,13},{17,18},{18,... | collective-permute-start | bytes 73736 | tf_op jit(solution)/shard_map/ppermute | solution.py:436
  19.2 5.2 %collective-permute-start.3 = (f32[3,8,256]{2,1,0:T(8,128)S(1)}, f32[3,8,256]{2,1,0:T(8,128)S(1)}, u32[]{:S(2)}, u32[]{:S(2)}) collective-permute-start(f32[3,8,256]{2,1,0:T(8,128)S(1)} %get-tuple-element.34), channel_id=1, source_target_pairs={{0,1},{2,3},{1,0},{3,2},{4,5},{6,7},{5,4},{7,6},{8,9},{10,11},{9,8... | collective-permute-start | bytes 73736 | tf_op jit(solution)/shard_map/ppermute | solution.py:437
  24.4 0.2 collective-permute-done.first
  24.6 3.5 %collective-permute-done.1.second = f32[3,48,256]{2,1,0:T(8,128)S(1)} collective-permute-done((f32[3,48,256]{2,1,0:T(8,128)S(1)}, f32[3,48,256]{2,1,0:T(8,128)S(1)}, u32[]{:S(2)}, u32[]{:S(2)}) %collective-permute-start.1) | collective-permute-done | bytes 147488 | tf_op jit(solution)/shard_map/ppermute | solution.py:425
  28.1 1.1 %inner.1 = (f32[3,8,48,256]{3,2,1,0:T(8,128)S(1)}, f32[8,48,128]{2,1,0:T(8,128)S(1)}) custom-call(f32[3,8,48,256]{3,2,1,0:T(8,128)S(1)} %get-tuple-element.22.near, f32[3,48,256]{2,1,0:T(8,128)S(1)} %collective-permute-done.first, f32[3,48,256]{2,1,0:T(8,128)S(1)} %collective-permute-done.1.second), custom_call_target="tpu_custom_call" | custom-call | bytes 6000000 | tf_op jit(solution)/shard_map/inner/pallas_call | solution.py:438
  29.2 0.0 collective-permute-done.2.z1
  29.2 0.0 collective-permute-done.3.z2
  29.2 0.0 all-to-all-done.got
  29.3 0.7 %near.1 = (f32[8,48,256]{2,1,0:T(8,128)S(1)}, f32[16,48,128]{2,1,0:T(8,128)S(1)}) custom-call(f32[3,8,48,256]{3,2,1,0:T(8,128)S(1)} %get-tuple-element.31.mid, f32[8,48,128]{2,1,0:T(8,128)S(1)} %get-tuple-element.32.vely, f32[16,24,128]{2,1,0:T(8,128)S(1)} %all-to-all-done.got, f32[3,8,256]{2,1,0:T(8,128)S(1)} %collective-permute-done.2.z1, ...), custom_call_target="tpu_custom_call" | custom-call | bytes 6000000 | tf_op jit(solution)/shard_map/near/pallas_call | solution.py:447
  29.9 13.6 %all_to_all.10.sums = f32[16,48,128]{2,1,0:T(8,128)S(1)} all-to-all(f32[16,48,128]{2,1,0:T(8,128)S(1)} %get-tuple-element.35), channel_id=1, replica_groups=mesh['px'=48,'py'=4,'dz'=4] {'py','dz'}, dimensions={0} | all-to-all | bytes 786432 | tf_op jit(solution)/shard_map/all_to_all | solution.py:456
  43.5 1.2 %edge.1 = (f32[2,4,48,128]{3,2,1,0:T(8,128)S(1)}, f32[8,256]{1,0:T(8,128)S(1)}, f32[8,256]{1,0:T(8,128)S(1)}) custom-call(f32[16,24,128]{2,1,0:T(8,128)S(1)} %all-to-all-done.got, f32[16,48,128]{2,1,0:T(8,128)S(1)} %all_to_all.10.sums, f32[64,256]{1,0:T(8,128)S(1)} %get-tuple-element.25.depth, f32[2,64,256]{2,1,0:T(8,128)S(1)} %get-tuple-element.26.flows, ...), custom_call_target="tpu_custom_call" | custom-call | bytes 6000000 | tf_op jit(solution)/shard_map/edge/pallas_call | solution.py:457
  44.7 3.8 %collective-permute-start.4 = (f32[8,256]{1,0:T(8,128)S(1)}, f32[8,256]{1,0:T(8,128)S(1)}, u32[]{:S(2)}, u32[]{:S(2)}) collective-permute-start(f32[8,256]{1,0:T(8,128)S(1)} %get-tuple-element.40), channel_id=1, source_target_pairs={{16,32},{48,64},{80,96},{112,128},{144,160},{176,192},{208,224},{2... | collective-permute-start | bytes 24584 | tf_op jit(solution)/shard_map/ppermute | solution.py:467
  48.5 1.9 %collective-permute-start.5 = (f32[8,256]{1,0:T(8,128)S(1)}, f32[8,256]{1,0:T(8,128)S(1)}, u32[]{:S(2)}, u32[]{:S(2)}) collective-permute-start(f32[8,256]{1,0:T(8,128)S(1)} %get-tuple-element.41), channel_id=1, source_target_pairs={{0,16},{32,48},{64,80},{96,112},{128,144},{160,176},{192,208},{224... | collective-permute-start | bytes 24584 | tf_op jit(solution)/shard_map/ppermute | solution.py:468
  50.4 2.7 %far.1 = (f32[3,64,256]{2,1,0:T(8,128)S(1)}, f32[8,48,256]{2,1,0:T(8,128)}) custom-call(f32[16,24,128]{2,1,0:T(8,128)S(1)} %all-to-all-done.got, f32[2,4,48,128]{3,2,1,0:T(8,128)S(1)} %get-tuple-element.36.pieces, f32[64,256]{1,0:T(8,128)S(1)} %get-tuple-element.25.depth, f32[2,64,256]{2,1,0:T(8,128)S(1)} %get-tuple-element.26.flows, ...), custom_call_target="tpu_custom_call" | custom-call | bytes 15000000 | tf_op jit(solution)/shard_map/far/pallas_call | solution.py:469
  53.1 1.4 %collective-permute-done.4.got1 = f32[8,256]{1,0:T(8,128)S(1)} collective-permute-done((f32[8,256]{1,0:T(8,128)S(1)}, f32[8,256]{1,0:T(8,128)S(1)}, u32[]{:S(2)}, u32[]{:S(2)}) %collective-permute-start.4) | collective-permute-done | bytes 8224 | tf_op jit(solution)/shard_map/ppermute | solution.py:467
  54.5 0.5 collective-permute-done.5.got2
  54.9 0.7 %join.1 = f32[3,64,256]{2,1,0:T(8,128)} custom-call(f32[3,64,256]{2,1,0:T(8,128)S(1)} %get-tuple-element.39.part, f32[8,256]{1,0:T(8,128)S(1)} %collective-permute-done.4.got1, f32[8,256]{1,0:T(8,128)S(1)} %collective-permute-done.5.got2), custom_call_target="tpu_custom_call" | custom-call | bytes 3000000 | tf_op jit(solution)/shard_map/join/pallas_call | solution.py:479
Async XLA Ops:
  3.4 25.8 %all-to-all-start = ((f32[16,24,128]{2,1,0:T(8,128)}), f32[16,24,128]{2,1,0:T(8,128)S(1)}, u32[]{:S(2)}, u32[]{:S(2)}) async-start(f32[16,24,128]{2,1,0:T(8,128)} %get-tuple-element.28), calls=%async_computation | async-start | bytes 393216 | tf_op jit(solution)/shard_map/all_to_all | solution.py:435
  9.2 15.4 %collective-permute-start = (f32[3,48,256]{2,1,0:T(8,128)S(1)}, f32[3,48,256]{2,1,0:T(8,128)S(1)}, u32[]{:S(2)}, u32[]{:S(2)}) collective-permute-start(f32[3,48,256]{2,1,0:T(8,128)S(1)} %get-tuple-element.29), channel_id=1, source_target_pairs={{16,32},{48,64},{80,96},{112,128},{144,160},{176,192},{208,224},{2... | collective-permute-start | bytes 442376 | tf_op jit(solution)/shard_map/ppermute | solution.py:424
  15.7 12.5 %collective-permute-start.1 = (f32[3,48,256]{2,1,0:T(8,128)S(1)}, f32[3,48,256]{2,1,0:T(8,128)S(1)}, u32[]{:S(2)}, u32[]{:S(2)}) collective-permute-start(f32[3,48,256]{2,1,0:T(8,128)S(1)} %get-tuple-element.30), channel_id=1, source_target_pairs={{0,16},{32,48},{64,80},{96,112},{128,144},{160,176},{192,208},{224... | collective-permute-start | bytes 442376 | tf_op jit(solution)/shard_map/ppermute | solution.py:425
  18.5 10.7 %collective-permute-start.2 = (f32[3,8,256]{2,1,0:T(8,128)S(1)}, f32[3,8,256]{2,1,0:T(8,128)S(1)}, u32[]{:S(2)}, u32[]{:S(2)}) collective-permute-start(f32[3,8,256]{2,1,0:T(8,128)S(1)} %get-tuple-element.33), channel_id=1, source_target_pairs={{1,2},{2,1},{5,6},{6,5},{9,10},{10,9},{13,14},{14,13},{17,18},{18,... | collective-permute-start | bytes 73736 | tf_op jit(solution)/shard_map/ppermute | solution.py:436
  19.2 10.0 %collective-permute-start.3 = (f32[3,8,256]{2,1,0:T(8,128)S(1)}, f32[3,8,256]{2,1,0:T(8,128)S(1)}, u32[]{:S(2)}, u32[]{:S(2)}) collective-permute-start(f32[3,8,256]{2,1,0:T(8,128)S(1)} %get-tuple-element.34), channel_id=1, source_target_pairs={{0,1},{2,3},{1,0},{3,2},{4,5},{6,7},{5,4},{7,6},{8,9},{10,11},{9,8... | collective-permute-start | bytes 73736 | tf_op jit(solution)/shard_map/ppermute | solution.py:437
  44.7 9.8 %collective-permute-start.4 = (f32[8,256]{1,0:T(8,128)S(1)}, f32[8,256]{1,0:T(8,128)S(1)}, u32[]{:S(2)}, u32[]{:S(2)}) collective-permute-start(f32[8,256]{1,0:T(8,128)S(1)} %get-tuple-element.40), channel_id=1, source_target_pairs={{16,32},{48,64},{80,96},{112,128},{144,160},{176,192},{208,224},{2... | collective-permute-start | bytes 24584 | tf_op jit(solution)/shard_map/ppermute | solution.py:467
  48.5 6.4 %collective-permute-start.5 = (f32[8,256]{1,0:T(8,128)S(1)}, f32[8,256]{1,0:T(8,128)S(1)}, u32[]{:S(2)}, u32[]{:S(2)}) collective-permute-start(f32[8,256]{1,0:T(8,128)S(1)} %get-tuple-element.41), channel_id=1, source_target_pairs={{0,16},{32,48},{64,80},{96,112},{128,144},{160,176},{192,208},{224... | collective-permute-start | bytes 24584 | tf_op jit(solution)/shard_map/ppermute | solution.py:468
